TPU v7x, 32 devices: a whole 2x2x4 slice. The times are simulated.
32 devices in a mesh: dp: 8 (over y, x, core), mp: 4 (over z).
Axes of the slice: x: 2, y: 2, z: 4, core: 2. Of those that a mesh axis runs over, the one named last changes fastest.
Arguments:
- tokens: bfloat16 [16384, 1280], P(('dp', 'mp')), may hold values from -6 to 6
- segments: int32 [8, 2048], P('dp'), may hold values from 0 to 15, never falling along the last dimension, each value on 1 to 1024 neighbouring positions
- w_query: bfloat16 [1280, 1280], P('dp', 'mp'), may hold values from -0.15625 to 0.15625
- w_key: bfloat16 [1280, 1280], P('dp', 'mp'), may hold values from -0.15625 to 0.15625
- w_value: bfloat16 [1280, 1280], P('dp', 'mp'), may hold values from -0.15625 to 0.15625
- w_output: bfloat16 [1280, 1280], P('mp', 'dp'), may hold values from -1.25 to 1.25
- w_up: bfloat16 [1280, 1280], P('dp', 'mp'), may hold values from -0.15625 to 0.15625
- b_up: float32 [1280], P('mp'), may hold values from -3 to 3
- w_down: bfloat16 [1280, 1280], P('mp', 'dp'), may hold values from -0.25 to 0.25
- b_down: float32 [1280], replicated, may hold values from -3 to 3
- gain_attn: float32 [1280], replicated, may hold values from 0.5 to 1.5
- gain_mlp: float32 [1280], replicated, may hold values from 0.5 to 1.5
- query_scale: float32 [80], replicated, may hold values from -0.5 to 1
- cotangent: bfloat16 [16384, 1280], P(('dp', 'mp')), may hold values from -6 to 6
Outputs:
- layer_out: bfloat16 [16384, 1280], P(('dp', 'mp'))
- tokens_grad: bfloat16 [16384, 1280], P(('dp', 'mp'))
- grad_w_query: float32 [1280, 1280], P('dp', 'mp')
- grad_w_key: float32 [1280, 1280], P('dp', 'mp')
- grad_w_value: float32 [1280, 1280], P('dp', 'mp')
- grad_w_output: float32 [1280, 1280], P('mp', 'dp')
- grad_w_up: float32 [1280, 1280], P('dp', 'mp')
- grad_b_up: float32 [1280], P('mp')
- grad_w_down: float32 [1280, 1280], P('mp', 'dp')
- grad_b_down: float32 [1280], replicated
- grad_gain_attn: float32 [1280], replicated
- grad_gain_mlp: float32 [1280], replicated
- grad_query_scale: float32 [80], replicated
Inputs may be any that keep to these rules, and one draw needn't show every extreme that they name: `segments`: within a sequence segment numbers never fall; documents are 1 to 1024 tokens long.
All inputs are finite; a program needn't handle non-finite values.
Results may differ from a plain program's by a relative error of at most 0.014.
Values may be sent and summed in bfloat16 or wider, within the bound.
A program may use at most 192 MiB of HBM per device.

v0:
```python
import functools
import math

import jax
import jax.numpy as jnp
from jax import lax
from jax.experimental import pallas as pl
from jax.experimental.pallas import tpu as pltpu
from jax.sharding import PartitionSpec as P

HD = 80
LANES = 128
EPSILON = 1e-06
LOG2E = 1.442695
DOC_MAX = 1024
FAR = -1e30
F32 = jnp.float32
BF16 = jnp.bfloat16


def dot(a, b, ca, cb):
    return lax.dot_general(a, b, (((ca,), (cb,)), ((), ())), preferred_element_type=F32)


def row_inverse(values):
    return lax.rsqrt(jnp.mean(values * values, axis=1, keepdims=True) + EPSILON)


MESH = pl.DeviceIdType.MESH


def bit_of(index, b):
    return lax.rem(lax.div(index, 1 << b), 2)


def flipped(index, bits):
    for b in bits:
        index = index + (1 << b) * (1 - 2 * bit_of(index, b))
    return index


def split_order(count, turn):
    bits = list(range(count))
    rest = bits[1:][::-1]
    turn = turn % max(1, len(rest))
    return bits[:1] + rest[turn:] + rest[:turn]


def subsets(bits):
    out = [()]
    for b in bits:
        out = out + [s + (b,) for s in out]
    return out


def greet(dp_bits, stages, extra=()):
    d, z = lax.axis_index("dp"), lax.axis_index("mp")
    barrier = pltpu.get_barrier_semaphore()
    for b in range(dp_bits):
        pl.semaphore_signal(barrier, device_id={"dp": flipped(d, (b,))}, device_id_type=MESH)
    for step in range(1, stages):
        pl.semaphore_signal(
            barrier, device_id={"mp": lax.rem(z + step, stages)}, device_id_type=MESH
        )
    pl.semaphore_wait(barrier, dp_bits + stages - 1)
    return d, z


class Reduction:
    def __init__(self, dp_bits, stages, d, z, grads, outs, refs):
        self.dp_bits, self.stages, self.d, self.z = dp_bits, stages, d, z
        self.grads, self.outs = grads, outs
        self.pool = refs[0]
        self.kept, self.got = refs[0].at[0], refs[1 : 1 + dp_bits]
        self.zsend, self.zgot, self.ks, self.rs, self.rr, self.zs, self.zr = refs[1 + dp_bits :]
        self.half = 1 << (dp_bits - 1)
        self.parts = self.kept.shape[0] // len(outs)
        self.rows, self.features = self.kept.shape[2], self.kept.shape[3]
        self.sent = []

    def start(self, make, *args):
        make(*args).start()
        self.sent.append((make, args))

    def order(self, u):
        return split_order(self.dp_bits, u % self.parts)

    def place(self, u, slot, low):
        rest = self.order(u)[1:]
        at = low
        for i, b in enumerate(rest):
            if slot >> (len(rest) - 1 - i) & 1:
                at = at + (1 << b)
        return at

    def slot_of(self, u, index):
        rest = self.order(u)[1:]
        return sum(bit_of(index, b - 1) << (len(rest) - 1 - i) for i, b in enumerate(rest))

    def source(self, u, slot, low):
        cut = pl.ds(u % self.parts * self.rows, self.rows)
        return self.grads[u // self.parts].at[self.place(u, slot, low), cut]

    def first_copy(self, u, slot):
        return pltpu.make_async_remote_copy(
            src_ref=self.pool.at[1, u, slot]
            if self.grads is None
            else self.source(u, slot, 1 - bit_of(self.d, 0)),
            dst_ref=self.got[0].at[u, slot],
            send_sem=self.rs.at[u, slot], recv_sem=self.rr.at[u, slot],
            device_id={"dp": flipped(self.d, (0,))}, device_id_type=MESH,
        )

    def keep_copy(self, u, slot):
        return pltpu.make_async_copy(
            self.source(u, slot, bit_of(self.d, 0)), self.kept.at[u, slot], self.ks.at[u, slot]
        )

    def round_copy(self, u, k):
        count = self.half >> k
        b = self.order(u)[k]
        other = 1 - bit_of(self.d, b)
        return pltpu.make_async_remote_copy(
            src_ref=self.got[k - 1].at[u, pl.ds(other * count, count)],
            dst_ref=self.got[k].at[u],
            send_sem=self.rs.at[u, self.half + k], recv_sem=self.rr.at[u, self.half + k],
            device_id={"dp": flipped(self.d, (b,))}, device_id_type=MESH,
        )

    def last_copy(self, w, step):
        to = lax.rem(self.z + step, self.stages)
        return pltpu.make_async_remote_copy(
            src_ref=self.zsend.at[w, to], dst_ref=self.zgot.at[w, step],
            send_sem=self.zs.at[w, step], recv_sem=self.zr.at[w, step],
            device_id={"mp": to}, device_id_type=MESH,
        )

    def units(self, w):
        return range(w * self.parts, (w + 1) * self.parts)

    def begin(self, w):
        for u in self.units(w):
            for slot in range(self.half):
                self.start(self.first_copy, u, slot)
                if self.grads is not None:
                    self.keep_copy(u, slot).start()

    def add(self, dst, src, count):
        def step(i, carry):
            dst[i] = (dst[i].astype(F32) + src(i).astype(F32)).astype(BF16)
            return carry

        lax.fori_loop(0, count, step, 0)

    def advance(self, w, k):
        for u in self.units(w):
            count = self.half >> k
            if k == 0:
                for slot in range(self.half):
                    if self.grads is not None:
                        self.keep_copy(u, slot).wait()
                    self.first_copy(u, slot).wait_recv()
                self.add(self.got[0].at[u], lambda i: self.kept[u, i], count)
            else:
                self.round_copy(u, k).wait_recv()
                mine = bit_of(self.d, self.order(u)[k]) * count
                self.add(self.got[k].at[u], lambda i: self.got[k - 1][u, mine + i], count)
            if k + 1 < self.dp_bits:
                self.start(self.round_copy, u, k + 1)
        if k + 1 == self.dp_bits:
            self.begin_last(w)

    def begin_last(self, w):
        cols = self.features // self.stages
        for u in self.units(w):
            at = slice(u % self.parts * self.rows, (u % self.parts + 1) * self.rows)
            for s in range(self.stages):
                self.zsend[w, s, at, :] = self.got[self.dp_bits - 1][
                    u, 0, :, s * cols : (s + 1) * cols
                ]
        for step in range(1, self.stages):
            self.start(self.last_copy, w, step)

    def finish(self, w):
        value = self.zsend[w, self.z].astype(F32)
        for step in range(1, self.stages):
            self.last_copy(w, step).wait_recv()
            value = value + self.zgot[w, step].astype(F32)
        self.outs[w][...] = value

    def close(self):
        for make, args in self.sent:
            make(*args).wait_send()


def reduction_scratch(count, dp, stages, rows, features, local=False):
    dp_bits, half, cols = dp.bit_length() - 1, dp // 2, features // stages
    parts = 2 if rows % 32 == 0 else 1
    dma = pltpu.SemaphoreType.DMA
    units = count * parts
    return (
        [pltpu.VMEM((1 + local, units, half, rows // parts, features), BF16)]
        + [pltpu.VMEM((units, half >> k, rows // parts, features), BF16) for k in range(dp_bits)]
        + [pltpu.VMEM((count, stages, rows, cols), BF16)] * 2
        + [
            dma((units, half)), dma((units, half + dp_bits)), dma((units, half + dp_bits)),
            dma((count, stages)), dma((count, stages)),
        ]
    )


def spans(rows, width, block):
    own = width - rows
    out=[]
    for qb in range(rows//block):
        hi = own + (qb+1)*block
        lo = max(0, (own + qb*block - (DOC_MAX-1))//block*block)
        out.append((lo,hi))
    return out

def head_lanes(h, features):
    first = h*HD
    off = jnp.minimum(lax.div(first, LANES)*LANES, features-2*LANES)
    off = pl.multiple_of(off, LANES)
    lane = lax.broadcasted_iota(jnp.int32,(1,2*LANES),1) + (off-first)
    return pl.ds(off, 2*LANES), (lane>=0)&(lane<HD)

def fill_bias(seg_query, seg_key, bias, block, own):
    rows = seg_query.shape[1]; width=seg_key.shape[0]
    for kb in range(width//block):
        for qb in range(rows//block):
            row = seg_query[:, qb*block:(qb+1)*block]
            col = seg_key[kb*block:(kb+1)*block,:]
            ahead = (lax.broadcasted_iota(jnp.int32,(block,block),0)+(kb*block)) <= (lax.broadcasted_iota(jnp.int32,(block,block),1)+(own+qb*block))
            bias[kb*block:(kb+1)*block, qb*block:(qb+1)*block] = jnp.where((col==row)&ahead, 0.0, FAR)

def transpose_out(src, dst):
    for i in range(src.shape[0]//LANES):
        at = slice(i*LANES,(i+1)*LANES)
        dst[:, at] = src[at,:].T.astype(dst.dtype)

class Gathering:
    def __init__(self, dp_bits, stages, d, z, weights, homes, refs):
        self.dp_bits, self.stages, self.d, self.z = dp_bits, stages, d, z
        self.weights, self.homes = weights, homes
        self.blocks, self.slab, self.zs, self.zr, self.ds, self.dr, self.ls = refs
        self.rows, self.cols = weights[0].shape
        self.parts = self.ds.shape[0] // len(weights)
        self.cut = self.rows // self.parts
        self.sent = []

    def start(self, make, *args):
        make(*args).start()
        self.sent.append((make, args))

    def order(self, u):
        return split_order(self.dp_bits, u % self.parts)[::-1]

    def block_copy(self, w, step):
        return pltpu.make_async_remote_copy(
            src_ref=self.weights[w], dst_ref=self.blocks.at[w, step], send_sem=self.zs.at[w, step],
            recv_sem=self.zr.at[w, step], device_id={"mp": lax.rem(self.z + step, self.stages)},
            device_id_type=MESH,
        )

    def place(self, u, which):
        at = which * self.rows + u % self.parts * self.cut
        return self.homes[u // self.parts].at[pl.ds(pl.multiple_of(at, self.cut), self.cut)]

    def piece(self, u):
        at = u % self.parts * self.cut
        return self.slab.at[u // self.parts, pl.ds(at, self.cut)]

    def own_copy(self, u):
        return pltpu.make_async_copy(self.piece(u), self.place(u, self.d), self.ls.at[u])

    def round_copy(self, u, k, slot, held):
        which = flipped(self.d, held)
        return pltpu.make_async_remote_copy(
            src_ref=self.place(u, which) if held else self.piece(u),
            dst_ref=self.place(u, which),
            send_sem=self.ds.at[u, (1 << k) - 1 + slot], recv_sem=self.dr.at[u, which],
            device_id={"dp": flipped(self.d, self.order(u)[k : k + 1])}, device_id_type=MESH,
        )

    def arrival(self, u, k, held):
        which = flipped(self.d, held + tuple(self.order(u)[k : k + 1]))
        return pltpu.make_async_remote_copy(
            src_ref=self.piece(u), dst_ref=self.place(u, which),
            send_sem=self.ds.at[u, 0], recv_sem=self.dr.at[u, which],
            device_id={"dp": flipped(self.d, self.order(u)[k : k + 1])}, device_id_type=MESH,
        )

    def units(self, w):
        return range(w * self.parts, (w + 1) * self.parts)

    def begin(self, w):
        for step in range(1, self.stages):
            self.start(self.block_copy, w, step)

    def begin_round(self, w, k):
        for u in self.units(w):
            for slot, held in enumerate(subsets(self.order(u)[:k])):
                self.start(self.round_copy, u, k, slot, held)

    def collect(self, w):
        self.blocks[w, 0] = self.weights[w][...]
        for step in range(1, self.stages):
            self.block_copy(w, step).wait_recv()
        for me in range(self.stages):

            @pl.when(self.z == me)
            def _():
                self.slab[w] = jnp.concatenate(
                    [self.blocks[w, (me - s) % self.stages] for s in range(self.stages)], axis=1
                )

        for u in self.units(w):
            self.own_copy(u).start()
        self.begin_round(w, 0)

    def advance(self, w, k):
        for u in self.units(w):
            for held in subsets(self.order(u)[:k]):
                self.arrival(u, k, held).wait_recv()
        if k + 1 < self.dp_bits:
            self.begin_round(w, k + 1)
        else:
            for u in self.units(w):
                self.own_copy(u).wait()

    def close(self):
        for make, args in self.sent:
            make(*args).wait_send()


def gathering_scratch(count, dp, stages, rows, cols):
    parts = 2 if rows % 32 == 0 else 1
    dma = pltpu.SemaphoreType.DMA
    units = count * parts
    return [
        pltpu.VMEM((count, stages, rows, cols), BF16),
        pltpu.VMEM((count, rows, cols * stages), BF16),
        dma((count, stages)), dma((count, stages)), dma((units, dp)), dma((units, dp)), dma((units,)),
    ]


def forward_kernel(block, dp_bits, stages, back, *refs):
    weights, refs = refs[:6], refs[6:]
    bias_in, tokens, gain, factor, seg_query, seg_key = refs[:6]
    fulls, refs = refs[6:12], refs[12:]
    bias_all, raw_out, q_out, k_out, kt_out, v_out, nt_out, o_ref, lse_ref = refs[:9]
    refs = refs[9:]
    home, window, normed, nt, raw, q, k, kt, v, vt, ot, bias, scores = refs[:13]
    xs, xr, bs, br, os = refs[13:18]
    d, z = greet(dp_bits, stages)
    rows, features = tokens.shape
    width, heads = k.shape[0], features // HD
    own = width - rows
    tile = 2 * LANES
    homes = [home.at[w] for w in range(3)] + list(fulls[3:])
    work = Gathering(dp_bits, stages, d, z, weights, homes, refs[18:])

    def bias_copy(step):
        return pltpu.make_async_remote_copy(
            src_ref=bias_in, dst_ref=bias_all.at[step], send_sem=bs.at[step],
            recv_sem=br.at[step], device_id={"mp": lax.rem(z + step, stages)},
            device_id_type=MESH,
        )

    def token_copy(hop):
        return pltpu.make_async_remote_copy(
            src_ref=tokens if hop == 0 else window.at[hop - 1], dst_ref=window.at[hop],
            send_sem=xs.at[hop], recv_sem=xr.at[hop],
            device_id={"mp": jnp.minimum(z + 1, stages - 1)}, device_id_type=MESH,
        )

    kept = [
        (raw, raw_out), (q, q_out), (k, k_out), (kt, kt_out), (v, v_out), (nt, nt_out),
        (home.at[0], fulls[0]), (home.at[1], fulls[1]), (home.at[2], fulls[2]),
    ]

    def keep(i):
        return pltpu.make_async_copy(kept[i][0], kept[i][1], os.at[i])

    def norm(src, at):
        step_rows = 128

        def step(i, carry):
            part = pl.ds(pl.multiple_of(i * step_rows, step_rows), step_rows)
            x = src[part, :].astype(F32)
            value = (x * row_inverse(x) * gain[...]).astype(BF16)
            to = pl.ds(pl.multiple_of(at + i * step_rows, step_rows), step_rows)
            normed[to, :] = value
            return carry

        lax.fori_loop(0, rows // step_rows, step, 0)
        for c in range(features // tile):
            lanes = slice(c * tile, (c + 1) * tile)
            nt[lanes, at : at + rows] = normed[at : at + rows, lanes].T

    def project(w, at, out, out_t):
        def step(c, carry):
            lanes = pl.ds(pl.multiple_of(c * tile, tile), tile)
            value = dot(normed[at : at + rows, :], home[w, :, lanes], 1, 0).astype(BF16)
            out[at : at + rows, lanes] = value
            out_t[lanes, at : at + rows] = value.T
            return carry

        lax.fori_loop(0, features // tile, step, 0)

    for w in range(3):
        work.begin(w)
    for step in range(1, stages):
        work.start(bias_copy, step)

    @pl.when(z < stages - 1)
    def _():
        token_copy(0).start()

    bias_all[0] = bias_in[...]
    for hop in range(back):

        @pl.when(z <= hop)
        def _():
            window[hop] = jnp.zeros((rows, features), BF16)

    norm(tokens, own)
    fill_bias(seg_query, seg_key, bias, block, own)
    for w in range(3):
        work.collect(w)
    for r in range(dp_bits - 1):
        for w in range(3):
            work.advance(w, r)
    for w in range(3):
        work.advance(w, dp_bits - 1)
        keep(6 + w).start()
        if w == 0:

            def query(c, carry):
                lanes = pl.ds(pl.multiple_of(c * tile, tile), tile)
                value = dot(normed[own:, :], home[0, :, lanes], 1, 0)
                raw[:, lanes] = value
                q[:, lanes] = (value * factor[:, lanes]).astype(BF16)
                return carry

            lax.fori_loop(0, features // tile, query, 0)
            keep(0).start()
            keep(1).start()
        else:
            project(w, own, *((k, kt) if w == 1 else (v, vt)))
    for hop in range(back):

        @pl.when(z > hop)
        def _():
            token_copy(hop).wait_recv()

        if hop + 1 < back:

            @pl.when((z > hop) & (z < stages - 1))
            def _():
                token_copy(hop + 1).start()

        else:
            for w in range(3, 6):
                work.begin(w)
        at = own - (hop + 1) * rows
        norm(window.at[hop], at)
        project(1, at, k, kt)
        project(2, at, v, vt)
    for i in range(2, 6):
        keep(i).start()

    sp = spans(rows, width, block)
    tiles = []
    for kb in range(width // block):
        qs = [i for i, (lo, hi) in enumerate(sp) if lo <= kb * block < hi]
        if qs:
            tiles.append((kb, qs))
    due = {(w, r): min(heads - 1, 6 + 4 * (w - 3) + 4 * r) for w in range(3, 6) for r in range(2)}

    def head(h, carry):
        for at in sorted(set(due.values())):

            @pl.when(h == at)
            def _():
                for w, r in sorted(due, key=lambda e: (e[1], e[0])):
                    if due[w, r] == at:
                        if r == 0:
                            work.collect(w)
                        else:
                            work.advance(w, r - 1)

        lanes, mine = head_lanes(h, features)
        feats = pl.ds(pl.multiple_of(h * HD, 16), HD)
        query = jnp.where(mine, q[:, lanes], jnp.zeros((), BF16))
        top = [jnp.full((8, block), FAR, F32) for _ in sp]
        for kb, qs in tiles:
            qa, qz = qs[0] * block, (qs[-1] + 1) * block
            at = slice(kb * block, (kb + 1) * block)
            s = dot(k[at, lanes], query[qa:qz], 1, 1) + bias[at, qa:qz]
            scores[at, qa:qz] = s
            for i in qs:
                cut = s[:, i * block - qa : (i + 1) * block - qa]
                top[i] = jnp.maximum(top[i], jnp.max(cut.reshape(block // 8, 8, block), axis=0))
        top = jnp.concatenate([jnp.max(t, axis=0, keepdims=True) for t in top], axis=1)
        acc = [jnp.zeros((HD, block), F32) for _ in sp]
        total = [jnp.zeros((8, block), F32) for _ in sp]
        for kb, qs in tiles:
            qa, qz = qs[0] * block, (qs[-1] + 1) * block
            at = slice(kb * block, (kb + 1) * block)
            p = jnp.exp(scores[at, qa:qz] - top[:, qa:qz])
            part = dot(vt[feats, at], p.astype(BF16), 1, 0)
            for i in qs:
                cut = slice(i * block - qa, (i + 1) * block - qa)
                total[i] = total[i] + jnp.sum(p[:, cut].reshape(block // 8, 8, block), axis=0)
                acc[i] = acc[i] + part[:, cut]
        for i in range(len(sp)):
            at = slice(i * block, (i + 1) * block)
            one = jnp.sum(total[i], axis=0, keepdims=True)
            ot[feats, at] = acc[i] / one
            lse_ref[pl.ds(h, 1), at] = top[:, at] + jnp.log(one)
        return carry

    lax.fori_loop(0, heads, head, 0)
    transpose_out(ot, o_ref)
    for r in range(1, dp_bits):
        for w in range(3, 6):
            work.advance(w, r)
    for step in range(1, stages):
        bias_copy(step).wait_recv()
    for hop in range(back):

        @pl.when((z >= hop) & (z < stages - 1))
        def _():
            token_copy(hop).wait_send()

    for i in range(len(kept)):
        keep(i).wait()
    work.close()


def attend_forward(weights, bias, tokens, gain, factor, seg_q, seg_k, block, dp, stages, back):
    held, cols = weights[0].shape
    rows, features = tokens.shape
    width, heads = (back + 1) * rows, features // HD
    hbm = pl.BlockSpec(memory_space=pl.ANY)
    vmem = pl.BlockSpec(memory_space=pltpu.VMEM)
    dma = pltpu.SemaphoreType.DMA
    sds = jax.ShapeDtypeStruct
    return pl.pallas_call(
        functools.partial(forward_kernel, block, dp.bit_length() - 1, stages, back),
        in_specs=[vmem] * 12,
        out_specs=[hbm] * 6 + [vmem] + [hbm] * 6 + [vmem] * 2,
        out_shape=[sds((features, features), BF16)] * 6
        + [
            sds((stages,) + bias.shape, F32),
            sds((rows, features), F32),
            sds((rows, features), BF16),
            sds((width, features), BF16),
            sds((features, width), BF16),
            sds((width, features), BF16),
            sds((features, width), BF16),
            sds((rows, features), BF16),
            sds((heads, rows), F32),
        ],
        scratch_shapes=[
            pltpu.VMEM((3, features, features), BF16),
            pltpu.VMEM((back, rows, features), BF16),
            pltpu.VMEM((width, features), BF16),
            pltpu.VMEM((features, width), BF16),
            pltpu.VMEM((rows, features), F32),
            pltpu.VMEM((rows, features), BF16),
            pltpu.VMEM((width, features), BF16),
            pltpu.VMEM((features, width), BF16),
            pltpu.VMEM((width, features), BF16),
            pltpu.VMEM((features, width), BF16),
            pltpu.VMEM((features, rows), F32),
            pltpu.VMEM((width, rows), F32),
            pltpu.VMEM((width, rows), F32),
            dma((back,)), dma((back,)), dma((stages,)), dma((stages,)), dma((9,)),
        ]
        + gathering_scratch(6, dp, stages, held, cols),
        compiler_params=pltpu.CompilerParams(
            collective_id=0, has_side_effects=True, vmem_limit_bytes=62 << 20
        ),
        name="attend_forward",
    )(*weights, bias, tokens, gain, factor, seg_q, seg_k)


def backward_kernel(block, dp_bits, stages, count, *refs):
    q_ref, k_ref, kt_ref, v_ref, g_ref, lse_ref, delta_ref, seg_query, seg_key, wk, wv = refs[:11]
    grads, refs = refs[11 : 11 + count], refs[11 + count :]
    dq_ref, dk_ref, dv_ref, incoming = refs[:4]
    outs, refs = refs[4 : 4 + count], refs[4 + count :]
    dqt, bias, part, ps, pr, refs = refs[0], refs[1], refs[2], refs[3], refs[4], refs[5:]
    d, z = greet(dp_bits, stages)
    work = Reduction(dp_bits, stages, d, z, grads, outs, refs)
    for w in range(count):
        work.begin(w)
    rows, features = q_ref.shape
    heads, width = features // HD, k_ref.shape[0]
    back = width // rows - 1
    fill_bias(seg_query, seg_key, bias, block, width - rows)
    dk_ref[...] = jnp.zeros_like(dk_ref)
    dv_ref[...] = jnp.zeros_like(dv_ref)
    dqt[...] = jnp.zeros_like(dqt)
    sp = spans(rows, width, block)
    steps = heads * (back + 1)
    due = {}
    for w in range(count):
        for r, at in enumerate((0.16 + 0.08 * w, 0.56 + 0.25 * w, 0.74 + 0.25 * w)[:dp_bits]):
            if at < 1:
                due[w, r] = int(at * steps)

    def down():
        return pltpu.make_async_remote_copy(
            src_ref=part, dst_ref=incoming, send_sem=ps, recv_sem=pr,
            device_id={"mp": jnp.maximum(z - 1, 0)}, device_id_type=MESH,
        )

    for c in range(back + 1):

        def head(h, carry):
            for at in sorted(set(due.values())):
                if at // heads != c:
                    continue

                @pl.when(h == at % heads)
                def _():
                    for w, r in sorted(due, key=lambda e: (e[1], e[0])):
                        if due[w, r] == at:
                            work.advance(w, r)

            lanes, mine = head_lanes(h, features)
            feats = pl.ds(pl.multiple_of(h * HD, 16), HD)
            zero = jnp.zeros((), BF16)
            query = jnp.where(mine, q_ref[:, lanes], zero)
            grad = jnp.where(mine, g_ref[:, lanes], zero)
            lse = lse_ref[pl.ds(h, 1), :]
            delta = delta_ref[pl.ds(h, 1), :]
            acc = [None for _ in sp]
            for kb in range(c * rows // block, (c + 1) * rows // block):
                qs = [i for i, (lo, hi) in enumerate(sp) if lo <= kb * block < hi]
                if not qs:
                    continue
                qa, qz = qs[0] * block, (qs[-1] + 1) * block
                at = slice(kb * block, (kb + 1) * block)
                s = dot(k_ref[at, lanes], query[qa:qz], 1, 1) + bias[at, qa:qz]
                p = jnp.exp(s - lse[:, qa:qz])
                dp = dot(v_ref[at, lanes], grad[qa:qz], 1, 1)
                ds = (p * (dp - delta[:, qa:qz])).astype(BF16)
                dv_ref[at, lanes] += dot(p.astype(BF16), grad[qa:qz], 1, 0).astype(BF16)
                dk_ref[at, lanes] += dot(ds, query[qa:qz], 1, 0).astype(BF16)
                share = dot(kt_ref[feats, at], ds, 1, 0)
                for i in qs:
                    piece = share[:, i * block - qa : (i + 1) * block - qa]
                    acc[i] = piece if acc[i] is None else acc[i] + piece
            for i in range(len(sp)):
                if acc[i] is not None:
                    dqt[feats, i * block : (i + 1) * block] += acc[i]
            return carry

        lax.fori_loop(0, heads, head, 0)
        if c == 0 and back:
            back_project(part, ((dk_ref, wk), (dv_ref, wv)), 0, None)

            @pl.when(z >= back)
            def _():
                down().start()

    transpose_out(dqt, dq_ref)
    for r in range(dp_bits):
        for w in range(count):
            if (w, r) not in due:
                work.advance(w, r)
    for w in range(count):
        work.finish(w)
    if back:

        @pl.when((z + 1 >= back) & (z < stages - 1))
        def _():
            down().wait_recv()

        @pl.when(z >= back)
        def _():
            down().wait_send()

    work.close()


def back_project(out, pairs, at, more):
    rows, features = out.shape
    tile = 2 * LANES

    def step(c, carry):
        lanes = pl.ds(pl.multiple_of(c * tile, tile), tile)
        value = None
        for grad, weight in pairs:
            start = at if grad.shape[0] > rows else 0
            term = dot(grad[start : start + rows, :], weight[lanes, :], 1, 1)
            value = term if value is None else value + term
        if more is not None:
            value = value + more(lanes)
        out[:, lanes] = value.astype(out.dtype)
        return carry

    lax.fori_loop(0, features // tile, step, 0)


def attend_backward(q, k, kt, v, g, lse, delta, seg_q, seg_k, wk, wv, block, grads, dp, stages):
    rows, features = q.shape
    width, count = k.shape[0], len(grads)
    held, cols = grads[0].shape[0] // dp, features // stages
    hbm = pl.BlockSpec(memory_space=pl.ANY)
    vmem = pl.BlockSpec(memory_space=pltpu.VMEM)
    dma = pltpu.SemaphoreType.DMA
    sds = jax.ShapeDtypeStruct
    out = pl.pallas_call(
        functools.partial(backward_kernel, block, dp.bit_length() - 1, stages, count),
        in_specs=[vmem] * 11 + [hbm] * count,
        out_specs=[vmem] * 3 + [hbm] + [vmem] * count,
        out_shape=[
            sds((rows, features), BF16), sds((width, features), BF16), sds((width, features), BF16),
            sds((rows, features), BF16),
        ]
        + [sds((held, cols), F32)] * count,
        scratch_shapes=[
            pltpu.VMEM((features, rows), F32), pltpu.VMEM((width, rows), F32),
            pltpu.VMEM((rows, features), BF16), dma, dma,
        ]
        + reduction_scratch(count, dp, stages, held, features),
        compiler_params=pltpu.CompilerParams(
            collective_id=2, has_side_effects=True, vmem_limit_bytes=62 << 20
        ),
        name="attend_backward",
    )(
        q, k, kt, v, g, lse, delta, seg_q, seg_k, wk, wv,
        *[a.reshape(dp, held, features) for a in grads],
    )
    return out[:4], out[4:]


def input_kernel(dp_bits, stages, back, lead, *refs):
    nt, dq, dk, dv, wq, wk, wv, incoming, tokens, d_hidden, gain, sums = refs[:12]
    outs, tokens_grad, total, refs = refs[12:15], refs[15], refs[16], refs[17:]
    part, landed, d_first, sgot, ss, sr, ps, pr = refs[:8]
    d, z = greet(dp_bits, stages)
    work = Reduction(dp_bits, stages, d, z, None, outs, refs[8:])
    rows, features = tokens.shape
    own = back * rows
    levels = dp_bits + stages.bit_length() - 1
    held = features >> dp_bits
    grads = ((dv, 2, 0), (dk, 1, 0), (dq, 0, own))

    def down(hop):
        return pltpu.make_async_remote_copy(
            src_ref=part.at[hop - 1], dst_ref=landed.at[hop - 1], send_sem=ps.at[hop - 1],
            recv_sem=pr.at[hop - 1], device_id={"mp": jnp.maximum(z - 1, 0)}, device_id_type=MESH,
        )

    def arrived(hop):
        source = incoming if hop == 1 else landed.at[hop - 2]
        there = (z + 1 >= back - hop + 1) & (z < stages - 1)

        def take(lanes):
            return jnp.where(there, source[:, lanes].astype(F32), 0.0)

        return there, take

    def weight_grad(i):
        grad, w, at = grads[i]

        def step(t, carry):
            rows_at = pl.ds(pl.multiple_of(t * 2 * held, 2 * held), 2 * held)
            value = dot(nt[rows_at, at:], grad[...], 1, 0).astype(BF16)
            for low in range(2):
                which = lax.rem(bit_of(d, 0) + low, 2)
                for u in work.units(w):
                    cut = low * held + u % work.parts * work.rows
                    work.pool[which, u, work.slot_of(u, t)] = value[cut : cut + work.rows]
            return carry

        lax.fori_loop(0, 1 << (dp_bits - 1), step, 0)
        work.begin(w)

    def sum_copy(k):
        if k < dp_bits:
            to = {"dp": flipped(d, (k,))}
        else:
            to = {"mp": flipped(z, (k - dp_bits,))}
        return pltpu.make_async_remote_copy(
            src_ref=total.at[k], dst_ref=sgot.at[k], send_sem=ss.at[k], recv_sem=sr.at[k],
            device_id=to, device_id_type=MESH,
        )

    def sum_step(k):
        sum_copy(k).wait_recv()
        total[k + 1] = total[k] + sgot[k]
        if k + 1 < levels:
            work.start(sum_copy, k + 1)

    def pass_down(hop):
        there, take = arrived(hop)
        if hop > 1:

            @pl.when(there)
            def _():
                down(hop - 1).wait_recv()

        back_project(part.at[hop - 1], ((dk, wk), (dv, wv)), hop * rows, take)

        @pl.when(z >= back - hop)
        def _():
            down(hop).start()

    if back > 1:
        pass_down(1)
    weight_grad(0)
    weight_grad(1)
    work.advance(2, 0)
    weight_grad(2)
    work.advance(1, 0)
    for hop in range(2, back):
        pass_down(hop)
    back_project(d_first, ((dk, wk), (dv, wv), (dq, wq)), own, None)
    work.advance(0, 0)
    if dp_bits > 1:
        work.advance(2, 1)
    there, take = arrived(back) if back else (None, None)
    if back > 1:

        @pl.when(there)
        def _():
            down(back - 1).wait_recv()

    chunk = 64

    def finish(i, column):
        at = pl.ds(pl.multiple_of(i * chunk, chunk), chunk)
        x = tokens[at, :].astype(F32)
        grad = d_first[at, :]
        if back:
            source = incoming if back == 1 else landed.at[back - 2]
            grad = grad + jnp.where(there, source[at, :].astype(F32), 0.0)
        inverse = row_inverse(x)
        weighted = grad * gain[...]
        dots = jnp.sum(weighted * x, axis=1, keepdims=True)
        cube = inverse * inverse * inverse
        tokens_grad[at, :] = (
            d_hidden[at, :] + inverse * weighted - x * cube / features * dots
        ).astype(BF16)
        return column + jnp.sum(grad * x * inverse, axis=0, keepdims=True)

    column = lax.fori_loop(0, rows // chunk, finish, jnp.zeros((1, features), F32))
    total[0] = sums[...]
    for c in range(features // LANES):
        total[0, lead + c : lead + c + 1, :] = column[:, c * LANES : (c + 1) * LANES]
    work.start(sum_copy, 0)
    done = 0
    rest = [(w, k) for k in range(1, dp_bits) for w in (2, 1, 0) if (w, k) != (2, 1)]
    for w, k in rest:
        work.advance(w, k)
        if done < levels:
            sum_step(done)
            done += 1
    for k in range(done, levels):
        sum_step(k)
    for w in (2, 1, 0):
        work.finish(w)
    for hop in range(1, back):

        @pl.when(z >= back - hop)
        def _():
            down(hop).wait_send()

    work.close()


def input_gradients(
    nt, dq, dk, dv, wq, wk, wv, incoming, tokens, d_hidden, gain, sums, lead, dp, stages
):
    rows, features = tokens.shape
    back = dk.shape[0] // rows - 1
    held, cols = features // dp, features // stages
    dp_bits = dp.bit_length() - 1
    levels = dp_bits + stages.bit_length() - 1
    lines = sums.shape[0]
    vmem = pl.BlockSpec(memory_space=pltpu.VMEM)
    dma = pltpu.SemaphoreType.DMA
    hops = max(1, back - 1)
    out = pl.pallas_call(
        functools.partial(input_kernel, dp_bits, stages, back, lead),
        in_specs=[vmem] * 12,
        out_specs=[vmem] * 5,
        out_shape=[jax.ShapeDtypeStruct((held, cols), F32)] * 3
        + [
            jax.ShapeDtypeStruct((rows, features), BF16),
            jax.ShapeDtypeStruct((levels + 1, lines, LANES), F32),
        ],
        scratch_shapes=[
            pltpu.VMEM((hops, rows, features), BF16), pltpu.VMEM((hops, rows, features), BF16),
            pltpu.VMEM((rows, features), F32), pltpu.VMEM((levels, lines, LANES), F32),
            dma((levels,)), dma((levels,)), dma((hops,)), dma((hops,)),
        ]
        + reduction_scratch(3, dp, stages, held, features, True),
        compiler_params=pltpu.CompilerParams(
            collective_id=1, has_side_effects=True, vmem_limit_bytes=62 << 20
        ),
        name="input_gradients",
    )(nt, dq, dk, dv, wq, wk, wv, incoming, tokens, d_hidden, gain, sums)
    return out[:3], out[3], out[4][levels]


def body(
    tokens, segments, w_query, w_key, w_value, w_output, w_up, b_up, w_down, b_down,
    gain_attn, gain_mlp, query_scale, cotangent,
):
    stages = lax.axis_size("mp")
    z = lax.axis_index("mp")
    seg = segments[0]
    rows, features = tokens.shape
    back = min(stages - 1, -(-(DOC_MAX - 1) // rows))
    own = back * rows
    block = min(256, rows)

    inputs = tokens.astype(F32)
    inv_first = row_inverse(inputs)
    seg_wide = jnp.concatenate([jnp.full((own,), -1, jnp.int32), seg])
    seg_window = lax.dynamic_slice_in_dim(seg_wide, z * rows, own + rows, 0)
    seg_query = seg_window[own:]
    seg_query, seg_key = seg_query[None, :], seg_window[:, None]

    heads = features // HD
    factor = jax.nn.softplus(query_scale) * (LOG2E / math.sqrt(HD))
    factor_cols = jnp.tile(factor, heads)
    (
        wq, wk, wv, wu, wo, wd, b_all, query_raw, scaled, keys, keys_t, values, first_t, mixed, lse
    ) = attend_forward(
        (w_query, w_key, w_value, w_up, w_output.T, w_down.T), b_up[None], tokens,
        gain_attn[None], factor_cols[None], seg_query, seg_key, block,
        lax.axis_size("dp"), stages, back,
    )
    b_full = b_all[(z - jnp.arange(stages)) % stages].reshape(-1)

    hidden = inputs + dot(mixed, wo, 1, 1)
    inv_second = row_inverse(hidden)
    second = (hidden * inv_second * gain_mlp).astype(BF16)
    preact = jnp.dot(second, wu, preferred_element_type=F32) + b_full
    active = jax.nn.silu(preact).astype(BF16)
    layer_out = (hidden + dot(active, wd, 1, 1) + b_down).astype(BF16)

    upstream = cotangent.astype(F32)
    sigma = jax.nn.sigmoid(preact)
    d_active = dot(cotangent, wd, 1, 0)
    d_preact = (d_active * sigma * (1.0 + preact * (1.0 - sigma))).astype(BF16)
    d_second = dot(d_preact, wu, 1, 1)
    weighted = d_second * gain_mlp
    dots = jnp.sum(weighted * hidden, axis=1, keepdims=True)
    cube = inv_second * inv_second * inv_second
    d_hidden = upstream + inv_second * weighted - hidden * cube / features * dots
    d_attn = d_hidden.astype(BF16)
    d_mixed = dot(d_attn, wo, 1, 0).astype(BF16)

    owner = (jnp.arange(features)[None, :] // HD == jnp.arange(heads)[:, None]).astype(F32)
    delta = lax.dot_general(
        owner, d_mixed.astype(F32) * mixed.astype(F32), (((1,), (1,)), ((), ())),
        precision=lax.Precision.HIGHEST, preferred_element_type=F32,
    )
    (d_scaled, d_keys, d_values, incoming), mlp_grads = attend_backward(
        scaled, keys, keys_t, values, d_mixed, lse, delta, seg_query, seg_key, wk, wv, block,
        [
            dot(second, d_preact, 0, 0).astype(BF16),
            dot(d_attn, mixed, 0, 0).astype(BF16),
            dot(cotangent, active, 0, 0).astype(BF16),
        ],
        lax.axis_size("dp"), stages,
    )
    d_scaled_wide = d_scaled.astype(F32)
    d_query = (d_scaled_wide * factor_cols).astype(BF16)
    scale_part = jnp.sum(jnp.sum(d_scaled_wide * query_raw, axis=0).reshape(heads, HD), axis=0)

    grad_gain_mlp = jnp.sum(d_second * hidden * inv_second, axis=0)
    grad_b_up = jnp.sum(d_preact.astype(F32), axis=0)
    sums = jnp.concatenate(
        [
            grad_gain_mlp, jnp.sum(upstream, axis=0), grad_b_up, jnp.zeros((features,), F32),
            scale_part,
        ]
    )
    lines = -(-sums.shape[0] // (8 * LANES)) * 8
    grads, tokens_grad, sums = input_gradients(
        first_t, d_query, d_keys, d_values, wq, wk, wv, incoming, tokens, d_hidden,
        gain_attn[None],
        jnp.pad(sums, (0, lines * LANES - sums.shape[0])).reshape(lines, LANES),
        3 * features // LANES, lax.axis_size("dp"), stages,
    )
    sums = sums.reshape(-1)[: 4 * features + HD]
    sum_gain_mlp, sum_b_down, sum_b_up, sum_gain_attn, scale_total = jnp.split(
        sums, [features, 2 * features, 3 * features, 4 * features]
    )
    mine = b_up.shape[0]
    sum_b_up = lax.dynamic_slice_in_dim(sum_b_up, z * mine, mine, 0)
    grad_query_scale = scale_total * (LOG2E / math.sqrt(HD)) * jax.nn.sigmoid(query_scale)

    return (
        layer_out, tokens_grad, grads[0], grads[1], grads[2], mlp_grads[1].T, mlp_grads[0],
        sum_b_up, mlp_grads[2].T, sum_b_down, sum_gain_attn, sum_gain_mlp, grad_query_scale,
    )


def solution(mesh):
    tokens, rows_dp, rows_mp = P(("dp", "mp"), None), P("dp", "mp"), P("mp", "dp")
    return jax.shard_map(
        body,
        mesh=mesh,
        in_specs=(
            tokens, P("dp", None), rows_dp, rows_dp, rows_dp, rows_mp, rows_dp, P("mp"), rows_mp,
            P(), P(), P(), P(), tokens,
        ),
        out_specs=(
            tokens, tokens, rows_dp, rows_dp, rows_dp, rows_mp, rows_dp, P("mp"), rows_mp,
            P(), P(), P(), P(),
        ),
        check_vma=False,
    )
```

profile of v0, /device:TPU:0, one launch (start us, length us, event | category | flops | bytes accessed | tf_op | source)
XLA Modules:
  0.0 438.5 jit_solution(8242523611643319393)
XLA Ops:
  0.6 0.0 copy-start.1
  0.7 0.8 fusion.19
  1.4 1.3 pad_dynamic-slice_fusion
  2.8 1.2 broadcast_in_dim.10.refs_6_
  4.0 1.3 broadcast_in_dim.11.refs_8_.refs_10_
  5.3 0.7 broadcast_in_dim_tile.4.refs_9_
  6.0 0.1 mul.143
  6.1 0.8 pad_dynamic-slice_fusion.1
  6.9 1.2 broadcast_in_dim.30.refs_11_.refs_8_
  8.0 186.2 %attend_forward.1 = (bf16[1280,1280]{1,0:T(8,128)(2,1)}, bf16[1280,1280]{1,0:T(8,128)(2,1)}, bf16[1280,1280]{1,0:T(8,128)(2,1)}, bf16[1280,1280]{1,0:T(8,128)(2,...) custom-call(bf16[160,320]{1,0:T(8,128)(2,1)} %refs_0_.1, ...), custom_call_target="tpu_custom_call" | custom-call | tf_op jit(solution)/shard_map/attend_forward/pallas_call | solution.py:551
  194.2 0.7 copy.33
  194.9 0.6 gather_fusion
  195.5 0.1 add.102
  195.6 4.5 %multiply_reduce_fusion.2 = (f32[512]{0:T(512)S(1)}, f32[512,1280]{1,0:T(8,128)S(1)}) fusion(bf16[512,1280]{1,0:T(8,128)(2,1)} %get-tuple-element.40, bf16[1280,1280]{1,0:T(8,128)(2,1)} %get-tuple-element.41, bf16[512,1280]{1,0:T(8,128)(2,1)S(1)} %copy-done.1), kind=kOutput, calls=%fused_computation.31 | convolution fusion | flops 1680342528 | bytes 8521728 | tf_op jit(solution)/shard_map/dot_general | solution.py:22
  200.1 0.0 copy-start.15
  200.1 2.0 convolution_add_fusion.1
  202.1 0.0 copy-done.14
  202.1 0.0 copy-done.15
  202.2 0.0 copy-start.3
  202.2 3.3 fusion.4
  205.5 0.0 copy-done.3
  205.5 2.4 convert_reduce_fusion.1
  207.9 2.2 multiply_reduce_fusion
  210.1 0.8 convert_reduce_fusion
  210.9 3.7 convolution_convert_fusion.2
  214.6 2.1 convolution_convert_fusion.3.refs_4_
  216.7 0.0 copy-start.2
  216.8 2.1 fusion.8.refs_6_
  219.0 3.7 convolution_convert_fusion
  222.7 0.0 copy-done
  222.7 3.6 convolution_convert_fusion.1
  226.3 96.4 %attend_backward.1 = (bf16[512,1280]{1,0:T(8,128)(2,1)}, bf16[1536,1280]{1,0:T(8,128)(2,1)}, bf16[1536,1280]{1,0:T(8,128)(2,1)}, bf16[512,1280]{1,0:T(8,128)(2,1...) custom-call(bf16[512,1280]{1,0:T(8,128)(2,1)} %get-tuple-element.46.refs_0_, ...), custom_call_target="tpu_custom_call" | custom-call | tf_op jit(solution)/shard_map/attend_backward/pallas_call | solution.py:719
  322.7 3.5 fusion.7
  326.2 0.1 reshape.140
  326.3 0.6 pad_bitcast_fusion.refs_11_
  326.9 101.0 %input_gradients.1 = (f32[160,320]{1,0:T(8,128)}, f32[160,320]{1,0:T(8,128)}, f32[160,320]{1,0:T(8,128)}, bf16[512,1280]{1,0:T(8,128)(2,1)}, f32[6,48,128]{2,1,0:T(8,128)}) custom-call(bf16[1280,1536]{1,0:T(8,128)(2,1)} %get-tuple-element.45.refs_0_, bf16[512,1280]{1,0:T(8,128)(2,1)} %get-tuple-element.70.refs_1_, ...), custom_call_target="tpu_custom_call" | custom-call | tf_op jit(solution)/shard_map/input_gradients/pallas_call | solution.py:892
  428.0 0.8 slice_bitcast_fusion
  428.8 1.4 slice_bitcast_fusion.1
  430.3 0.5 divide_multiply_fusion
  430.8 0.7 dynamic_slice.7
  431.4 2.5 copy.46
  433.9 0.7 copy.47
  434.6 0.0 copy-done.9
  434.6 0.7 copy.48
  435.3 0.7 copy.49
  436.0 0.7 copy.50
  436.7 0.7 copy.51
  437.4 0.7 copy.52
  (38 shorter events, 0.1 us)
Async XLA Ops:
  0.6 194.9 %copy-start.1 = (bf16[512,1280]{1,0:T(8,128)(2,1)S(1)}, bf16[512,1280]{1,0:T(8,128)(2,1)}, u32[]{:S(2)}) copy-start(bf16[512,1280]{1,0:T(8,128)(2,1)} %refs_8_.1) | copy-start | bytes 3932164
  195.6 4.5 %copy-start.11 = (f32[1280]{0:T(1024)S(1)}, f32[1280]{0:T(1024)}, u32[]{:S(2)}) copy-start(f32[1280]{0:T(1024)} %param.25) | copy-start | bytes 15364
  195.6 4.5 %copy-start.13 = (bf16[1280,1280]{1,0:T(8,128)(2,1)S(1)}, bf16[1280,1280]{1,0:T(8,128)(2,1)}, u32[]{:S(2)}) copy-start(bf16[1280,1280]{1,0:T(8,128)(2,1)} %get-tuple-element.42) | copy-start | bytes 9830404
  200.1 2.0 copy-start.14
  200.1 2.0 copy-start.15
  202.2 3.4 copy-start.3
  210.9 11.8 %copy-start = (f32[512,1280]{1,0:T(8,128)}, f32[512,1280]{1,0:T(8,128)S(1)}, u32[]{:S(2)}) copy-start(f32[512,1280]{1,0:T(8,128)S(1)} %get-tuple-element.72.refs_9_) | copy-start | bytes 7864324
  210.9 3.7 copy-start.12
  214.6 2.2 copy-start.4
  216.7 5.9 %copy-start.2 = (bf16[512,1280]{1,0:T(8,128)(2,1)}, bf16[512,1280]{1,0:T(8,128)(2,1)S(1)}, u32[]{:S(2)}) copy-start(bf16[512,1280]{1,0:T(8,128)(2,1)S(1)} %convolution_convert_fusion.3.refs_4_) | copy-start | bytes 3932164
  326.9 103.3 %copy-start.16 = (f32[80]{0:T(128)S(1)}, f32[80]{0:T(128)}, u32[]{:S(2)}) copy-start(f32[80]{0:T(128)} %param.26) | copy-start | bytes 964
  427.9 6.0 %copy-start.10 = (f32[160,320]{1,0:T(8,128)S(1)}, f32[160,320]{1,0:T(8,128)}, u32[]{:S(2)}) copy-start(f32[160,320]{1,0:T(8,128)} %get-tuple-element.99) | copy-start | bytes 614404
  427.9 6.7 %copy-start.9 = (f32[160,320]{1,0:T(8,128)S(1)}, f32[160,320]{1,0:T(8,128)}, u32[]{:S(2)}) copy-start(f32[160,320]{1,0:T(8,128)} %get-tuple-element.100) | copy-start | bytes 614404
  427.9 7.3 %copy-start.8 = (f32[160,320]{1,0:T(8,128)S(1)}, f32[160,320]{1,0:T(8,128)}, u32[]{:S(2)}) copy-start(f32[160,320]{1,0:T(8,128)} %get-tuple-element.101) | copy-start | bytes 614404
  427.9 8.0 %copy-start.7 = (f32[160,320]{1,0:T(8,128)S(1)}, f32[160,320]{1,0:T(8,128)}, u32[]{:S(2)}) copy-start(f32[160,320]{1,0:T(8,128)} %get-tuple-element.63) | copy-start | bytes 614404
  428.0 8.7 %copy-start.6 = (f32[160,320]{1,0:T(8,128)S(1)}, f32[160,320]{1,0:T(8,128)}, u32[]{:S(2)}) copy-start(f32[160,320]{1,0:T(8,128)} %get-tuple-element.103) | copy-start | bytes 614404
  428.0 9.4 %copy-start.5 = (f32[160,320]{1,0:T(8,128)S(1)}, f32[160,320]{1,0:T(8,128)}, u32[]{:S(2)}) copy-start(f32[160,320]{1,0:T(8,128)} %get-tuple-element.66) | copy-start | bytes 614404
where the time goes:
time: 446 us; the launch traced here: 439 us
  Pallas kernels  384 us (86%)
  matrix products  29.6 us (7%)
  local copies, waits for them, and re-layouts  18.2 us (4%)
  other arithmetic  5.73 us (1%)
    pallas_call x1, Pallas kernels, attend_forward(): pl.pallas_call(functools.partial(forward_kernel, block, dp.bit_length() -...  186 us
    pallas_call x1, Pallas kernels, input_gradients(): pl.pallas_call(functools.partial(input_kernel, dp_bits, stages, back, lea...  101 us
    pallas_call x1, Pallas kernels, attend_backward(): pl.pallas_call(functools.partial(backward_kernel, block, dp.bit_length()...  96.4 us
    dot_general x8, matrix products, dot(): lax.dot_general(a, b, (((ca,), (cb,)), ((), ())), preferred_element_type=...  25.5 us

commit v1 on v0

--- a/solution.py
+++ b/solution.py
@@ -172,12 +172,11 @@
 
     def begin_last(self, w):
         cols = self.features // self.stages
-        for u in self.units(w):
-            at = slice(u % self.parts * self.rows, (u % self.parts + 1) * self.rows)
-            for s in range(self.stages):
-                self.zsend[w, s, at, :] = self.got[self.dp_bits - 1][
-                    u, 0, :, s * cols : (s + 1) * cols
-                ]
+        whole = [self.got[self.dp_bits - 1][u, 0] for u in self.units(w)]
+        for s in range(self.stages):
+            self.zsend[w, s] = jnp.concatenate(
+                [piece[:, s * cols : (s + 1) * cols] for piece in whole], axis=1
+            )
         for step in range(1, self.stages):
             self.start(self.last_copy, w, step)
 
@@ -186,7 +185,10 @@
         for step in range(1, self.stages):
             self.last_copy(w, step).wait_recv()
             value = value + self.zgot[w, step].astype(F32)
-        self.outs[w][...] = value
+        cols = self.features // self.stages
+        for p in range(self.parts):
+            at = slice(p * self.rows, (p + 1) * self.rows)
+            self.outs[w][at, :] = value[:, p * cols : (p + 1) * cols]
 
     def close(self):
         for make, args in self.sent:
@@ -201,7 +203,7 @@
     return (
         [pltpu.VMEM((1 + local, units, half, rows // parts, features), BF16)]
         + [pltpu.VMEM((units, half >> k, rows // parts, features), BF16) for k in range(dp_bits)]
-        + [pltpu.VMEM((count, stages, rows, cols), BF16)] * 2
+        + [pltpu.VMEM((count, stages, rows // parts, cols * parts), BF16)] * 2
         + [
             dma((units, half)), dma((units, half + dp_bits)), dma((units, half + dp_bits)),
             dma((count, stages)), dma((count, stages)),
@@ -251,17 +253,45 @@
 
     def start(self, make, *args):
         make(*args).start()
-        self.sent.append((make, args))
+        self.sent.append((make, args, None))
 
     def order(self, u):
         return split_order(self.dp_bits, u % self.parts)[::-1]
 
-    def block_copy(self, w, step):
+    def hop_copy(self, w, j, way):
+        at = lax.rem(self.z - way * j + self.stages, self.stages)
+        to = lax.rem(self.z + way + self.stages, self.stages)
         return pltpu.make_async_remote_copy(
-            src_ref=self.weights[w], dst_ref=self.blocks.at[w, step], send_sem=self.zs.at[w, step],
-            recv_sem=self.zr.at[w, step], device_id={"mp": lax.rem(self.z + step, self.stages)},
-            device_id_type=MESH,
-        )
+            src_ref=self.blocks.at[w, at], dst_ref=self.blocks.at[w, at],
+            send_sem=self.zs.at[w, 2 * j + (way + 1) // 2], recv_sem=self.zr.at[w, at],
+            device_id={"mp": to}, device_id_type=MESH,
+        )
+
+    def there(self, j, way):
+        return self.z >= j if way == 1 else self.z < self.stages - j
+
+    def pack(self, w):
+        pieces = [self.weights[w][p * self.cut : (p + 1) * self.cut] for p in range(self.parts)]
+        self.blocks[w, self.z] = jnp.concatenate(pieces, axis=1)
+
+    def take(self, w, j):
+        for way in (1, -1):
+
+            @pl.when(self.there(j, way))
+            def _():
+                self.hop_copy(w, j, way).wait_recv()
+
+    def hop(self, w, j):
+        if j:
+            self.take(w, j)
+        for way in (1, -1):
+            sends = self.there(j, way) & self.there(1, -way)
+
+            @pl.when(sends)
+            def _():
+                self.hop_copy(w, j, way).start()
+
+            self.sent.append((self.hop_copy, (w, j, way), sends))
 
     def place(self, u, which):
         at = which * self.rows + u % self.parts * self.cut
@@ -294,30 +324,20 @@
     def units(self, w):
         return range(w * self.parts, (w + 1) * self.parts)
 
-    def begin(self, w):
-        for step in range(1, self.stages):
-            self.start(self.block_copy, w, step)
-
     def begin_round(self, w, k):
         for u in self.units(w):
             for slot, held in enumerate(subsets(self.order(u)[:k])):
                 self.start(self.round_copy, u, k, slot, held)
 
     def collect(self, w):
-        self.blocks[w, 0] = self.weights[w][...]
-        for step in range(1, self.stages):
-            self.block_copy(w, step).wait_recv()
-        for me in range(self.stages):
-
-            @pl.when(self.z == me)
-            def _():
-                self.slab[w] = jnp.concatenate(
-                    [self.blocks[w, (me - s) % self.stages] for s in range(self.stages)], axis=1
-                )
-
+        self.take(w, self.stages - 1)
+        for p in range(self.parts):
+            lanes = slice(p * self.cols, (p + 1) * self.cols)
+            self.slab[w, p * self.cut : (p + 1) * self.cut] = jnp.concatenate(
+                [self.blocks[w, s, :, lanes] for s in range(self.stages)], axis=1
+            )
         for u in self.units(w):
             self.own_copy(u).start()
-        self.begin_round(w, 0)
 
     def advance(self, w, k):
         for u in self.units(w):
@@ -330,8 +350,14 @@
                 self.own_copy(u).wait()
 
     def close(self):
-        for make, args in self.sent:
-            make(*args).wait_send()
+        for make, args, sends in self.sent:
+            if sends is None:
+                make(*args).wait_send()
+            else:
+
+                @pl.when(sends)
+                def _():
+                    make(*args).wait_send()
 
 
 def gathering_scratch(count, dp, stages, rows, cols):
@@ -339,9 +365,9 @@
     dma = pltpu.SemaphoreType.DMA
     units = count * parts
     return [
-        pltpu.VMEM((count, stages, rows, cols), BF16),
+        pltpu.VMEM((count, stages, rows // parts, cols * parts), BF16),
         pltpu.VMEM((count, rows, cols * stages), BF16),
-        dma((count, stages)), dma((count, stages)), dma((units, dp)), dma((units, dp)), dma((units,)),
+        dma((count, 2 * stages)), dma((count, stages)), dma((units, dp)), dma((units, dp)), dma((units,)),
     ]
 
 
@@ -351,15 +377,15 @@
     fulls, refs = refs[6:12], refs[12:]
     bias_all, raw_out, q_out, k_out, kt_out, v_out, nt_out, o_ref, lse_ref = refs[:9]
     refs = refs[9:]
-    home, window, normed, nt, raw, q, k, kt, v, vt, ot, bias, scores = refs[:13]
-    xs, xr, bs, br, os = refs[13:18]
+    home, window, normed, nt, raw, q, k, kt, v, vt, ot, bias, scores, tops, totals = refs[:15]
+    xs, xr, bs, br, os = refs[15:20]
     d, z = greet(dp_bits, stages)
     rows, features = tokens.shape
     width, heads = k.shape[0], features // HD
     own = width - rows
     tile = 2 * LANES
     homes = [home.at[w] for w in range(3)] + list(fulls[3:])
-    work = Gathering(dp_bits, stages, d, z, weights, homes, refs[18:])
+    work = Gathering(dp_bits, stages, d, z, weights, homes, refs[20:])
 
     def bias_copy(step):
         return pltpu.make_async_remote_copy(
@@ -409,30 +435,51 @@
 
         lax.fori_loop(0, features // tile, step, 0)
 
-    for w in range(3):
-        work.begin(w)
+    first, rest = range(3), range(3, 6)
+    for w in range(6):
+        work.pack(w)
+    for w in first:
+        work.hop(w, 0)
     for step in range(1, stages):
         work.start(bias_copy, step)
+    bias_all[0] = bias_in[...]
+    for hop in range(back):
+
+        @pl.when(z <= hop)
+        def _():
+            window[hop] = jnp.zeros((rows, features), BF16)
+
+    norm(tokens, own)
+    fill_bias(seg_query, seg_key, bias, block, own)
+    for j in range(1, stages - 1):
+        for w in first:
+            work.hop(w, j)
+    for w in rest:
+        work.hop(w, 0)
+    for w in first:
+        work.collect(w)
+        work.begin_round(w, 0)
+    for j in range(1, stages - 1):
+        if j <= 3 and dp_bits > 1:
+            work.advance(j - 1, 0)
+        for w in rest:
+            work.hop(w, j)
 
     @pl.when(z < stages - 1)
     def _():
         token_copy(0).start()
 
-    bias_all[0] = bias_in[...]
-    for hop in range(back):
-
-        @pl.when(z <= hop)
-        def _():
-            window[hop] = jnp.zeros((rows, features), BF16)
-
-    norm(tokens, own)
-    fill_bias(seg_query, seg_key, bias, block, own)
-    for w in range(3):
+    if dp_bits > 1:
+        for w in range(max(0, min(stages - 2, 3)), 3):
+            work.advance(w, 0)
+    for w in rest:
         work.collect(w)
-    for r in range(dp_bits - 1):
-        for w in range(3):
+    for r in range(1, dp_bits - 1):
+        for w in first:
             work.advance(w, r)
-    for w in range(3):
+    for w in rest:
+        work.begin_round(w, 0)
+    for w in first:
         work.advance(w, dp_bits - 1)
         keep(6 + w).start()
         if w == 0:
@@ -449,7 +496,77 @@
             keep(1).start()
         else:
             project(w, own, *((k, kt) if w == 1 else (v, vt)))
+
+    sp = spans(rows, width, block)
+
+    def attend(low, high, fresh, last, due):
+        tiles = []
+        for kb in range(low // block, high // block):
+            qs = [i for i, (lo, hi) in enumerate(sp) if lo <= kb * block < hi]
+            if qs:
+                tiles.append((kb, qs))
+
+        def head(h, carry):
+            for at in sorted(set(due.values())):
+
+                @pl.when(h == at)
+                def _():
+                    for w, r in due:
+                        if due[w, r] == at:
+                            work.advance(w, r)
+
+            lanes, mine = head_lanes(h, features)
+            feats = pl.ds(pl.multiple_of(h * HD, 16), HD)
+            query = jnp.where(mine, q[:, lanes], jnp.zeros((), BF16))
+            top = [jnp.full((8, block), FAR, F32) for _ in sp]
+            for kb, qs in tiles:
+                qa, qz = qs[0] * block, (qs[-1] + 1) * block
+                at = slice(kb * block, (kb + 1) * block)
+                s = dot(k[at, lanes], query[qa:qz], 1, 1) + bias[at, qa:qz]
+                scores[at, qa:qz] = s
+                for i in qs:
+                    cut = s[:, i * block - qa : (i + 1) * block - qa]
+                    top[i] = jnp.maximum(top[i], jnp.max(cut.reshape(block // 8, 8, block), axis=0))
+            top = jnp.concatenate([jnp.max(t, axis=0, keepdims=True) for t in top], axis=1)
+            if not fresh:
+                before = tops[pl.ds(h, 1), :]
+                top = jnp.maximum(top, before)
+                scale = jnp.exp(before - top)
+            acc = [jnp.zeros((HD, block), F32) for _ in sp]
+            total = [jnp.zeros((8, block), F32) for _ in sp]
+            for kb, qs in tiles:
+                qa, qz = qs[0] * block, (qs[-1] + 1) * block
+                at = slice(kb * block, (kb + 1) * block)
+                p = jnp.exp(scores[at, qa:qz] - top[:, qa:qz])
+                part = dot(vt[feats, at], p.astype(BF16), 1, 0)
+                for i in qs:
+                    cut = slice(i * block - qa, (i + 1) * block - qa)
+                    total[i] = total[i] + jnp.sum(p[:, cut].reshape(block // 8, 8, block), axis=0)
+                    acc[i] = acc[i] + part[:, cut]
+            for i in range(len(sp)):
+                at = slice(i * block, (i + 1) * block)
+                one = jnp.sum(total[i], axis=0, keepdims=True)
+                out = acc[i]
+                if not fresh:
+                    one = one + totals[pl.ds(h, 1), at] * scale[:, at]
+                    out = out + ot[feats, at] * scale[:, at]
+                if last:
+                    ot[feats, at] = out / one
+                    lse_ref[pl.ds(h, 1), at] = top[:, at] + jnp.log(one)
+                else:
+                    ot[feats, at] = out
+                    totals[pl.ds(h, 1), at] = one
+                    tops[pl.ds(h, 1), at] = top[:, at]
+            return carry
+
+        lax.fori_loop(0, heads, head, 0)
+
+    inside = {}
+    if back and dp_bits > 2:
+        inside = {(3, 0): 0, (4, 0): heads // 4, (5, 0): heads // 2, (3, 1): heads * 3 // 4}
     for hop in range(back):
+        if hop + 1 == back:
+            attend(rows, width, True, False, inside)
 
         @pl.when(z > hop)
         def _():
@@ -461,72 +578,18 @@
             def _():
                 token_copy(hop + 1).start()
 
-        else:
-            for w in range(3, 6):
-                work.begin(w)
         at = own - (hop + 1) * rows
         norm(window.at[hop], at)
         project(1, at, k, kt)
         project(2, at, v, vt)
     for i in range(2, 6):
         keep(i).start()
-
-    sp = spans(rows, width, block)
-    tiles = []
-    for kb in range(width // block):
-        qs = [i for i, (lo, hi) in enumerate(sp) if lo <= kb * block < hi]
-        if qs:
-            tiles.append((kb, qs))
-    due = {(w, r): min(heads - 1, 6 + 4 * (w - 3) + 4 * r) for w in range(3, 6) for r in range(2)}
-
-    def head(h, carry):
-        for at in sorted(set(due.values())):
-
-            @pl.when(h == at)
-            def _():
-                for w, r in sorted(due, key=lambda e: (e[1], e[0])):
-                    if due[w, r] == at:
-                        if r == 0:
-                            work.collect(w)
-                        else:
-                            work.advance(w, r - 1)
-
-        lanes, mine = head_lanes(h, features)
-        feats = pl.ds(pl.multiple_of(h * HD, 16), HD)
-        query = jnp.where(mine, q[:, lanes], jnp.zeros((), BF16))
-        top = [jnp.full((8, block), FAR, F32) for _ in sp]
-        for kb, qs in tiles:
-            qa, qz = qs[0] * block, (qs[-1] + 1) * block
-            at = slice(kb * block, (kb + 1) * block)
-            s = dot(k[at, lanes], query[qa:qz], 1, 1) + bias[at, qa:qz]
-            scores[at, qa:qz] = s
-            for i in qs:
-                cut = s[:, i * block - qa : (i + 1) * block - qa]
-                top[i] = jnp.maximum(top[i], jnp.max(cut.reshape(block // 8, 8, block), axis=0))
-        top = jnp.concatenate([jnp.max(t, axis=0, keepdims=True) for t in top], axis=1)
-        acc = [jnp.zeros((HD, block), F32) for _ in sp]
-        total = [jnp.zeros((8, block), F32) for _ in sp]
-        for kb, qs in tiles:
-            qa, qz = qs[0] * block, (qs[-1] + 1) * block
-            at = slice(kb * block, (kb + 1) * block)
-            p = jnp.exp(scores[at, qa:qz] - top[:, qa:qz])
-            part = dot(vt[feats, at], p.astype(BF16), 1, 0)
-            for i in qs:
-                cut = slice(i * block - qa, (i + 1) * block - qa)
-                total[i] = total[i] + jnp.sum(p[:, cut].reshape(block // 8, 8, block), axis=0)
-                acc[i] = acc[i] + part[:, cut]
-        for i in range(len(sp)):
-            at = slice(i * block, (i + 1) * block)
-            one = jnp.sum(total[i], axis=0, keepdims=True)
-            ot[feats, at] = acc[i] / one
-            lse_ref[pl.ds(h, 1), at] = top[:, at] + jnp.log(one)
-        return carry
-
-    lax.fori_loop(0, heads, head, 0)
+    attend(0, rows if back else width, not back, True, {})
     transpose_out(ot, o_ref)
-    for r in range(1, dp_bits):
-        for w in range(3, 6):
-            work.advance(w, r)
+    for r in range(dp_bits):
+        for w in rest:
+            if (w, r) not in inside:
+                work.advance(w, r)
     for step in range(1, stages):
         bias_copy(step).wait_recv()
     for hop in range(back):
@@ -578,6 +641,8 @@
             pltpu.VMEM((features, rows), F32),
             pltpu.VMEM((width, rows), F32),
             pltpu.VMEM((width, rows), F32),
+            pltpu.VMEM((heads, rows), F32),
+            pltpu.VMEM((heads, rows), F32),
             dma((back,)), dma((back,)), dma((stages,)), dma((stages,)), dma((9,)),
         ]
         + gathering_scratch(6, dp, stages, held, cols),
@@ -670,8 +735,8 @@
                 down().start()
 
     transpose_out(dqt, dq_ref)
-    for r in range(dp_bits):
-        for w in range(count):
+    for w in range(count):
+        for r in range(dp_bits):
             if (w, r) not in due:
                 work.advance(w, r)
     for w in range(count):
@@ -858,7 +923,7 @@
         total[0, lead + c : lead + c + 1, :] = column[:, c * LANES : (c + 1) * LANES]
     work.start(sum_copy, 0)
     done = 0
-    rest = [(w, k) for k in range(1, dp_bits) for w in (2, 1, 0) if (w, k) != (2, 1)]
+    rest = [(w, k) for w in (2, 1, 0) for k in range(1, dp_bits) if (w, k) != (2, 1)]
     for w, k in rest:
         work.advance(w, k)
         if done < levels:

time: 446 us -> 371 us (0.83)
  Pallas kernels: 384 us -> 309 us
    pallas_call x1, Pallas kernels: 186 us -> 125 us  [attend_forward(): pl.pallas_call(functools.partial(forward_kernel, block, dp.bit_length() -...]
    pallas_call x1, Pallas kernels: 101 us -> 90.9 us  [input_gradients(): pl.pallas_call(functools.partial(input_kernel, dp_bits, stages, back, lea...]
where the time goes in v1:
time: 371 us; the launch traced here: 364 us
  Pallas kernels  309 us (83%)
  matrix products  29.6 us (8%)
  local copies, waits for them, and re-layouts  18.2 us (5%)
  other arithmetic  5.73 us (2%)
    pallas_call x1, Pallas kernels, attend_forward(): pl.pallas_call(functools.partial(forward_kernel, block, dp.bit_length() -...  125 us
    pallas_call x1, Pallas kernels, attend_backward(): pl.pallas_call(functools.partial(backward_kernel, block, dp.bit_length()...  93.8 us
    pallas_call x1, Pallas kernels, input_gradients(): pl.pallas_call(functools.partial(input_kernel, dp_bits, stages, back, lea...  90.9 us
    dot_general x8, matrix products, dot(): lax.dot_general(a, b, (((ca,), (cb,)), ((), ())), preferred_element_type=...  25.5 us

profile of v1, /device:TPU:0, one launch (start us, length us, event | category | flops | bytes accessed | tf_op | source)
XLA Modules:
  0.0 364.3 jit_solution(4647157180476789349)
XLA Ops:
  0.6 0.0 copy-start.1
  0.7 0.8 fusion.19
  1.4 1.3 pad_dynamic-slice_fusion
  2.8 1.2 broadcast_in_dim.10.refs_6_
  4.0 1.3 broadcast_in_dim.11.refs_8_.refs_10_
  5.3 0.7 broadcast_in_dim_tile.4.refs_9_
  6.0 0.1 mul.143
  6.1 0.8 pad_dynamic-slice_fusion.1
  6.9 1.2 broadcast_in_dim.30.refs_11_.refs_8_
  8.0 124.6 %attend_forward.1 = (bf16[1280,1280]{1,0:T(8,128)(2,1)}, bf16[1280,1280]{1,0:T(8,128)(2,1)}, bf16[1280,1280]{1,0:T(8,128)(2,1)}, bf16[1280,1280]{1,0:T(8,128)(2,...) custom-call(bf16[160,320]{1,0:T(8,128)(2,1)} %refs_0_.1, ...), custom_call_target="tpu_custom_call" | custom-call | tf_op jit(solution)/shard_map/attend_forward/pallas_call | solution.py:614
  132.6 0.7 copy.33
  133.3 0.6 gather_fusion
  133.9 0.1 add.102
  134.0 4.5 %multiply_reduce_fusion.2 = (f32[512]{0:T(512)S(1)}, f32[512,1280]{1,0:T(8,128)S(1)}) fusion(bf16[512,1280]{1,0:T(8,128)(2,1)} %get-tuple-element.40, bf16[1280,1280]{1,0:T(8,128)(2,1)} %get-tuple-element.41, bf16[512,1280]{1,0:T(8,128)(2,1)S(1)} %copy-done.1), kind=kOutput, calls=%fused_computation.31 | convolution fusion | flops 1680342528 | bytes 8521728 | tf_op jit(solution)/shard_map/dot_general | solution.py:22
  138.5 0.0 copy-start.15
  138.5 2.0 convolution_add_fusion.1
  140.5 0.0 copy-start.3
  140.5 3.3 fusion.4
  143.9 0.0 copy-done.3
  143.9 2.4 convert_reduce_fusion.1
  146.3 2.2 multiply_reduce_fusion
  148.5 0.8 convert_reduce_fusion
  149.3 3.7 %convolution_convert_fusion.2 = bf16[1280,1280]{1,0:T(8,128)(2,1)} fusion(bf16[512,1280]{1,0:T(8,128)(2,1)S(1)} %get-tuple-element.83, f32[512,1280]{1,0:T(8,128)S(1)} %get-tuple-element.80, f32[1280]{0:T(1024)S(1)} %copy-done.11, f32[512]{0:T(512)S(1)} %get-tuple-element.78), kind=kOutput, calls=%fused_computation.3 | convolution fusion | flops 1681326080 | bytes 7216128 | tf_op jit(solution)/shard_map/dot_general | solution.py:22
  153.0 0.0 copy-done.12
  153.0 2.1 convolution_convert_fusion.3.refs_4_
  155.1 0.0 copy-start.2
  155.2 2.1 fusion.8.refs_6_
  157.3 3.7 %convolution_convert_fusion = bf16[1280,1280]{0,1:T(8,128)(2,1)} fusion(bf16[512,1280]{1,0:T(8,128)(2,1)S(1)} %copy-done.3, f32[512,1280]{1,0:T(8,128)S(1)} %convolution_add_fusion.1), kind=kOutput, calls=%fused_computation.1 | convolution fusion | flops 1682636800 | bytes 7208960 | tf_op jit(solution)/shard_map/dot_general | solution.py:22
  161.1 0.0 copy-done
  161.1 3.6 convolution_convert_fusion.1
  164.7 93.8 %attend_backward.1 = (bf16[512,1280]{1,0:T(8,128)(2,1)}, bf16[1536,1280]{1,0:T(8,128)(2,1)}, bf16[1536,1280]{1,0:T(8,128)(2,1)}, bf16[512,1280]{1,0:T(8,128)(2,1...) custom-call(bf16[512,1280]{1,0:T(8,128)(2,1)} %get-tuple-element.46.refs_0_, ...), custom_call_target="tpu_custom_call" | custom-call | tf_op jit(solution)/shard_map/attend_backward/pallas_call | solution.py:784
  258.5 3.5 fusion.7
  262.0 0.1 reshape.140
  262.1 0.6 pad_bitcast_fusion.refs_11_
  262.8 90.9 %input_gradients.1 = (f32[160,320]{1,0:T(8,128)}, f32[160,320]{1,0:T(8,128)}, f32[160,320]{1,0:T(8,128)}, bf16[512,1280]{1,0:T(8,128)(2,1)}, f32[6,48,128]{2,1,0:T(8,128)}) custom-call(bf16[1280,1536]{1,0:T(8,128)(2,1)} %get-tuple-element.45.refs_0_, bf16[512,1280]{1,0:T(8,128)(2,1)} %get-tuple-element.70.refs_1_, ...), custom_call_target="tpu_custom_call" | custom-call | tf_op jit(solution)/shard_map/input_gradients/pallas_call | solution.py:957
  353.7 0.8 slice_bitcast_fusion
  354.6 1.4 slice_bitcast_fusion.1
  356.0 0.0 copy-done.16
  356.0 0.5 divide_multiply_fusion
  356.5 0.7 dynamic_slice.7
  357.2 2.5 copy.46
  359.6 0.7 copy.47
  360.3 0.7 copy.48
  361.0 0.7 copy.49
  361.7 0.0 copy-done.7
  361.7 0.7 copy.50
  362.4 0.7 copy.51
  363.1 0.7 copy.52
  (38 shorter events, 0.1 us)
Async XLA Ops:
  0.6 133.3 %copy-start.1 = (bf16[512,1280]{1,0:T(8,128)(2,1)S(1)}, bf16[512,1280]{1,0:T(8,128)(2,1)}, u32[]{:S(2)}) copy-start(bf16[512,1280]{1,0:T(8,128)(2,1)} %refs_8_.1) | copy-start | bytes 3932164
  134.0 4.5 %copy-start.11 = (f32[1280]{0:T(1024)S(1)}, f32[1280]{0:T(1024)}, u32[]{:S(2)}) copy-start(f32[1280]{0:T(1024)} %param.25) | copy-start | bytes 15364
  134.0 4.5 %copy-start.13 = (bf16[1280,1280]{1,0:T(8,128)(2,1)S(1)}, bf16[1280,1280]{1,0:T(8,128)(2,1)}, u32[]{:S(2)}) copy-start(bf16[1280,1280]{1,0:T(8,128)(2,1)} %get-tuple-element.42) | copy-start | bytes 9830404
  138.5 2.0 copy-start.14
  138.5 2.0 copy-start.15
  140.5 3.4 copy-start.3
  149.3 11.8 %copy-start = (f32[512,1280]{1,0:T(8,128)}, f32[512,1280]{1,0:T(8,128)S(1)}, u32[]{:S(2)}) copy-start(f32[512,1280]{1,0:T(8,128)S(1)} %get-tuple-element.72.refs_9_) | copy-start | bytes 7864324
  149.3 3.7 %copy-start.12 = (bf16[1280,1280]{1,0:T(8,128)(2,1)S(1)}, bf16[1280,1280]{1,0:T(8,128)(2,1)}, u32[]{:S(2)}) copy-start(bf16[1280,1280]{1,0:T(8,128)(2,1)} %get-tuple-element.41) | copy-start | bytes 9830404
  153.0 2.2 copy-start.4
  155.1 5.9 %copy-start.2 = (bf16[512,1280]{1,0:T(8,128)(2,1)}, bf16[512,1280]{1,0:T(8,128)(2,1)S(1)}, u32[]{:S(2)}) copy-start(bf16[512,1280]{1,0:T(8,128)(2,1)S(1)} %convolution_convert_fusion.3.refs_4_) | copy-start | bytes 3932164
  262.8 93.2 %copy-start.16 = (f32[80]{0:T(128)S(1)}, f32[80]{0:T(128)}, u32[]{:S(2)}) copy-start(f32[80]{0:T(128)} %param.26) | copy-start | bytes 964
  353.7 6.0 %copy-start.10 = (f32[160,320]{1,0:T(8,128)S(1)}, f32[160,320]{1,0:T(8,128)}, u32[]{:S(2)}) copy-start(f32[160,320]{1,0:T(8,128)} %get-tuple-element.99) | copy-start | bytes 614404
  353.7 6.7 %copy-start.9 = (f32[160,320]{1,0:T(8,128)S(1)}, f32[160,320]{1,0:T(8,128)}, u32[]{:S(2)}) copy-start(f32[160,320]{1,0:T(8,128)} %get-tuple-element.100) | copy-start | bytes 614404
  353.7 7.3 %copy-start.8 = (f32[160,320]{1,0:T(8,128)S(1)}, f32[160,320]{1,0:T(8,128)}, u32[]{:S(2)}) copy-start(f32[160,320]{1,0:T(8,128)} %get-tuple-element.101) | copy-start | bytes 614404
  353.7 8.0 %copy-start.7 = (f32[160,320]{1,0:T(8,128)S(1)}, f32[160,320]{1,0:T(8,128)}, u32[]{:S(2)}) copy-start(f32[160,320]{1,0:T(8,128)} %get-tuple-element.63) | copy-start | bytes 614404
  353.7 8.7 %copy-start.6 = (f32[160,320]{1,0:T(8,128)S(1)}, f32[160,320]{1,0:T(8,128)}, u32[]{:S(2)}) copy-start(f32[160,320]{1,0:T(8,128)} %get-tuple-element.103) | copy-start | bytes 614404
  353.7 9.4 %copy-start.5 = (f32[160,320]{1,0:T(8,128)S(1)}, f32[160,320]{1,0:T(8,128)}, u32[]{:S(2)}) copy-start(f32[160,320]{1,0:T(8,128)} %get-tuple-element.66) | copy-start | bytes 614404

commit v2 on v1

--- a/solution.py
+++ b/solution.py
@@ -14,6 +14,7 @@
 LOG2E = 1.442695
 DOC_MAX = 1024
 FAR = -1e30
+EVENTS = (0.04, 0.1, 0.25, 0.32, 0.46, 0.6, 0.75)
 F32 = jnp.float32
 BF16 = jnp.bfloat16
 
@@ -66,6 +67,22 @@
     return d, z
 
 
+class Loads:
+    def __init__(self, pairs, sems):
+        self.pairs, self.sems = pairs, sems
+
+    def copy(self, i):
+        return pltpu.make_async_copy(self.pairs[i][0], self.pairs[i][1], self.sems.at[i])
+
+    def start(self, *which):
+        for i in which:
+            self.copy(i).start()
+
+    def wait(self, *which):
+        for i in which:
+            self.copy(i).wait()
+
+
 class Reduction:
     def __init__(self, dp_bits, stages, d, z, grads, outs, refs):
         self.dp_bits, self.stages, self.d, self.z = dp_bits, stages, d, z
@@ -152,7 +169,7 @@
 
         lax.fori_loop(0, count, step, 0)
 
-    def advance(self, w, k):
+    def take(self, w, k):
         for u in self.units(w):
             count = self.half >> k
             if k == 0:
@@ -165,10 +182,54 @@
                 self.round_copy(u, k).wait_recv()
                 mine = bit_of(self.d, self.order(u)[k]) * count
                 self.add(self.got[k].at[u], lambda i: self.got[k - 1][u, mine + i], count)
-            if k + 1 < self.dp_bits:
-                self.start(self.round_copy, u, k + 1)
-        if k + 1 == self.dp_bits:
-            self.begin_last(w)
+
+    def send(self, w, k):
+        for u in self.units(w):
+            self.start(self.round_copy, u, k)
+
+    def schedule(self, order):
+        events = []
+        ahead = 2
+
+        def event(w, k, starts):
+            def run():
+                self.take(w, k)
+                if k and k + 1 < self.dp_bits:
+                    self.send(w, k + 1)
+                for other in starts:
+                    self.send(other, 1)
+                if k + 1 == self.dp_bits:
+                    self.begin_last(w)
+
+            return run
+
+        for i, w in enumerate(order):
+            starts = [w] if i < ahead and self.dp_bits > 1 else []
+            events.append(event(w, 0, starts))
+        for i, w in enumerate(order):
+            for k in range(1, self.dp_bits):
+                starts = [order[i + ahead]] if k == 1 and i + ahead < len(order) else []
+                events.append(event(w, k, starts))
+        return events
+
+    def put(self, w, index, value):
+        held = self.parts * self.rows
+        for low in range(2):
+            which = lax.rem(bit_of(self.d, 0) + low, 2)
+            for u in self.units(w):
+                cut = low * held + u % self.parts * self.rows
+                self.pool[which, u, self.slot_of(u, index)] = value[cut : cut + self.rows]
+
+    def weight_grad(self, w, left, right):
+        held = self.parts * self.rows
+
+        def step(t, carry):
+            at = pl.ds(pl.multiple_of(t * 2 * held, 2 * held), 2 * held)
+            self.put(w, t, dot(left(at), right(), 1, 0).astype(BF16))
+            return carry
+
+        lax.fori_loop(0, 1 << (self.dp_bits - 1), step, 0)
+        self.begin(w)
 
     def begin_last(self, w):
         cols = self.features // self.stages
@@ -375,9 +436,9 @@
     weights, refs = refs[:6], refs[6:]
     bias_in, tokens, gain, factor, seg_query, seg_key = refs[:6]
     fulls, refs = refs[6:12], refs[12:]
-    bias_all, raw_out, q_out, k_out, kt_out, v_out, nt_out, o_ref, lse_ref = refs[:9]
-    refs = refs[9:]
-    home, window, normed, nt, raw, q, k, kt, v, vt, ot, bias, scores, tops, totals = refs[:15]
+    bias_full, raw_out, q_out, k_out, v_out, nt_out, o_ref, lse_ref = refs[:8]
+    refs = refs[8:]
+    home, window, normed, nt, raw, q, k, v, vt, ot, bias, scores, tops, totals, bias_all = refs[:15]
     xs, xr, bs, br, os = refs[15:20]
     d, z = greet(dp_bits, stages)
     rows, features = tokens.shape
@@ -402,7 +463,7 @@
         )
 
     kept = [
-        (raw, raw_out), (q, q_out), (k, k_out), (kt, kt_out), (v, v_out), (nt, nt_out),
+        (raw, raw_out), (q, q_out), (k, k_out), (v, v_out), (nt, nt_out),
         (home.at[0], fulls[0]), (home.at[1], fulls[1]), (home.at[2], fulls[2]),
     ]
 
@@ -430,7 +491,8 @@
             lanes = pl.ds(pl.multiple_of(c * tile, tile), tile)
             value = dot(normed[at : at + rows, :], home[w, :, lanes], 1, 0).astype(BF16)
             out[at : at + rows, lanes] = value
-            out_t[lanes, at : at + rows] = value.T
+            if out_t is not None:
+                out_t[lanes, at : at + rows] = value.T
             return carry
 
         lax.fori_loop(0, features // tile, step, 0)
@@ -481,7 +543,7 @@
         work.begin_round(w, 0)
     for w in first:
         work.advance(w, dp_bits - 1)
-        keep(6 + w).start()
+        keep(5 + w).start()
         if w == 0:
 
             def query(c, carry):
@@ -495,7 +557,7 @@
             keep(0).start()
             keep(1).start()
         else:
-            project(w, own, *((k, kt) if w == 1 else (v, vt)))
+            project(w, own, *((k, None) if w == 1 else (v, vt)))
 
     sp = spans(rows, width, block)
 
@@ -580,9 +642,9 @@
 
         at = own - (hop + 1) * rows
         norm(window.at[hop], at)
-        project(1, at, k, kt)
+        project(1, at, k, None)
         project(2, at, v, vt)
-    for i in range(2, 6):
+    for i in range(2, 5):
         keep(i).start()
     attend(0, rows if back else width, not back, True, {})
     transpose_out(ot, o_ref)
@@ -592,6 +654,9 @@
                 work.advance(w, r)
     for step in range(1, stages):
         bias_copy(step).wait_recv()
+    bias_full[...] = jnp.concatenate(
+        [bias_all[lax.rem(z - s + stages, stages)] for s in range(stages)], axis=1
+    )
     for hop in range(back):
 
         @pl.when((z >= hop) & (z < stages - 1))
@@ -614,14 +679,13 @@
     return pl.pallas_call(
         functools.partial(forward_kernel, block, dp.bit_length() - 1, stages, back),
         in_specs=[vmem] * 12,
-        out_specs=[hbm] * 6 + [vmem] + [hbm] * 6 + [vmem] * 2,
+        out_specs=[hbm] * 6 + [vmem] + [hbm] * 5 + [vmem] * 2,
         out_shape=[sds((features, features), BF16)] * 6
         + [
-            sds((stages,) + bias.shape, F32),
+            sds((1, features), F32),
             sds((rows, features), F32),
             sds((rows, features), BF16),
             sds((width, features), BF16),
-            sds((features, width), BF16),
             sds((width, features), BF16),
             sds((features, width), BF16),
             sds((rows, features), BF16),
@@ -635,7 +699,6 @@
             pltpu.VMEM((rows, features), F32),
             pltpu.VMEM((rows, features), BF16),
             pltpu.VMEM((width, features), BF16),
-            pltpu.VMEM((features, width), BF16),
             pltpu.VMEM((width, features), BF16),
             pltpu.VMEM((features, width), BF16),
             pltpu.VMEM((features, rows), F32),
@@ -643,7 +706,8 @@
             pltpu.VMEM((width, rows), F32),
             pltpu.VMEM((heads, rows), F32),
             pltpu.VMEM((heads, rows), F32),
-            dma((back,)), dma((back,)), dma((stages,)), dma((stages,)), dma((9,)),
+            pltpu.VMEM((stages,) + bias.shape, F32),
+            dma((back,)), dma((back,)), dma((stages,)), dma((stages,)), dma((8,)),
         ]
         + gathering_scratch(6, dp, stages, held, cols),
         compiler_params=pltpu.CompilerParams(
@@ -653,30 +717,129 @@
     )(*weights, bias, tokens, gain, factor, seg_q, seg_k)
 
 
-def backward_kernel(block, dp_bits, stages, count, *refs):
-    q_ref, k_ref, kt_ref, v_ref, g_ref, lse_ref, delta_ref, seg_query, seg_key, wk, wv = refs[:11]
-    grads, refs = refs[11 : 11 + count], refs[11 + count :]
-    dq_ref, dk_ref, dv_ref, incoming = refs[:4]
-    outs, refs = refs[4 : 4 + count], refs[4 + count :]
-    dqt, bias, part, ps, pr, refs = refs[0], refs[1], refs[2], refs[3], refs[4], refs[5:]
+def middle_kernel(block, dp_bits, stages, *refs):
+    sources, refs = refs[:12], refs[12:]
+    b_up, b_down, gain, factor, lse_ref, seg_query, seg_key = refs[:7]
+    results, incoming, outs, sums, refs = refs[7:12], refs[12], refs[13:16], refs[16], refs[17:]
+    weights, hidden, wide, tmp, tr, keys, values, query_in, grad_in, bias, delta_ref = refs[:11]
+    ps, pr, sems, refs = refs[11], refs[12], refs[13], refs[14:]
     d, z = greet(dp_bits, stages)
-    work = Reduction(dp_bits, stages, d, z, grads, outs, refs)
-    for w in range(count):
-        work.begin(w)
-    rows, features = q_ref.shape
-    heads, width = features // HD, k_ref.shape[0]
+    work = Reduction(dp_bits, stages, d, z, None, outs, refs)
+    rows, features = query_in.shape
+    heads, width = features // HD, keys.shape[0]
     back = width // rows - 1
+    tile = 2 * LANES
+    w_out, w_up, w_down = weights.at[0], weights.at[1], weights.at[2]
+    w_key, w_value = weights.at[2], weights.at[1]
+    mixed, cot, x, second, active, d_pre, d_attn, spare = (tmp.at[i] for i in range(8))
+    dk, dv = tmp.at[: back + 1], tmp.at[back + 1 : 2 * back + 2]
+    dq, part = tmp.at[2 * back + 2], tmp.at[2 * back + 3]
+    inside = (
+        mixed, w_out, x, cot, w_up, w_down, keys, values, query_in, w_key, w_value, hidden,
+    )
+    outside = (spare, hidden, dq, dk, dv)
+    loads = Loads(list(zip(sources, inside)) + list(zip(outside, results)), sems)
+    loads.start(*range(9))
     fill_bias(seg_query, seg_key, bias, block, width - rows)
-    dk_ref[...] = jnp.zeros_like(dk_ref)
-    dv_ref[...] = jnp.zeros_like(dv_ref)
-    dqt[...] = jnp.zeros_like(dqt)
+
+    def by_tile(body):
+        def step(c, carry):
+            body(pl.ds(pl.multiple_of(c * tile, tile), tile), c)
+            return carry
+
+        lax.fori_loop(0, features // tile, step, 0)
+
+    def by_rows(body, start):
+        def step(i, carry):
+            return body(pl.ds(pl.multiple_of(i * 64, 64), 64), carry)
+
+        return lax.fori_loop(0, rows // 64, step, start)
+
+    def flip(src):
+        for c in range(features // tile):
+            lanes = slice(c * tile, (c + 1) * tile)
+            tr[lanes, :] = src[:, lanes].T
+
+    nothing = jnp.zeros((1, features), F32)
+
+    def add_attention(lanes, c):
+        hidden[:, lanes] = x[:, lanes].astype(F32) + dot(mixed[...], w_out[lanes, :], 1, 1)
+
+    def norm(at, carry):
+        h = hidden[at, :]
+        second[at, :] = (h * row_inverse(h) * gain[...]).astype(BF16)
+        return carry
+
+    def activate(lanes, c):
+        pre = dot(second[...], w_up[:, lanes], 1, 0) + b_up[:, lanes]
+        sigma = 1.0 / (1.0 + jnp.exp(-pre))
+        active[:, lanes] = (pre * sigma).astype(BF16)
+        grad = dot(cot[...], w_down[:, lanes], 1, 0)
+        grad = (grad * sigma * (1.0 + pre * (1.0 - sigma))).astype(BF16)
+        d_pre[:, lanes] = grad
+        sums[2:3, lanes] = jnp.sum(grad.astype(F32), axis=0, keepdims=True)
+
+    def finish_layer(lanes, c):
+        out = dot(active[...], w_down[lanes, :], 1, 1)
+        spare[:, lanes] = (hidden[:, lanes] + out + b_down[:, lanes]).astype(BF16)
+        sums[1:2, lanes] = jnp.sum(cot[:, lanes].astype(F32), axis=0, keepdims=True)
+
+    def to_second(lanes, c):
+        wide[:, lanes] = dot(d_pre[...], w_up[lanes, :], 1, 1)
+
+    def to_hidden(at, column):
+        h, grad = hidden[at, :], wide[at, :]
+        inverse = row_inverse(h)
+        weighted = grad * gain[...]
+        dots = jnp.sum(weighted * h, axis=1, keepdims=True)
+        cube = inverse * inverse * inverse
+        d_hidden = cot[at, :].astype(F32) + inverse * weighted - h * cube / features * dots
+        hidden[at, :] = d_hidden
+        d_attn[at, :] = d_hidden.astype(BF16)
+        return column + jnp.sum(grad * h * inverse, axis=0, keepdims=True)
+
+    def to_mixed(lanes, c):
+        grad = dot(d_attn[...], w_out[:, lanes], 1, 0).astype(BF16)
+        grad_in[:, lanes] = grad
+        both = grad.astype(F32) * mixed[:, lanes].astype(F32)
+        lane = lax.broadcasted_iota(jnp.int32, (heads, tile), 1) + c * tile
+        first = lax.broadcasted_iota(jnp.int32, (heads, tile), 0) * HD
+        owner = jnp.where((lane >= first) & (lane < first + HD), 1.0, 0.0).astype(BF16)
+        high = both.astype(BF16)
+        rest = (both - high.astype(F32)).astype(BF16)
+        delta_ref[...] += dot(owner, high, 1, 1) + dot(owner, rest, 1, 1)
+
+    events = work.schedule(range(3))
+    sums[3:8, :] = jnp.zeros((5, features), F32)
+    delta_ref[...] = jnp.zeros_like(delta_ref)
+    loads.wait(0, 1, 2)
+    by_tile(add_attention)
+    by_rows(norm, 0)
+    loads.wait(3, 4, 5)
+    by_tile(activate)
+    flip(cot)
+    work.weight_grad(0, lambda at: tr[at, :], lambda: active[...])
+    by_tile(finish_layer)
+    loads.start(12, 9)
+    by_tile(to_second)
+    loads.start(10)
+    flip(second)
+    work.weight_grad(1, lambda at: tr[at, :], lambda: d_pre[...])
+    events[0]()
+    sums[0:1, :] = by_rows(to_hidden, nothing)
+    loads.start(13)
+    by_tile(to_mixed)
+    flip(d_attn)
+    work.weight_grad(2, lambda at: tr[at, :], lambda: mixed[...])
+    events[1]()
+    loads.wait(12)
+    for c in range(2 * back + 2):
+        tmp[c] = jnp.zeros((rows, features), BF16)
+    wide[...] = jnp.zeros_like(wide)
+    loads.wait(6, 7, 8)
     sp = spans(rows, width, block)
     steps = heads * (back + 1)
-    due = {}
-    for w in range(count):
-        for r, at in enumerate((0.16 + 0.08 * w, 0.56 + 0.25 * w, 0.74 + 0.25 * w)[:dp_bits]):
-            if at < 1:
-                due[w, r] = int(at * steps)
+    due = {i + 2: int(at * steps) // 2 * 2 for i, at in enumerate(EVENTS[: len(events) - 2])}
 
     def down():
         return pltpu.make_async_remote_copy(
@@ -686,61 +849,73 @@
 
     for c in range(back + 1):
 
-        def head(h, carry):
-            for at in sorted(set(due.values())):
-                if at // heads != c:
-                    continue
-
-                @pl.when(h == at % heads)
-                def _():
-                    for w, r in sorted(due, key=lambda e: (e[1], e[0])):
-                        if due[w, r] == at:
-                            work.advance(w, r)
-
+        def head(h):
             lanes, mine = head_lanes(h, features)
-            feats = pl.ds(pl.multiple_of(h * HD, 16), HD)
             zero = jnp.zeros((), BF16)
-            query = jnp.where(mine, q_ref[:, lanes], zero)
-            grad = jnp.where(mine, g_ref[:, lanes], zero)
+            query = jnp.where(mine, query_in[:, lanes], zero)
+            grad = jnp.where(mine, grad_in[:, lanes], zero)
             lse = lse_ref[pl.ds(h, 1), :]
             delta = delta_ref[pl.ds(h, 1), :]
-            acc = [None for _ in sp]
             for kb in range(c * rows // block, (c + 1) * rows // block):
                 qs = [i for i, (lo, hi) in enumerate(sp) if lo <= kb * block < hi]
                 if not qs:
                     continue
                 qa, qz = qs[0] * block, (qs[-1] + 1) * block
                 at = slice(kb * block, (kb + 1) * block)
-                s = dot(k_ref[at, lanes], query[qa:qz], 1, 1) + bias[at, qa:qz]
+                to = slice(kb * block - c * rows, (kb + 1) * block - c * rows)
+                key = keys[at, lanes]
+                s = dot(key, query[qa:qz], 1, 1) + bias[at, qa:qz]
                 p = jnp.exp(s - lse[:, qa:qz])
-                dp = dot(v_ref[at, lanes], grad[qa:qz], 1, 1)
+                dp = dot(values[at, lanes], grad[qa:qz], 1, 1)
                 ds = (p * (dp - delta[:, qa:qz])).astype(BF16)
-                dv_ref[at, lanes] += dot(p.astype(BF16), grad[qa:qz], 1, 0).astype(BF16)
-                dk_ref[at, lanes] += dot(ds, query[qa:qz], 1, 0).astype(BF16)
-                share = dot(kt_ref[feats, at], ds, 1, 0)
-                for i in qs:
-                    piece = share[:, i * block - qa : (i + 1) * block - qa]
-                    acc[i] = piece if acc[i] is None else acc[i] + piece
-            for i in range(len(sp)):
-                if acc[i] is not None:
-                    dqt[feats, i * block : (i + 1) * block] += acc[i]
+                dv[c, to, lanes] += dot(p.astype(BF16), grad[qa:qz], 1, 0).astype(BF16)
+                dk[c, to, lanes] += dot(ds, query[qa:qz], 1, 0).astype(BF16)
+                wide[qa:qz, lanes] += dot(ds, jnp.where(mine, key, zero), 0, 0)
+
+        def pair(i, carry):
+            for at in sorted(set(due.values())):
+                if at // heads != c:
+                    continue
+
+                @pl.when(2 * i == at % heads)
+                def _():
+                    for e in due:
+                        if due[e] == at:
+                            events[e]()
+
+            head(2 * i)
+            head(2 * i + 1)
             return carry
 
-        lax.fori_loop(0, heads, head, 0)
-        if c == 0 and back:
-            back_project(part, ((dk_ref, wk), (dv_ref, wv)), 0, None)
-
-            @pl.when(z >= back)
-            def _():
-                down().start()
-
-    transpose_out(dqt, dq_ref)
-    for w in range(count):
-        for r in range(dp_bits):
-            if (w, r) not in due:
-                work.advance(w, r)
-    for w in range(count):
+        lax.fori_loop(0, heads // 2, pair, 0)
+        if c == 0:
+            loads.wait(9, 10)
+            if back:
+                back_project(part, ((dk.at[0], w_key), (dv.at[0], w_value)), 0, None)
+
+                @pl.when(z >= back)
+                def _():
+                    down().start()
+
+            loads.wait(13)
+            loads.start(11)
+
+    loads.start(15, 16)
+    loads.wait(11)
+
+    def to_query(at, column):
+        scaled = wide[at, :].astype(BF16).astype(F32)
+        dq[at, :] = (scaled * factor[...]).astype(BF16)
+        return column + jnp.sum(scaled * hidden[at, :], axis=0, keepdims=True)
+
+    sums[4:5, :] = by_rows(to_query, nothing)
+    loads.start(14)
+    for i in range(2, len(events)):
+        if i not in due:
+            events[i]()
+    for w in range(3):
         work.finish(w)
+    loads.wait(14, 15, 16)
     if back:
 
         @pl.when((z + 1 >= back) & (z < stages - 1))
@@ -773,45 +948,62 @@
     lax.fori_loop(0, features // tile, step, 0)
 
 
-def attend_backward(q, k, kt, v, g, lse, delta, seg_q, seg_k, wk, wv, block, grads, dp, stages):
+def middle(
+    mixed, w_out, x, cot, w_up, w_down, k, v, q, w_key, w_value, raw, b_up, b_down, gain, factor,
+    lse, seg_q, seg_k, block, dp, stages,
+):
     rows, features = q.shape
-    width, count = k.shape[0], len(grads)
-    held, cols = grads[0].shape[0] // dp, features // stages
+    width, heads = k.shape[0], features // HD
+    held, cols = features // dp, features // stages
+    chunks = width // rows
     hbm = pl.BlockSpec(memory_space=pl.ANY)
     vmem = pl.BlockSpec(memory_space=pltpu.VMEM)
     dma = pltpu.SemaphoreType.DMA
     sds = jax.ShapeDtypeStruct
-    out = pl.pallas_call(
-        functools.partial(backward_kernel, block, dp.bit_length() - 1, stages, count),
-        in_specs=[vmem] * 11 + [hbm] * count,
-        out_specs=[vmem] * 3 + [hbm] + [vmem] * count,
-        out_shape=[
-            sds((rows, features), BF16), sds((width, features), BF16), sds((width, features), BF16),
-            sds((rows, features), BF16),
+    low, high = sds((rows, features), BF16), sds((rows, features), F32)
+    many = sds((chunks, rows, features), BF16)
+    return pl.pallas_call(
+        functools.partial(middle_kernel, block, dp.bit_length() - 1, stages),
+        in_specs=[hbm] * 12 + [vmem] * 7,
+        out_specs=[hbm] * 6 + [vmem] * 4,
+        out_shape=[low, high, low, many, many, low]
+        + [sds((held, cols), F32)] * 3
+        + [sds((8, features), F32)],
+        scratch_shapes=[
+            pltpu.VMEM((3, features, features), BF16),
+            pltpu.VMEM((rows, features), F32),
+            pltpu.VMEM((rows, features), F32),
+            pltpu.VMEM((max(8, 2 * chunks + 2), rows, features), BF16),
+            pltpu.VMEM((features, rows), BF16),
+            pltpu.VMEM((width, features), BF16),
+            pltpu.VMEM((width, features), BF16),
+            pltpu.VMEM((rows, features), BF16),
+            pltpu.VMEM((rows, features), BF16),
+            pltpu.VMEM((width, rows), F32),
+            pltpu.VMEM((heads, rows), F32),
+            dma, dma, dma((17,)),
         ]
-        + [sds((held, cols), F32)] * count,
-        scratch_shapes=[
-            pltpu.VMEM((features, rows), F32), pltpu.VMEM((width, rows), F32),
-            pltpu.VMEM((rows, features), BF16), dma, dma,
-        ]
-        + reduction_scratch(count, dp, stages, held, features),
+        + reduction_scratch(3, dp, stages, held, features, True),
         compiler_params=pltpu.CompilerParams(
-            collective_id=2, has_side_effects=True, vmem_limit_bytes=62 << 20
+            collective_id=2, has_side_effects=True, vmem_limit_bytes=63 << 20
         ),
-        name="attend_backward",
+        name="middle",
     )(
-        q, k, kt, v, g, lse, delta, seg_q, seg_k, wk, wv,
-        *[a.reshape(dp, held, features) for a in grads],
+        mixed, w_out, x, cot, w_up, w_down, k, v, q, w_key, w_value, raw, b_up, b_down, gain,
+        factor, lse, seg_q, seg_k,
     )
-    return out[:4], out[4:]
-
-
-def input_kernel(dp_bits, stages, back, lead, *refs):
-    nt, dq, dk, dv, wq, wk, wv, incoming, tokens, d_hidden, gain, sums = refs[:12]
-    outs, tokens_grad, total, refs = refs[12:15], refs[15], refs[16], refs[17:]
-    part, landed, d_first, sgot, ss, sr, ps, pr = refs[:8]
+
+
+def input_kernel(dp_bits, stages, back, *refs):
+    sources, gain, sums, refs = refs[:10], refs[10], refs[11], refs[12:]
+    outs, result, total, refs = refs[:3], refs[3], refs[4], refs[5:]
+    inside, tokens_grad, refs = refs[:10], refs[10], refs[11:]
+    dv, nt, dk, wk, wv, incoming, dq, wq, tokens, d_hidden = inside
+    part, landed, d_first, sgot, ss, sr, ps, pr, sems = refs[:9]
     d, z = greet(dp_bits, stages)
-    work = Reduction(dp_bits, stages, d, z, None, outs, refs[8:])
+    work = Reduction(dp_bits, stages, d, z, None, outs, refs[9:])
+    loads = Loads(list(zip(sources, inside)) + [(tokens_grad, result)], sems)
+    loads.start(*range(10))
     rows, features = tokens.shape
     own = back * rows
     levels = dp_bits + stages.bit_length() - 1
@@ -835,19 +1027,7 @@
 
     def weight_grad(i):
         grad, w, at = grads[i]
-
-        def step(t, carry):
-            rows_at = pl.ds(pl.multiple_of(t * 2 * held, 2 * held), 2 * held)
-            value = dot(nt[rows_at, at:], grad[...], 1, 0).astype(BF16)
-            for low in range(2):
-                which = lax.rem(bit_of(d, 0) + low, 2)
-                for u in work.units(w):
-                    cut = low * held + u % work.parts * work.rows
-                    work.pool[which, u, work.slot_of(u, t)] = value[cut : cut + work.rows]
-            return carry
-
-        lax.fori_loop(0, 1 << (dp_bits - 1), step, 0)
-        work.begin(w)
+        work.weight_grad(w, lambda rows_at: nt[rows_at, at:], lambda: grad[...])
 
     def sum_copy(k):
         if k < dp_bits:
@@ -879,19 +1059,25 @@
         def _():
             down(hop).start()
 
+    events = work.schedule((2, 1, 0))
+    loads.wait(0, 1)
+    weight_grad(0)
+    loads.wait(2, 3, 4, 5)
     if back > 1:
         pass_down(1)
-    weight_grad(0)
+    events[0]()
     weight_grad(1)
-    work.advance(2, 0)
+    loads.wait(6, 7)
     weight_grad(2)
-    work.advance(1, 0)
+    events[1]()
     for hop in range(2, back):
         pass_down(hop)
+    events[2]()
     back_project(d_first, ((dk, wk), (dv, wv), (dq, wq)), own, None)
-    work.advance(0, 0)
-    if dp_bits > 1:
-        work.advance(2, 1)
+    early = 4 if dp_bits > 1 else 3
+    for i in range(3, early):
+        events[i]()
+    loads.wait(8, 9)
     there, take = arrived(back) if back else (None, None)
     if back > 1:
 
@@ -919,13 +1105,12 @@
 
     column = lax.fori_loop(0, rows // chunk, finish, jnp.zeros((1, features), F32))
     total[0] = sums[...]
-    for c in range(features // LANES):
-        total[0, lead + c : lead + c + 1, :] = column[:, c * LANES : (c + 1) * LANES]
+    total[0, 3:4, :] = column
     work.start(sum_copy, 0)
+    loads.start(10)
     done = 0
-    rest = [(w, k) for w in (2, 1, 0) for k in range(1, dp_bits) if (w, k) != (2, 1)]
-    for w, k in rest:
-        work.advance(w, k)
+    for event in events[early:]:
+        event()
         if done < levels:
             sum_step(done)
             done += 1
@@ -939,41 +1124,44 @@
         def _():
             down(hop).wait_send()
 
+    loads.wait(10)
     work.close()
 
 
 def input_gradients(
-    nt, dq, dk, dv, wq, wk, wv, incoming, tokens, d_hidden, gain, sums, lead, dp, stages
+    nt, dq, dk, dv, wq, wk, wv, incoming, tokens, d_hidden, gain, sums, dp, stages
 ):
     rows, features = tokens.shape
     back = dk.shape[0] // rows - 1
     held, cols = features // dp, features // stages
     dp_bits = dp.bit_length() - 1
     levels = dp_bits + stages.bit_length() - 1
-    lines = sums.shape[0]
+    hbm = pl.BlockSpec(memory_space=pl.ANY)
     vmem = pl.BlockSpec(memory_space=pltpu.VMEM)
     dma = pltpu.SemaphoreType.DMA
     hops = max(1, back - 1)
+    sources = (dv, nt, dk, wk, wv, incoming, dq, wq, tokens, d_hidden)
     out = pl.pallas_call(
-        functools.partial(input_kernel, dp_bits, stages, back, lead),
-        in_specs=[vmem] * 12,
-        out_specs=[vmem] * 5,
+        functools.partial(input_kernel, dp_bits, stages, back),
+        in_specs=[hbm] * 10 + [vmem] * 2,
+        out_specs=[vmem] * 3 + [hbm, vmem],
         out_shape=[jax.ShapeDtypeStruct((held, cols), F32)] * 3
         + [
             jax.ShapeDtypeStruct((rows, features), BF16),
-            jax.ShapeDtypeStruct((levels + 1, lines, LANES), F32),
+            jax.ShapeDtypeStruct((levels + 1,) + sums.shape, F32),
         ],
-        scratch_shapes=[
+        scratch_shapes=[pltpu.VMEM(a.shape, a.dtype) for a in sources + (tokens,)]
+        + [
             pltpu.VMEM((hops, rows, features), BF16), pltpu.VMEM((hops, rows, features), BF16),
-            pltpu.VMEM((rows, features), F32), pltpu.VMEM((levels, lines, LANES), F32),
-            dma((levels,)), dma((levels,)), dma((hops,)), dma((hops,)),
+            pltpu.VMEM((rows, features), F32), pltpu.VMEM((levels,) + sums.shape, F32),
+            dma((levels,)), dma((levels,)), dma((hops,)), dma((hops,)), dma((11,)),
         ]
         + reduction_scratch(3, dp, stages, held, features, True),
         compiler_params=pltpu.CompilerParams(
             collective_id=1, has_side_effects=True, vmem_limit_bytes=62 << 20
         ),
         name="input_gradients",
-    )(nt, dq, dk, dv, wq, wk, wv, incoming, tokens, d_hidden, gain, sums)
+    )(*sources, gain, sums)
     return out[:3], out[3], out[4][levels]
 
 
@@ -989,8 +1177,6 @@
     own = back * rows
     block = min(256, rows)
 
-    inputs = tokens.astype(F32)
-    inv_first = row_inverse(inputs)
     seg_wide = jnp.concatenate([jnp.full((own,), -1, jnp.int32), seg])
     seg_window = lax.dynamic_slice_in_dim(seg_wide, z * rows, own + rows, 0)
     seg_query = seg_window[own:]
@@ -999,78 +1185,30 @@
     heads = features // HD
     factor = jax.nn.softplus(query_scale) * (LOG2E / math.sqrt(HD))
     factor_cols = jnp.tile(factor, heads)
+    dp = lax.axis_size("dp")
     (
-        wq, wk, wv, wu, wo, wd, b_all, query_raw, scaled, keys, keys_t, values, first_t, mixed, lse
+        wq, wk, wv, wu, wo, wd, b_full, query_raw, scaled, keys, values, first_t, mixed, lse
     ) = attend_forward(
         (w_query, w_key, w_value, w_up, w_output.T, w_down.T), b_up[None], tokens,
-        gain_attn[None], factor_cols[None], seg_query, seg_key, block,
-        lax.axis_size("dp"), stages, back,
+        gain_attn[None], factor_cols[None], seg_query, seg_key, block, dp, stages, back,
     )
-    b_full = b_all[(z - jnp.arange(stages)) % stages].reshape(-1)
-
-    hidden = inputs + dot(mixed, wo, 1, 1)
-    inv_second = row_inverse(hidden)
-    second = (hidden * inv_second * gain_mlp).astype(BF16)
-    preact = jnp.dot(second, wu, preferred_element_type=F32) + b_full
-    active = jax.nn.silu(preact).astype(BF16)
-    layer_out = (hidden + dot(active, wd, 1, 1) + b_down).astype(BF16)
-
-    upstream = cotangent.astype(F32)
-    sigma = jax.nn.sigmoid(preact)
-    d_active = dot(cotangent, wd, 1, 0)
-    d_preact = (d_active * sigma * (1.0 + preact * (1.0 - sigma))).astype(BF16)
-    d_second = dot(d_preact, wu, 1, 1)
-    weighted = d_second * gain_mlp
-    dots = jnp.sum(weighted * hidden, axis=1, keepdims=True)
-    cube = inv_second * inv_second * inv_second
-    d_hidden = upstream + inv_second * weighted - hidden * cube / features * dots
-    d_attn = d_hidden.astype(BF16)
-    d_mixed = dot(d_attn, wo, 1, 0).astype(BF16)
-
-    owner = (jnp.arange(features)[None, :] // HD == jnp.arange(heads)[:, None]).astype(F32)
-    delta = lax.dot_general(
-        owner, d_mixed.astype(F32) * mixed.astype(F32), (((1,), (1,)), ((), ())),
-        precision=lax.Precision.HIGHEST, preferred_element_type=F32,
+    layer_out, d_hidden, d_query, d_keys, d_values, incoming, *mlp, sums = middle(
+        mixed, wo, tokens, cotangent, wu, wd, keys, values, scaled, wk, wv, query_raw,
+        b_full, b_down[None], gain_mlp[None], factor_cols[None], lse, seg_query, seg_key,
+        block, dp, stages,
     )
-    (d_scaled, d_keys, d_values, incoming), mlp_grads = attend_backward(
-        scaled, keys, keys_t, values, d_mixed, lse, delta, seg_query, seg_key, wk, wv, block,
-        [
-            dot(second, d_preact, 0, 0).astype(BF16),
-            dot(d_attn, mixed, 0, 0).astype(BF16),
-            dot(cotangent, active, 0, 0).astype(BF16),
-        ],
-        lax.axis_size("dp"), stages,
-    )
-    d_scaled_wide = d_scaled.astype(F32)
-    d_query = (d_scaled_wide * factor_cols).astype(BF16)
-    scale_part = jnp.sum(jnp.sum(d_scaled_wide * query_raw, axis=0).reshape(heads, HD), axis=0)
-
-    grad_gain_mlp = jnp.sum(d_second * hidden * inv_second, axis=0)
-    grad_b_up = jnp.sum(d_preact.astype(F32), axis=0)
-    sums = jnp.concatenate(
-        [
-            grad_gain_mlp, jnp.sum(upstream, axis=0), grad_b_up, jnp.zeros((features,), F32),
-            scale_part,
-        ]
-    )
-    lines = -(-sums.shape[0] // (8 * LANES)) * 8
     grads, tokens_grad, sums = input_gradients(
-        first_t, d_query, d_keys, d_values, wq, wk, wv, incoming, tokens, d_hidden,
-        gain_attn[None],
-        jnp.pad(sums, (0, lines * LANES - sums.shape[0])).reshape(lines, LANES),
-        3 * features // LANES, lax.axis_size("dp"), stages,
-    )
-    sums = sums.reshape(-1)[: 4 * features + HD]
-    sum_gain_mlp, sum_b_down, sum_b_up, sum_gain_attn, scale_total = jnp.split(
-        sums, [features, 2 * features, 3 * features, 4 * features]
+        first_t, d_query, d_keys.reshape(own + rows, features),
+        d_values.reshape(own + rows, features), wq, wk, wv, incoming, tokens, d_hidden,
+        gain_attn[None], sums, dp, stages,
     )
     mine = b_up.shape[0]
-    sum_b_up = lax.dynamic_slice_in_dim(sum_b_up, z * mine, mine, 0)
+    sum_b_up = lax.dynamic_slice_in_dim(sums[2], z * mine, mine, 0)
+    scale_total = jnp.sum(sums[4].reshape(heads, HD), axis=0)
     grad_query_scale = scale_total * (LOG2E / math.sqrt(HD)) * jax.nn.sigmoid(query_scale)
-
     return (
-        layer_out, tokens_grad, grads[0], grads[1], grads[2], mlp_grads[1].T, mlp_grads[0],
-        sum_b_up, mlp_grads[2].T, sum_b_down, sum_gain_attn, sum_gain_mlp, grad_query_scale,
+        layer_out, tokens_grad, grads[0], grads[1], grads[2], mlp[2].T, mlp[1], sum_b_up,
+        mlp[0].T, sums[1], sums[3], sums[0], grad_query_scale,
     )
 
 

time: 371 us -> 340 us (0.916); the launches traced: 364 us -> 340 us
  matrix products: 29.6 us -> 0 us
  Pallas kernels: 309 us -> 320 us
  other arithmetic: 5.73 us -> 1.22 us
    dot_general x10 -> x0, matrix products: 29.6 us -> none  [the longest x8 25.5 us: dot(): lax.dot_general(a, b, (((ca,), (cb,)), ((), ())), preferred_element_type=...]
    pallas_call x2, Pallas kernels: 185 us -> 197 us  [the longest x1 118 us: middle(): pl.pallas_call(functools.partial(middle_kernel, block, dp.bit_length() -...]
    reduce_sum x3 -> x1, other arithmetic: 4.4 us -> 0.02 us  [body(): scale_total = jnp.sum(sums[4].reshape(heads, HD), axis=0)]
where the time goes in v2:
time: 340 us
  Pallas kernels  320 us (94%)
  local copies, waits for them, and re-layouts  17.8 us (5%)
    pallas_call x1, Pallas kernels, attend_forward(): pl.pallas_call(functools.partial(forward_kernel, block, dp.bit_length() -...  124 us
    pallas_call x1, Pallas kernels, middle(): pl.pallas_call(functools.partial(middle_kernel, block, dp.bit_length() -...  118 us
    pallas_call x1, Pallas kernels, input_gradients(): pl.pallas_call(functools.partial(input_kernel, dp_bits, stages, back), in...  78.8 us

profile of v2, /device:TPU:0, one launch (start us, length us, event | category | flops | bytes accessed | tf_op | source)
XLA Modules:
  0.0 340.0 jit_solution(5050739311385932423)
XLA Ops:
  0.6 0.7 fusion
  1.3 1.3 pad_dynamic-slice_fusion
  2.7 1.2 broadcast_in_dim.20.refs_6_
  3.9 1.3 broadcast_in_dim.21.refs_8_.refs_10_
  5.2 1.3 broadcast_in_dim.24.refs_13_
  6.5 1.3 broadcast_in_dim.25.refs_14_
  7.8 0.7 broadcast_in_dim_tile.4.refs_9_.refs_15_
  8.5 0.8 pad_dynamic-slice_fusion.1
  9.2 1.1 broadcast_in_dim.26.refs_11_.refs_18_
  10.4 123.6 %attend_forward.1 = (bf16[1280,1280]{1,0:T(8,128)(2,1)}, bf16[1280,1280]{1,0:T(8,128)(2,1)}, bf16[1280,1280]{1,0:T(8,128)(2,1)}, bf16[1280,1280]{1,0:T(8,128)(2,...) custom-call(bf16[160,320]{1,0:T(8,128)(2,1)} %refs_0_.1, ...), custom_call_target="tpu_custom_call" | custom-call | tf_op jit(solution)/shard_map/attend_forward/pallas_call | solution.py:679
  134.0 117.8 %middle.1 = (bf16[512,1280]{1,0:T(8,128)(2,1)}, f32[512,1280]{1,0:T(8,128)}, bf16[512,1280]{1,0:T(8,128)(2,1)}, bf16[3,512,1280]{2,1,0:T(8,128)(2,1)}, bf16[3,51...) custom-call(bf16[512,1280]{1,0:T(8,128)(2,1)} %get-tuple-element.42., ...), custom_call_target="tpu_custom_call" | custom-call | tf_op jit(solution)/shard_map/middle/pallas_call | solution.py:965
  251.8 0.0 copy-start.8
  251.8 0.0 copy-start
  251.9 78.8 %input_gradients.1 = (f32[160,320]{1,0:T(8,128)}, f32[160,320]{1,0:T(8,128)}, f32[160,320]{1,0:T(8,128)}, bf16[512,1280]{1,0:T(8,128)(2,1)}, f32[6,8,1280]{2,1,0:T(8,128)}) custom-call(bf16[1536,1280]{1,0:T(8,128)(2,1)} %bitcast.9, bf16[1280,1536]{1,0:T(8,128)(2,1)} %get-tuple-element.56.refs_1_, bf16[1536,1280]{1,0:T(8,128)(2,1)} %bitcast.8, ...), custom_call_target="tpu_custom_call" | custom-call | tf_op jit(solution)/shard_map/input_gradients/pallas_call | solution.py:1144
  330.7 0.0 copy-start.1
  330.7 1.7 slice_reduce_fusion
  332.4 0.1 reshape_squeeze.3
  332.5 0.0 copy-done.8
  332.5 0.5 divide_multiply_fusion
  333.0 0.7 dynamic-slice_reduce_fusion
  333.7 0.0 copy-done
  333.7 0.0 copy-start.7
  333.7 0.0 copy-start.6
  333.7 0.0 copy-start.5
  333.7 1.1 copy.37
  334.7 0.0 copy-done.1
  334.7 0.0 copy-start.4
  334.8 0.0 copy-start.3
  334.8 0.0 copy-start.2
  334.8 1.1 copy.38
  335.8 0.0 copy-done.7
  335.8 0.7 copy.39
  336.5 0.0 copy-done.6
  336.5 0.7 copy.40
  337.2 0.0 copy-done.5
  337.2 0.7 copy.41
  337.9 0.0 copy-done.4
  337.9 0.7 copy.42
  338.6 0.0 copy-done.3
  338.6 0.7 copy.43
  339.3 0.0 copy-done.2
  339.3 0.7 copy.44
  (2 shorter events, 0.0 us)
Async XLA Ops:
  251.8 80.6 %copy-start.8 = (f32[80]{0:T(128)S(1)}, f32[80]{0:T(128)}, u32[]{:S(2)}) copy-start(f32[80]{0:T(128)} %param.26) | copy-start | bytes 964
  251.8 81.8 %copy-start = (bf16[512,1280]{1,0:T(8,128)(2,1)S(1)}, bf16[512,1280]{1,0:T(8,128)(2,1)}, u32[]{:S(2)}) copy-start(bf16[512,1280]{1,0:T(8,128)(2,1)} %get-tuple-element.89) | copy-start | bytes 3932164
  330.7 4.1 %copy-start.1 = (bf16[512,1280]{1,0:T(8,128)(2,1)S(1)}, bf16[512,1280]{1,0:T(8,128)(2,1)}, u32[]{:S(2)}) copy-start(bf16[512,1280]{1,0:T(8,128)(2,1)} %get-tuple-element.90) | copy-start | bytes 3932164
  333.7 2.1 copy-start.7
  333.7 2.8 copy-start.6
  333.7 3.5 %copy-start.5 = (f32[160,320]{1,0:T(8,128)S(1)}, f32[160,320]{1,0:T(8,128)}, u32[]{:S(2)}) copy-start(f32[160,320]{1,0:T(8,128)} %get-tuple-element.93) | copy-start | bytes 614404
  334.7 3.2 copy-start.4
  334.8 3.9 %copy-start.3 = (f32[160,320]{1,0:T(8,128)S(1)}, f32[160,320]{1,0:T(8,128)}, u32[]{:S(2)}) copy-start(f32[160,320]{1,0:T(8,128)} %get-tuple-element.95) | copy-start | bytes 614404
  334.8 4.5 %copy-start.2 = (f32[160,320]{1,0:T(8,128)S(1)}, f32[160,320]{1,0:T(8,128)}, u32[]{:S(2)}) copy-start(f32[160,320]{1,0:T(8,128)} %get-tuple-element.70) | copy-start | bytes 614404

commit v3 on v2

--- a/solution.py
+++ b/solution.py
@@ -14,7 +14,7 @@
 LOG2E = 1.442695
 DOC_MAX = 1024
 FAR = -1e30
-EVENTS = (0.04, 0.1, 0.25, 0.32, 0.46, 0.6, 0.75)
+EVENTS = (0.15, 0.3, 0.5, 0.6, 0.75, 0.9)
 F32 = jnp.float32
 BF16 = jnp.bfloat16
 
@@ -164,7 +164,7 @@
 
     def add(self, dst, src, count):
         def step(i, carry):
-            dst[i] = (dst[i].astype(F32) + src(i).astype(F32)).astype(BF16)
+            dst[i] = dst[i] + src(i)
             return carry
 
         lax.fori_loop(0, count, step, 0)
@@ -187,30 +187,12 @@
         for u in self.units(w):
             self.start(self.round_copy, u, k)
 
-    def schedule(self, order):
-        events = []
-        ahead = 2
-
-        def event(w, k, starts):
-            def run():
-                self.take(w, k)
-                if k and k + 1 < self.dp_bits:
-                    self.send(w, k + 1)
-                for other in starts:
-                    self.send(other, 1)
-                if k + 1 == self.dp_bits:
-                    self.begin_last(w)
-
-            return run
-
-        for i, w in enumerate(order):
-            starts = [w] if i < ahead and self.dp_bits > 1 else []
-            events.append(event(w, 0, starts))
-        for i, w in enumerate(order):
-            for k in range(1, self.dp_bits):
-                starts = [order[i + ahead]] if k == 1 and i + ahead < len(order) else []
-                events.append(event(w, k, starts))
-        return events
+    def advance(self, w, k):
+        self.take(w, k)
+        if k + 1 == self.dp_bits:
+            self.begin_last(w)
+        else:
+            self.send(w, k + 1)
 
     def put(self, w, index, value):
         held = self.parts * self.rows
@@ -434,8 +416,9 @@
 
 def forward_kernel(block, dp_bits, stages, back, *refs):
     weights, refs = refs[:6], refs[6:]
-    bias_in, tokens, gain, factor, seg_query, seg_key = refs[:6]
-    fulls, refs = refs[6:12], refs[12:]
+    bias_in, tokens, vectors, seg_query, seg_key = refs[:5]
+    gain, factor = vectors.at[0:1], vectors.at[1:2]
+    fulls, refs = refs[5:11], refs[11:]
     bias_full, raw_out, q_out, k_out, v_out, nt_out, o_ref, lse_ref = refs[:8]
     refs = refs[8:]
     home, window, normed, nt, raw, q, k, v, vt, ot, bias, scores, tops, totals, bias_all = refs[:15]
@@ -668,7 +651,7 @@
     work.close()
 
 
-def attend_forward(weights, bias, tokens, gain, factor, seg_q, seg_k, block, dp, stages, back):
+def attend_forward(weights, bias, tokens, vectors, seg_q, seg_k, block, dp, stages, back):
     held, cols = weights[0].shape
     rows, features = tokens.shape
     width, heads = (back + 1) * rows, features // HD
@@ -678,7 +661,7 @@
     sds = jax.ShapeDtypeStruct
     return pl.pallas_call(
         functools.partial(forward_kernel, block, dp.bit_length() - 1, stages, back),
-        in_specs=[vmem] * 12,
+        in_specs=[vmem] * 11,
         out_specs=[hbm] * 6 + [vmem] + [hbm] * 5 + [vmem] * 2,
         out_shape=[sds((features, features), BF16)] * 6
         + [
@@ -714,13 +697,14 @@
             collective_id=0, has_side_effects=True, vmem_limit_bytes=62 << 20
         ),
         name="attend_forward",
-    )(*weights, bias, tokens, gain, factor, seg_q, seg_k)
+    )(*weights, bias, tokens, vectors, seg_q, seg_k)
 
 
 def middle_kernel(block, dp_bits, stages, *refs):
     sources, refs = refs[:12], refs[12:]
-    b_up, b_down, gain, factor, lse_ref, seg_query, seg_key = refs[:7]
-    results, incoming, outs, sums, refs = refs[7:12], refs[12], refs[13:16], refs[16], refs[17:]
+    b_up, vectors, lse_ref, seg_query, seg_key = refs[:5]
+    factor, gain, b_down = (vectors.at[i : i + 1] for i in (1, 2, 3))
+    results, incoming, outs, sums, refs = refs[5:11], refs[11], refs[12:15], refs[15], refs[16:]
     weights, hidden, wide, tmp, tr, keys, values, query_in, grad_in, bias, delta_ref = refs[:11]
     ps, pr, sems, refs = refs[11], refs[12], refs[13], refs[14:]
     d, z = greet(dp_bits, stages)
@@ -737,17 +721,15 @@
     inside = (
         mixed, w_out, x, cot, w_up, w_down, keys, values, query_in, w_key, w_value, hidden,
     )
-    outside = (spare, hidden, dq, dk, dv)
+    half = rows // 2
+    outside = (spare, hidden, dq, dk, dv, part.at[half:])
     loads = Loads(list(zip(sources, inside)) + list(zip(outside, results)), sems)
     loads.start(*range(9))
     fill_bias(seg_query, seg_key, bias, block, width - rows)
 
     def by_tile(body):
-        def step(c, carry):
-            body(pl.ds(pl.multiple_of(c * tile, tile), tile), c)
-            return carry
-
-        lax.fori_loop(0, features // tile, step, 0)
+        for c in range(features // tile):
+            body(slice(c * tile, (c + 1) * tile), c)
 
     def by_rows(body, start):
         def step(i, carry):
@@ -809,7 +791,6 @@
         rest = (both - high.astype(F32)).astype(BF16)
         delta_ref[...] += dot(owner, high, 1, 1) + dot(owner, rest, 1, 1)
 
-    events = work.schedule(range(3))
     sums[3:8, :] = jnp.zeros((5, features), F32)
     delta_ref[...] = jnp.zeros_like(delta_ref)
     loads.wait(0, 1, 2)
@@ -825,13 +806,15 @@
     loads.start(10)
     flip(second)
     work.weight_grad(1, lambda at: tr[at, :], lambda: d_pre[...])
-    events[0]()
+    work.advance(0, 0)
     sums[0:1, :] = by_rows(to_hidden, nothing)
     loads.start(13)
     by_tile(to_mixed)
     flip(d_attn)
     work.weight_grad(2, lambda at: tr[at, :], lambda: mixed[...])
-    events[1]()
+    work.advance(1, 0)
+    if dp_bits > 1:
+        work.advance(0, 1)
     loads.wait(12)
     for c in range(2 * back + 2):
         tmp[c] = jnp.zeros((rows, features), BF16)
@@ -839,11 +822,12 @@
     loads.wait(6, 7, 8)
     sp = spans(rows, width, block)
     steps = heads * (back + 1)
-    due = {i + 2: int(at * steps) // 2 * 2 for i, at in enumerate(EVENTS[: len(events) - 2])}
+    events = [(2, 0)] + [(w, k) for w in range(3) for k in range(1, dp_bits) if (w, k) != (0, 1)]
+    due = {i: int(at * steps) // 2 * 2 for i, at in enumerate(EVENTS[: len(events)])}
 
     def down():
         return pltpu.make_async_remote_copy(
-            src_ref=part, dst_ref=incoming, send_sem=ps, recv_sem=pr,
+            src_ref=part.at[:half], dst_ref=incoming, send_sem=ps, recv_sem=pr,
             device_id={"mp": jnp.maximum(z - 1, 0)}, device_id_type=MESH,
         )
 
@@ -881,7 +865,7 @@
                 def _():
                     for e in due:
                         if due[e] == at:
-                            events[e]()
+                            work.advance(*events[e])
 
             head(2 * i)
             head(2 * i + 1)
@@ -892,6 +876,7 @@
             loads.wait(9, 10)
             if back:
                 back_project(part, ((dk.at[0], w_key), (dv.at[0], w_value)), 0, None)
+                loads.start(17)
 
                 @pl.when(z >= back)
                 def _():
@@ -910,13 +895,13 @@
 
     sums[4:5, :] = by_rows(to_query, nothing)
     loads.start(14)
-    for i in range(2, len(events)):
-        if i not in due:
-            events[i]()
+    for i in range(len(due), len(events)):
+        work.advance(*events[i])
     for w in range(3):
         work.finish(w)
     loads.wait(14, 15, 16)
     if back:
+        loads.wait(17)
 
         @pl.when((z + 1 >= back) & (z < stages - 1))
         def _():
@@ -949,7 +934,7 @@
 
 
 def middle(
-    mixed, w_out, x, cot, w_up, w_down, k, v, q, w_key, w_value, raw, b_up, b_down, gain, factor,
+    mixed, w_out, x, cot, w_up, w_down, k, v, q, w_key, w_value, raw, b_up, vectors,
     lse, seg_q, seg_k, block, dp, stages,
 ):
     rows, features = q.shape
@@ -961,12 +946,12 @@
     dma = pltpu.SemaphoreType.DMA
     sds = jax.ShapeDtypeStruct
     low, high = sds((rows, features), BF16), sds((rows, features), F32)
-    many = sds((chunks, rows, features), BF16)
+    many, part = sds((chunks, rows, features), BF16), sds((rows // 2, features), BF16)
     return pl.pallas_call(
         functools.partial(middle_kernel, block, dp.bit_length() - 1, stages),
-        in_specs=[hbm] * 12 + [vmem] * 7,
-        out_specs=[hbm] * 6 + [vmem] * 4,
-        out_shape=[low, high, low, many, many, low]
+        in_specs=[hbm] * 12 + [vmem] * 5,
+        out_specs=[hbm] * 7 + [vmem] * 4,
+        out_shape=[low, high, low, many, many, part, part]
         + [sds((held, cols), F32)] * 3
         + [sds((8, features), F32)],
         scratch_shapes=[
@@ -981,7 +966,7 @@
             pltpu.VMEM((rows, features), BF16),
             pltpu.VMEM((width, rows), F32),
             pltpu.VMEM((heads, rows), F32),
-            dma, dma, dma((17,)),
+            dma, dma, dma((18,)),
         ]
         + reduction_scratch(3, dp, stages, held, features, True),
         compiler_params=pltpu.CompilerParams(
@@ -989,32 +974,43 @@
         ),
         name="middle",
     )(
-        mixed, w_out, x, cot, w_up, w_down, k, v, q, w_key, w_value, raw, b_up, b_down, gain,
-        factor, lse, seg_q, seg_k,
+        mixed, w_out, x, cot, w_up, w_down, k, v, q, w_key, w_value, raw, b_up, vectors,
+        lse, seg_q, seg_k,
     )
 
 
 def input_kernel(dp_bits, stages, back, *refs):
-    sources, gain, sums, refs = refs[:10], refs[10], refs[11], refs[12:]
+    sources, farther, vectors, sums, refs = refs[:10], refs[10], refs[11], refs[12], refs[13:]
+    gain = vectors.at[0:1]
     outs, result, total, refs = refs[:3], refs[3], refs[4], refs[5:]
     inside, tokens_grad, refs = refs[:10], refs[10], refs[11:]
     dv, nt, dk, wk, wv, incoming, dq, wq, tokens, d_hidden = inside
     part, landed, d_first, sgot, ss, sr, ps, pr, sems = refs[:9]
     d, z = greet(dp_bits, stages)
     work = Reduction(dp_bits, stages, d, z, None, outs, refs[9:])
+    rows, features = tokens.shape
+    own, half = back * rows, rows // 2
+    inside = inside[:5] + (incoming.at[:half],) + inside[6:]
     loads = Loads(list(zip(sources, inside)) + [(tokens_grad, result)], sems)
-    loads.start(*range(10))
-    rows, features = tokens.shape
-    own = back * rows
     levels = dp_bits + stages.bit_length() - 1
     held = features >> dp_bits
     grads = ((dv, 2, 0), (dk, 1, 0), (dq, 0, own))
 
     def down(hop):
         return pltpu.make_async_remote_copy(
-            src_ref=part.at[hop - 1], dst_ref=landed.at[hop - 1], send_sem=ps.at[hop - 1],
-            recv_sem=pr.at[hop - 1], device_id={"mp": jnp.maximum(z - 1, 0)}, device_id_type=MESH,
+            src_ref=part.at[hop - 1] if hop else farther,
+            dst_ref=landed.at[hop - 1] if hop else incoming.at[half:],
+            send_sem=ps.at[hop], recv_sem=pr.at[hop],
+            device_id={"mp": jnp.maximum(z - 1, 0)}, device_id_type=MESH,
         )
+
+    if back:
+
+        @pl.when(z >= back)
+        def _():
+            down(0).start()
+
+    loads.start(*range(10))
 
     def arrived(hop):
         source = incoming if hop == 1 else landed.at[hop - 2]
@@ -1047,11 +1043,10 @@
 
     def pass_down(hop):
         there, take = arrived(hop)
-        if hop > 1:
-
-            @pl.when(there)
-            def _():
-                down(hop - 1).wait_recv()
+
+        @pl.when(there)
+        def _():
+            down(hop - 1).wait_recv()
 
         back_project(part.at[hop - 1], ((dk, wk), (dv, wv)), hop * rows, take)
 
@@ -1059,27 +1054,27 @@
         def _():
             down(hop).start()
 
-    events = work.schedule((2, 1, 0))
     loads.wait(0, 1)
     weight_grad(0)
-    loads.wait(2, 3, 4, 5)
+    loads.wait(2)
+    weight_grad(1)
+    work.advance(2, 0)
+    loads.wait(3, 4, 5)
     if back > 1:
         pass_down(1)
-    events[0]()
-    weight_grad(1)
+    work.advance(1, 0)
     loads.wait(6, 7)
     weight_grad(2)
-    events[1]()
     for hop in range(2, back):
         pass_down(hop)
-    events[2]()
+    work.advance(0, 0)
     back_project(d_first, ((dk, wk), (dv, wv), (dq, wq)), own, None)
-    early = 4 if dp_bits > 1 else 3
-    for i in range(3, early):
-        events[i]()
+    events = [(w, k) for w in (2, 1, 0) for k in range(1, dp_bits)]
+    for event in events[:1]:
+        work.advance(*event)
     loads.wait(8, 9)
     there, take = arrived(back) if back else (None, None)
-    if back > 1:
+    if back:
 
         @pl.when(there)
         def _():
@@ -1109,8 +1104,8 @@
     work.start(sum_copy, 0)
     loads.start(10)
     done = 0
-    for event in events[early:]:
-        event()
+    for event in events[1:]:
+        work.advance(*event)
         if done < levels:
             sum_step(done)
             done += 1
@@ -1118,7 +1113,7 @@
         sum_step(k)
     for w in (2, 1, 0):
         work.finish(w)
-    for hop in range(1, back):
+    for hop in range(back):
 
         @pl.when(z >= back - hop)
         def _():
@@ -1129,7 +1124,7 @@
 
 
 def input_gradients(
-    nt, dq, dk, dv, wq, wk, wv, incoming, tokens, d_hidden, gain, sums, dp, stages
+    nt, dq, dk, dv, wq, wk, wv, incoming, farther, tokens, d_hidden, vectors, sums, dp, stages
 ):
     rows, features = tokens.shape
     back = dk.shape[0] // rows - 1
@@ -1143,25 +1138,25 @@
     sources = (dv, nt, dk, wk, wv, incoming, dq, wq, tokens, d_hidden)
     out = pl.pallas_call(
         functools.partial(input_kernel, dp_bits, stages, back),
-        in_specs=[hbm] * 10 + [vmem] * 2,
+        in_specs=[hbm] * 11 + [vmem] * 2,
         out_specs=[vmem] * 3 + [hbm, vmem],
         out_shape=[jax.ShapeDtypeStruct((held, cols), F32)] * 3
         + [
             jax.ShapeDtypeStruct((rows, features), BF16),
             jax.ShapeDtypeStruct((levels + 1,) + sums.shape, F32),
         ],
-        scratch_shapes=[pltpu.VMEM(a.shape, a.dtype) for a in sources + (tokens,)]
+        scratch_shapes=[pltpu.VMEM(tokens.shape if a is incoming else a.shape, a.dtype) for a in sources + (tokens,)]
         + [
             pltpu.VMEM((hops, rows, features), BF16), pltpu.VMEM((hops, rows, features), BF16),
             pltpu.VMEM((rows, features), F32), pltpu.VMEM((levels,) + sums.shape, F32),
-            dma((levels,)), dma((levels,)), dma((hops,)), dma((hops,)), dma((11,)),
+            dma((levels,)), dma((levels,)), dma((hops + 1,)), dma((hops + 1,)), dma((11,)),
         ]
         + reduction_scratch(3, dp, stages, held, features, True),
         compiler_params=pltpu.CompilerParams(
             collective_id=1, has_side_effects=True, vmem_limit_bytes=62 << 20
         ),
         name="input_gradients",
-    )(*sources, gain, sums)
+    )(*sources, farther, vectors, sums)
     return out[:3], out[3], out[4][levels]
 
 
@@ -1184,23 +1179,22 @@
 
     heads = features // HD
     factor = jax.nn.softplus(query_scale) * (LOG2E / math.sqrt(HD))
-    factor_cols = jnp.tile(factor, heads)
+    vectors = jnp.stack([gain_attn, jnp.tile(factor, heads), gain_mlp, b_down])
     dp = lax.axis_size("dp")
     (
         wq, wk, wv, wu, wo, wd, b_full, query_raw, scaled, keys, values, first_t, mixed, lse
     ) = attend_forward(
         (w_query, w_key, w_value, w_up, w_output.T, w_down.T), b_up[None], tokens,
-        gain_attn[None], factor_cols[None], seg_query, seg_key, block, dp, stages, back,
+        vectors, seg_query, seg_key, block, dp, stages, back,
     )
-    layer_out, d_hidden, d_query, d_keys, d_values, incoming, *mlp, sums = middle(
+    layer_out, d_hidden, d_query, d_keys, d_values, farther, incoming, *mlp, sums = middle(
         mixed, wo, tokens, cotangent, wu, wd, keys, values, scaled, wk, wv, query_raw,
-        b_full, b_down[None], gain_mlp[None], factor_cols[None], lse, seg_query, seg_key,
-        block, dp, stages,
+        b_full, vectors, lse, seg_query, seg_key, block, dp, stages,
     )
     grads, tokens_grad, sums = input_gradients(
         first_t, d_query, d_keys.reshape(own + rows, features),
-        d_values.reshape(own + rows, features), wq, wk, wv, incoming, tokens, d_hidden,
-        gain_attn[None], sums, dp, stages,
+        d_values.reshape(own + rows, features), wq, wk, wv, incoming, farther, tokens,
+        d_hidden, vectors, sums, dp, stages,
     )
     mine = b_up.shape[0]
     sum_b_up = lax.dynamic_slice_in_dim(sums[2], z * mine, mine, 0)

time: 340 us -> 323 us (0.950)
  Pallas kernels: 320 us -> 302 us
    pallas_call x1, Pallas kernels: 118 us -> 95.8 us  [middle(): pl.pallas_call(functools.partial(middle_kernel, block, dp.bit_length() -...]
    broadcast_in_dim x3 -> x0, local copies, waits for them, and re-layouts: 3.88 us -> none  [the longest x1 1.29 us: body(): gain_attn[None]]
    pallas_call x1, Pallas kernels: 78.8 us -> 82.3 us  [input_gradients(): pl.pallas_call(functools.partial(input_kernel, dp_bits, stages, back), in...]
where the time goes in v3:
time: 323 us; the launch traced here: 320 us
  Pallas kernels  302 us (93%)
  local copies, waits for them, and re-layouts  15.4 us (5%)
    pallas_call x1, Pallas kernels, attend_forward(): pl.pallas_call(functools.partial(forward_kernel, block, dp.bit_length() -...  124 us
    pallas_call x1, Pallas kernels, middle(): pl.pallas_call(functools.partial(middle_kernel, block, dp.bit_length() -...  95.8 us
    pallas_call x1, Pallas kernels, input_gradients(): pl.pallas_call(functools.partial(input_kernel, dp_bits, stages, back), in...  82.3 us

profile of v3, /device:TPU:0, one launch (start us, length us, event | category | flops | bytes accessed | tf_op | source)
XLA Modules:
  0.0 319.6 jit_solution(17538178526264607177)
XLA Ops:
  0.6 0.7 fusion
  1.3 1.3 pad_dynamic-slice_fusion
  2.7 1.2 broadcast_in_dim.10.refs_6_
  3.9 0.7 stack.14
  4.6 0.7 stack.12
  5.3 0.7 stack.13
  6.0 0.1 stack_tile.3
  6.1 0.6 pad_maximum_fusion.refs_8_.refs_13_.refs_11_
  6.7 0.8 pad_dynamic-slice_fusion.1
  7.5 1.1 broadcast_in_dim.13.refs_10_.refs_16_
  8.7 123.5 %attend_forward.1 = (bf16[1280,1280]{1,0:T(8,128)(2,1)}, bf16[1280,1280]{1,0:T(8,128)(2,1)}, bf16[1280,1280]{1,0:T(8,128)(2,1)}, bf16[1280,1280]{1,0:T(8,128)(2,...) custom-call(bf16[160,320]{1,0:T(8,128)(2,1)} %refs_0_.1, ...), custom_call_target="tpu_custom_call" | custom-call | tf_op jit(solution)/shard_map/attend_forward/pallas_call | solution.py:662
  132.2 95.8 %middle.1 = (bf16[512,1280]{1,0:T(8,128)(2,1)}, f32[512,1280]{1,0:T(8,128)}, bf16[512,1280]{1,0:T(8,128)(2,1)}, bf16[3,512,1280]{2,1,0:T(8,128)(2,1)}, bf16[3,51...) custom-call(bf16[512,1280]{1,0:T(8,128)(2,1)} %get-tuple-element.43., ...), custom_call_target="tpu_custom_call" | custom-call | tf_op jit(solution)/shard_map/middle/pallas_call | solution.py:950
  228.0 0.0 copy-start.8
  228.0 0.0 copy-start
  228.0 82.3 %input_gradients.1 = (f32[160,320]{1,0:T(8,128)}, f32[160,320]{1,0:T(8,128)}, f32[160,320]{1,0:T(8,128)}, bf16[512,1280]{1,0:T(8,128)(2,1)}, f32[6,8,1280]{2,1,0:T(8,128)}) custom-call(bf16[1536,1280]{1,0:T(8,128)(2,1)} %bitcast.9, bf16[1280,1536]{1,0:T(8,128)(2,1)} %get-tuple-element.57.refs_1_, bf16[1536,1280]{1,0:T(8,128)(2,1)} %bitcast.8, ...), custom_call_target="tpu_custom_call" | custom-call | tf_op jit(solution)/shard_map/input_gradients/pallas_call | solution.py:1139
  310.3 0.0 copy-start.1
  310.3 0.0 copy-start.6
  310.3 0.0 copy-start.5
  310.3 1.7 slice_reduce_fusion
  312.0 0.1 reshape_squeeze.3
  312.1 0.0 copy-done.8
  312.1 0.0 copy-start.7
  312.1 0.5 divide_multiply_fusion
  312.6 0.7 dynamic-slice_reduce_fusion
  313.3 0.0 copy-done
  313.3 0.0 copy-start.4
  313.3 0.0 copy-start.3
  313.3 0.0 copy-start.2
  313.3 1.1 copy.37
  314.4 0.0 copy-done.1
  314.4 1.1 copy.38
  315.4 0.0 copy-done.7
  315.4 0.7 copy.39
  316.1 0.0 copy-done.6
  316.1 0.7 copy.40
  316.8 0.0 copy-done.5
  316.8 0.7 copy.41
  317.5 0.0 copy-done.4
  317.5 0.7 copy.42
  318.2 0.0 copy-done.3
  318.2 0.7 copy.43
  318.9 0.0 copy-done.2
  318.9 0.7 copy.44
  (2 shorter events, 0.0 us)
Async XLA Ops:
  228.0 84.1 %copy-start.8 = (f32[80]{0:T(128)S(1)}, f32[80]{0:T(128)}, u32[]{:S(2)}) copy-start(f32[80]{0:T(128)} %param.26) | copy-start | bytes 964
  228.0 85.3 %copy-start = (bf16[512,1280]{1,0:T(8,128)(2,1)S(1)}, bf16[512,1280]{1,0:T(8,128)(2,1)}, u32[]{:S(2)}) copy-start(bf16[512,1280]{1,0:T(8,128)(2,1)} %get-tuple-element.91) | copy-start | bytes 3932164
  310.3 4.1 %copy-start.1 = (bf16[512,1280]{1,0:T(8,128)(2,1)S(1)}, bf16[512,1280]{1,0:T(8,128)(2,1)}, u32[]{:S(2)}) copy-start(bf16[512,1280]{1,0:T(8,128)(2,1)} %get-tuple-element.92) | copy-start | bytes 3932164
  310.3 5.8 %copy-start.6 = (f32[160,320]{1,0:T(8,128)S(1)}, f32[160,320]{1,0:T(8,128)}, u32[]{:S(2)}) copy-start(f32[160,320]{1,0:T(8,128)} %get-tuple-element.94) | copy-start | bytes 614404
  310.3 6.5 %copy-start.5 = (f32[160,320]{1,0:T(8,128)S(1)}, f32[160,320]{1,0:T(8,128)}, u32[]{:S(2)}) copy-start(f32[160,320]{1,0:T(8,128)} %get-tuple-element.95) | copy-start | bytes 614404
  312.1 3.3 %copy-start.7 = (f32[160,320]{1,0:T(8,128)S(1)}, f32[160,320]{1,0:T(8,128)}, u32[]{:S(2)}) copy-start(f32[160,320]{1,0:T(8,128)} %get-tuple-element.93) | copy-start | bytes 614404
  313.3 4.2 %copy-start.4 = (f32[160,320]{1,0:T(8,128)S(1)}, f32[160,320]{1,0:T(8,128)}, u32[]{:S(2)}) copy-start(f32[160,320]{1,0:T(8,128)} %get-tuple-element.69) | copy-start | bytes 614404
  313.3 4.9 %copy-start.3 = (f32[160,320]{1,0:T(8,128)S(1)}, f32[160,320]{1,0:T(8,128)}, u32[]{:S(2)}) copy-start(f32[160,320]{1,0:T(8,128)} %get-tuple-element.97) | copy-start | bytes 614404
  313.3 5.6 %copy-start.2 = (f32[160,320]{1,0:T(8,128)S(1)}, f32[160,320]{1,0:T(8,128)}, u32[]{:S(2)}) copy-start(f32[160,320]{1,0:T(8,128)} %get-tuple-element.72) | copy-start | bytes 614404

commit v4 on v3

--- a/solution.py
+++ b/solution.py
@@ -270,14 +270,22 @@
     lane = lax.broadcasted_iota(jnp.int32,(1,2*LANES),1) + (off-first)
     return pl.ds(off, 2*LANES), (lane>=0)&(lane<HD)
 
-def fill_bias(seg_query, seg_key, bias, block, own):
-    rows = seg_query.shape[1]; width=seg_key.shape[0]
-    for kb in range(width//block):
-        for qb in range(rows//block):
-            row = seg_query[:, qb*block:(qb+1)*block]
-            col = seg_key[kb*block:(kb+1)*block,:]
-            ahead = (lax.broadcasted_iota(jnp.int32,(block,block),0)+(kb*block)) <= (lax.broadcasted_iota(jnp.int32,(block,block),1)+(own+qb*block))
-            bias[kb*block:(kb+1)*block, qb*block:(qb+1)*block] = jnp.where((col==row)&ahead, 0.0, FAR)
+def fill_bias(segments, z, bias, block, own):
+    width, rows = bias.shape
+    first = z * rows
+    for kb in range(width // block):
+        start = first + (kb * block - own)
+        at = pl.ds(pl.multiple_of(jnp.maximum(start, 0), block), block)
+        col = jnp.broadcast_to(segments[:, at], (block, block)).T
+        sub = lax.broadcasted_iota(jnp.int32, (block, block), 0) + kb * block
+        for qb in range(rows // block):
+            row = segments[:, pl.ds(pl.multiple_of(first + qb * block, block), block)]
+            last = lax.broadcasted_iota(jnp.int32, (block, block), 1) + (own + qb * block)
+            allowed = (col == row) & (sub <= last) & (start >= 0)
+            bias[kb * block : (kb + 1) * block, qb * block : (qb + 1) * block] = jnp.where(
+                allowed, 0.0, FAR
+            )
+
 
 def transpose_out(src, dst):
     for i in range(src.shape[0]//LANES):
@@ -416,20 +424,20 @@
 
 def forward_kernel(block, dp_bits, stages, back, *refs):
     weights, refs = refs[:6], refs[6:]
-    bias_in, tokens, vectors, seg_query, seg_key = refs[:5]
+    tokens, vectors, segments = refs[:3]
     gain, factor = vectors.at[0:1], vectors.at[1:2]
-    fulls, refs = refs[5:11], refs[11:]
+    fulls, refs = refs[3:9], refs[9:]
     bias_full, raw_out, q_out, k_out, v_out, nt_out, o_ref, lse_ref = refs[:8]
     refs = refs[8:]
-    home, window, normed, nt, raw, q, k, v, vt, ot, bias, scores, tops, totals, bias_all = refs[:15]
-    xs, xr, bs, br, os = refs[15:20]
+    home, window, normed, nt, raw, q, k, v, vt, ot, bias, scores, tops, totals, bias_in, bias_all = refs[:16]
+    xs, xr, bs, br, os = refs[16:21]
     d, z = greet(dp_bits, stages)
     rows, features = tokens.shape
     width, heads = k.shape[0], features // HD
     own = width - rows
     tile = 2 * LANES
     homes = [home.at[w] for w in range(3)] + list(fulls[3:])
-    work = Gathering(dp_bits, stages, d, z, weights, homes, refs[20:])
+    work = Gathering(dp_bits, stages, d, z, weights, homes, refs[21:])
 
     def bias_copy(step):
         return pltpu.make_async_remote_copy(
@@ -485,6 +493,7 @@
         work.pack(w)
     for w in first:
         work.hop(w, 0)
+    bias_in[...] = vectors[4:5, : features // stages]
     for step in range(1, stages):
         work.start(bias_copy, step)
     bias_all[0] = bias_in[...]
@@ -495,7 +504,7 @@
             window[hop] = jnp.zeros((rows, features), BF16)
 
     norm(tokens, own)
-    fill_bias(seg_query, seg_key, bias, block, own)
+    fill_bias(segments, z, bias, block, own)
     for j in range(1, stages - 1):
         for w in first:
             work.hop(w, j)
@@ -606,11 +615,16 @@
 
         lax.fori_loop(0, heads, head, 0)
 
-    inside = {}
+    inside, ready = {}, []
     if back and dp_bits > 2:
-        inside = {(3, 0): 0, (4, 0): heads // 4, (5, 0): heads // 2, (3, 1): heads * 3 // 4}
+        inside = {(3, 1): heads * 3 // 8, (4, 1): heads * 5 // 8, (5, 1): heads * 7 // 8}
+        ready = [(3, 0), (4, 0), (5, 0)]
+    for pair in ready[:1]:
+        work.advance(*pair)
     for hop in range(back):
         if hop + 1 == back:
+            for pair in ready[1:]:
+                work.advance(*pair)
             attend(rows, width, True, False, inside)
 
         @pl.when(z > hop)
@@ -633,7 +647,7 @@
     transpose_out(ot, o_ref)
     for r in range(dp_bits):
         for w in rest:
-            if (w, r) not in inside:
+            if (w, r) not in inside and (w, r) not in ready:
                 work.advance(w, r)
     for step in range(1, stages):
         bias_copy(step).wait_recv()
@@ -651,7 +665,7 @@
     work.close()
 
 
-def attend_forward(weights, bias, tokens, vectors, seg_q, seg_k, block, dp, stages, back):
+def attend_forward(weights, tokens, vectors, segments, block, dp, stages, back):
     held, cols = weights[0].shape
     rows, features = tokens.shape
     width, heads = (back + 1) * rows, features // HD
@@ -661,7 +675,7 @@
     sds = jax.ShapeDtypeStruct
     return pl.pallas_call(
         functools.partial(forward_kernel, block, dp.bit_length() - 1, stages, back),
-        in_specs=[vmem] * 11,
+        in_specs=[vmem] * 9,
         out_specs=[hbm] * 6 + [vmem] + [hbm] * 5 + [vmem] * 2,
         out_shape=[sds((features, features), BF16)] * 6
         + [
@@ -689,7 +703,8 @@
             pltpu.VMEM((width, rows), F32),
             pltpu.VMEM((heads, rows), F32),
             pltpu.VMEM((heads, rows), F32),
-            pltpu.VMEM((stages,) + bias.shape, F32),
+            pltpu.VMEM((1, features // stages), F32),
+            pltpu.VMEM((stages, 1, features // stages), F32),
             dma((back,)), dma((back,)), dma((stages,)), dma((stages,)), dma((8,)),
         ]
         + gathering_scratch(6, dp, stages, held, cols),
@@ -697,14 +712,14 @@
             collective_id=0, has_side_effects=True, vmem_limit_bytes=62 << 20
         ),
         name="attend_forward",
-    )(*weights, bias, tokens, vectors, seg_q, seg_k)
+    )(*weights, tokens, vectors, segments)
 
 
 def middle_kernel(block, dp_bits, stages, *refs):
     sources, refs = refs[:12], refs[12:]
-    b_up, vectors, lse_ref, seg_query, seg_key = refs[:5]
+    b_up, vectors, lse_ref, segments = refs[:4]
     factor, gain, b_down = (vectors.at[i : i + 1] for i in (1, 2, 3))
-    results, incoming, outs, sums, refs = refs[5:11], refs[11], refs[12:15], refs[15], refs[16:]
+    results, incoming, outs, sums, refs = refs[4:10], refs[10], refs[11:14], refs[14], refs[15:]
     weights, hidden, wide, tmp, tr, keys, values, query_in, grad_in, bias, delta_ref = refs[:11]
     ps, pr, sems, refs = refs[11], refs[12], refs[13], refs[14:]
     d, z = greet(dp_bits, stages)
@@ -725,7 +740,7 @@
     outside = (spare, hidden, dq, dk, dv, part.at[half:])
     loads = Loads(list(zip(sources, inside)) + list(zip(outside, results)), sems)
     loads.start(*range(9))
-    fill_bias(seg_query, seg_key, bias, block, width - rows)
+    fill_bias(segments, z, bias, block, width - rows)
 
     def by_tile(body):
         for c in range(features // tile):
@@ -935,7 +950,7 @@
 
 def middle(
     mixed, w_out, x, cot, w_up, w_down, k, v, q, w_key, w_value, raw, b_up, vectors,
-    lse, seg_q, seg_k, block, dp, stages,
+    lse, segments, block, dp, stages,
 ):
     rows, features = q.shape
     width, heads = k.shape[0], features // HD
@@ -949,7 +964,7 @@
     many, part = sds((chunks, rows, features), BF16), sds((rows // 2, features), BF16)
     return pl.pallas_call(
         functools.partial(middle_kernel, block, dp.bit_length() - 1, stages),
-        in_specs=[hbm] * 12 + [vmem] * 5,
+        in_specs=[hbm] * 12 + [vmem] * 4,
         out_specs=[hbm] * 7 + [vmem] * 4,
         out_shape=[low, high, low, many, many, part, part]
         + [sds((held, cols), F32)] * 3
@@ -975,7 +990,7 @@
         name="middle",
     )(
         mixed, w_out, x, cot, w_up, w_down, k, v, q, w_key, w_value, raw, b_up, vectors,
-        lse, seg_q, seg_k,
+        lse, segments,
     )
 
 
@@ -1160,49 +1175,74 @@
     return out[:3], out[3], out[4][levels]
 
 
+def hand_over_kernel(count, *refs):
+    half = (len(refs) - 1) // 2
+    sources, results, sems = refs[:half], refs[half : 2 * half], refs[-1]
+    loads = Loads(list(zip(sources[:count], results[:count])), sems)
+    loads.start(*range(count))
+    for source, result in zip(sources[count:], results[count:]):
+        result[...] = source[...].T
+    loads.wait(*range(count))
+
+
+def hand_over(plain, turned):
+    hbm = pl.BlockSpec(memory_space=pl.ANY)
+    vmem = pl.BlockSpec(memory_space=pltpu.VMEM)
+    sds = jax.ShapeDtypeStruct
+    return pl.pallas_call(
+        functools.partial(hand_over_kernel, len(plain)),
+        in_specs=[hbm] * len(plain) + [vmem] * len(turned),
+        out_specs=[hbm] * len(plain) + [vmem] * len(turned),
+        out_shape=[sds(a.shape, a.dtype) for a in plain]
+        + [sds(a.shape[::-1], a.dtype) for a in turned],
+        scratch_shapes=[pltpu.SemaphoreType.DMA((len(plain),))],
+        name="hand_over",
+    )(*plain, *turned)
+
+
 def body(
     tokens, segments, w_query, w_key, w_value, w_output, w_up, b_up, w_down, b_down,
     gain_attn, gain_mlp, query_scale, cotangent,
 ):
     stages = lax.axis_size("mp")
     z = lax.axis_index("mp")
-    seg = segments[0]
     rows, features = tokens.shape
     back = min(stages - 1, -(-(DOC_MAX - 1) // rows))
     own = back * rows
     block = min(256, rows)
-
-    seg_wide = jnp.concatenate([jnp.full((own,), -1, jnp.int32), seg])
-    seg_window = lax.dynamic_slice_in_dim(seg_wide, z * rows, own + rows, 0)
-    seg_query = seg_window[own:]
-    seg_query, seg_key = seg_query[None, :], seg_window[:, None]
-
     heads = features // HD
+    dp = lax.axis_size("dp")
     factor = jax.nn.softplus(query_scale) * (LOG2E / math.sqrt(HD))
-    vectors = jnp.stack([gain_attn, jnp.tile(factor, heads), gain_mlp, b_down])
-    dp = lax.axis_size("dp")
+    mine = b_up.shape[0]
+    vectors = jnp.zeros((8, features), F32)
+    row = lax.broadcasted_iota(jnp.int32, (8, features), 0)
+    given = (gain_attn, jnp.tile(factor, heads), gain_mlp, b_down, jnp.pad(b_up, (0, features - mine)))
+    for i, value in enumerate(given):
+        vectors = jnp.where(row == i, value[None], vectors)
     (
         wq, wk, wv, wu, wo, wd, b_full, query_raw, scaled, keys, values, first_t, mixed, lse
     ) = attend_forward(
-        (w_query, w_key, w_value, w_up, w_output.T, w_down.T), b_up[None], tokens,
-        vectors, seg_query, seg_key, block, dp, stages, back,
+        (w_query, w_key, w_value, w_up, w_output.T, w_down.T), tokens, vectors, segments,
+        block, dp, stages, back,
     )
     layer_out, d_hidden, d_query, d_keys, d_values, farther, incoming, *mlp, sums = middle(
         mixed, wo, tokens, cotangent, wu, wd, keys, values, scaled, wk, wv, query_raw,
-        b_full, vectors, lse, seg_query, seg_key, block, dp, stages,
+        b_full, vectors, lse, segments, block, dp, stages,
     )
     grads, tokens_grad, sums = input_gradients(
         first_t, d_query, d_keys.reshape(own + rows, features),
         d_values.reshape(own + rows, features), wq, wk, wv, incoming, farther, tokens,
         d_hidden, vectors, sums, dp, stages,
     )
-    mine = b_up.shape[0]
     sum_b_up = lax.dynamic_slice_in_dim(sums[2], z * mine, mine, 0)
     scale_total = jnp.sum(sums[4].reshape(heads, HD), axis=0)
     grad_query_scale = scale_total * (LOG2E / math.sqrt(HD)) * jax.nn.sigmoid(query_scale)
+    layer_out, tokens_grad, g_query, g_key, g_value, g_up, g_output, g_down = hand_over(
+        (layer_out, tokens_grad, *grads, mlp[1]), (mlp[2], mlp[0])
+    )
     return (
-        layer_out, tokens_grad, grads[0], grads[1], grads[2], mlp[2].T, mlp[1], sum_b_up,
-        mlp[0].T, sums[1], sums[3], sums[0], grad_query_scale,
+        layer_out, tokens_grad, g_query, g_key, g_value, g_output, g_up, sum_b_up,
+        g_down, sums[1], sums[3], sums[0], grad_query_scale,
     )
 
 

time: 323 us -> 419 us (1.30)
  Pallas kernels: 302 us -> 406 us
  local copies, waits for them, and re-layouts: 15.4 us -> 6.81 us
    pallas_call x0 -> x1, Pallas kernels: none -> 112 us  [hand_over(): pl.pallas_call(functools.partial(hand_over_kernel, len(plain)), in_specs=...]
    pallas_call x1, Pallas kernels: 95.8 us -> 86.4 us  [middle(): pl.pallas_call(functools.partial(middle_kernel, block, dp.bit_length() -...]
where the time goes in v4:
time: 419 us; the launch traced here: 416 us
  Pallas kernels  406 us (97%)
  local copies, waits for them, and re-layouts  6.81 us (2%)
    pallas_call x1, Pallas kernels, attend_forward(): pl.pallas_call(functools.partial(forward_kernel, block, dp.bit_length() -...  127 us
    pallas_call x1, Pallas kernels, hand_over(): pl.pallas_call(functools.partial(hand_over_kernel, len(plain)), in_specs=...  112 us
    pallas_call x1, Pallas kernels, middle(): pl.pallas_call(functools.partial(middle_kernel, block, dp.bit_length() -...  86.4 us
    pallas_call x1, Pallas kernels, input_gradients(): pl.pallas_call(functools.partial(input_kernel, dp_bits, stages, back), in...  80.6 us

profile of v4, /device:TPU:0, one launch (start us, length us, event | category | flops | bytes accessed | tf_op | source)
XLA Modules:
  0.0 416.4 jit_solution(16078172254287374381)
XLA Ops:
  0.7 0.7 fusion
  1.3 0.1 broadcast_in_dim.40
  1.4 0.7 pad.4
  2.1 1.4 select_select_fusion.refs_7_.refs_13_.refs_11_
  3.5 126.9 %attend_forward.1 = (bf16[1280,1280]{1,0:T(8,128)(2,1)}, bf16[1280,1280]{1,0:T(8,128)(2,1)}, bf16[1280,1280]{1,0:T(8,128)(2,1)}, bf16[1280,1280]{1,0:T(8,128)(2,...) custom-call(bf16[160,320]{1,0:T(8,128)(2,1)} %refs_0_.1, ...), custom_call_target="tpu_custom_call" | custom-call | tf_op jit(solution)/shard_map/attend_forward/pallas_call | solution.py:676
  130.5 86.4 %middle.1 = (bf16[512,1280]{1,0:T(8,128)(2,1)}, f32[512,1280]{1,0:T(8,128)}, bf16[512,1280]{1,0:T(8,128)(2,1)}, bf16[3,512,1280]{2,1,0:T(8,128)(2,1)}, bf16[3,51...) custom-call(bf16[512,1280]{1,0:T(8,128)(2,1)} %get-tuple-element.51., ...), custom_call_target="tpu_custom_call" | custom-call | tf_op jit(solution)/shard_map/middle/pallas_call | solution.py:965
  216.9 80.6 %input_gradients.1 = (f32[160,320]{1,0:T(8,128)}, f32[160,320]{1,0:T(8,128)}, f32[160,320]{1,0:T(8,128)}, bf16[512,1280]{1,0:T(8,128)(2,1)}, f32[6,8,1280]{2,1,0:T(8,128)}) custom-call(bf16[1536,1280]{1,0:T(8,128)(2,1)} %bitcast.5, bf16[1280,1536]{1,0:T(8,128)(2,1)} %get-tuple-element.65.refs_1_, bf16[1536,1280]{1,0:T(8,128)(2,1)} %bitcast.4, ...), custom_call_target="tpu_custom_call" | custom-call | tf_op jit(solution)/shard_map/input_gradients/pallas_call | solution.py:1154
  297.5 0.0 copy-start
  297.6 112.3 %hand_over.1 = (bf16[512,1280]{1,0:T(8,128)(2,1)}, bf16[512,1280]{1,0:T(8,128)(2,1)}, f32[160,320]{1,0:T(8,128)}, f32[160,320]{1,0:T(8,128)}, f32[160,320]{1,0:T...) custom-call(bf16[512,1280]{1,0:T(8,128)(2,1)} %get-tuple-element.63.refs_0_, ...), custom_call_target="tpu_custom_call" | custom-call | tf_op jit(solution)/shard_map/hand_over/pallas_call | solution.py:1192
  409.8 1.8 copy.27
  411.6 1.8 copy.28
  413.5 1.7 slice_reduce_fusion
  415.1 0.7 dynamic-slice_reduce_fusion
  415.8 0.1 reshape_squeeze.3
  415.9 0.0 copy-done
  415.9 0.5 divide_multiply_fusion
  (5 shorter events, 0.0 us)
Async XLA Ops:
  297.5 118.3 %copy-start = (f32[80]{0:T(128)S(1)}, f32[80]{0:T(128)}, u32[]{:S(2)}) copy-start(f32[80]{0:T(128)} %param.26) | copy-start | bytes 964

commit v5 on v4

--- a/solution.py
+++ b/solution.py
@@ -1176,26 +1176,20 @@
 
 
 def hand_over_kernel(count, *refs):
-    half = (len(refs) - 1) // 2
-    sources, results, sems = refs[:half], refs[half : 2 * half], refs[-1]
-    loads = Loads(list(zip(sources[:count], results[:count])), sems)
-    loads.start(*range(count))
-    for source, result in zip(sources[count:], results[count:]):
-        result[...] = source[...].T
-    loads.wait(*range(count))
+    half = len(refs) // 2
+    for i, (source, result) in enumerate(zip(refs[:half], refs[half:])):
+        result[...] = source[...] if i < count else source[...].T
 
 
 def hand_over(plain, turned):
-    hbm = pl.BlockSpec(memory_space=pl.ANY)
     vmem = pl.BlockSpec(memory_space=pltpu.VMEM)
     sds = jax.ShapeDtypeStruct
     return pl.pallas_call(
         functools.partial(hand_over_kernel, len(plain)),
-        in_specs=[hbm] * len(plain) + [vmem] * len(turned),
-        out_specs=[hbm] * len(plain) + [vmem] * len(turned),
+        in_specs=[vmem] * (len(plain) + len(turned)),
+        out_specs=[vmem] * (len(plain) + len(turned)),
         out_shape=[sds(a.shape, a.dtype) for a in plain]
         + [sds(a.shape[::-1], a.dtype) for a in turned],
-        scratch_shapes=[pltpu.SemaphoreType.DMA((len(plain),))],
         name="hand_over",
     )(*plain, *turned)
 

time: 419 us -> 311 us (0.74)
  Pallas kernels: 406 us -> 298 us
    pallas_call x1, Pallas kernels: 112 us -> 4.39 us  [hand_over(): pl.pallas_call(functools.partial(hand_over_kernel, len(plain)), in_specs=...]
where the time goes in v5:
time: 311 us; the launch traced here: 309 us
  Pallas kernels  298 us (96%)
  local copies, waits for them, and re-layouts  6.81 us (2%)
    pallas_call x1, Pallas kernels, attend_forward(): pl.pallas_call(functools.partial(forward_kernel, block, dp.bit_length() -...  127 us
    pallas_call x1, Pallas kernels, middle(): pl.pallas_call(functools.partial(middle_kernel, block, dp.bit_length() -...  86.4 us
    pallas_call x1, Pallas kernels, input_gradients(): pl.pallas_call(functools.partial(input_kernel, dp_bits, stages, back), in...  80.6 us

profile of v5, /device:TPU:0, one launch (start us, length us, event | category | flops | bytes accessed | tf_op | source)
XLA Modules:
  0.0 308.5 jit_solution(17334340854416728497)
XLA Ops:
  0.7 0.7 fusion
  1.3 0.1 broadcast_in_dim.40
  1.4 0.7 pad.4
  2.1 1.4 select_select_fusion.refs_7_.refs_13_.refs_11_
  3.5 126.9 %attend_forward.1 = (bf16[1280,1280]{1,0:T(8,128)(2,1)}, bf16[1280,1280]{1,0:T(8,128)(2,1)}, bf16[1280,1280]{1,0:T(8,128)(2,1)}, bf16[1280,1280]{1,0:T(8,128)(2,...) custom-call(bf16[160,320]{1,0:T(8,128)(2,1)} %refs_0_.1, ...), custom_call_target="tpu_custom_call" | custom-call | tf_op jit(solution)/shard_map/attend_forward/pallas_call | solution.py:676
  130.5 86.4 %middle.1 = (bf16[512,1280]{1,0:T(8,128)(2,1)}, f32[512,1280]{1,0:T(8,128)}, bf16[512,1280]{1,0:T(8,128)(2,1)}, bf16[3,512,1280]{2,1,0:T(8,128)(2,1)}, bf16[3,51...) custom-call(bf16[512,1280]{1,0:T(8,128)(2,1)} %get-tuple-element.51., ...), custom_call_target="tpu_custom_call" | custom-call | tf_op jit(solution)/shard_map/middle/pallas_call | solution.py:965
  216.9 80.6 %input_gradients.1 = (f32[160,320]{1,0:T(8,128)}, f32[160,320]{1,0:T(8,128)}, f32[160,320]{1,0:T(8,128)}, bf16[512,1280]{1,0:T(8,128)(2,1)}, f32[6,8,1280]{2,1,0:T(8,128)}) custom-call(bf16[1536,1280]{1,0:T(8,128)(2,1)} %bitcast.5, bf16[1280,1536]{1,0:T(8,128)(2,1)} %get-tuple-element.65.refs_1_, bf16[1536,1280]{1,0:T(8,128)(2,1)} %bitcast.4, ...), custom_call_target="tpu_custom_call" | custom-call | tf_op jit(solution)/shard_map/input_gradients/pallas_call | solution.py:1154
  297.5 0.0 copy-start
  297.6 4.4 %hand_over.1 = (bf16[512,1280]{1,0:T(8,128)(2,1)}, bf16[512,1280]{1,0:T(8,128)(2,1)}, f32[160,320]{1,0:T(8,128)}, f32[160,320]{1,0:T(8,128)}, f32[160,320]{1,0:T...) custom-call(bf16[512,1280]{1,0:T(8,128)(2,1)} %get-tuple-element.63.refs_0_, ...), custom_call_target="tpu_custom_call" | custom-call | tf_op jit(solution)/shard_map/hand_over/pallas_call | solution.py:1187
  301.9 1.8 copy.27
  303.8 1.8 copy.28
  305.6 1.7 slice_reduce_fusion
  307.2 0.7 dynamic-slice_reduce_fusion
  307.9 0.1 reshape_squeeze.3
  308.0 0.0 copy-done
  308.0 0.5 divide_multiply_fusion
  (5 shorter events, 0.0 us)
Async XLA Ops:
  297.5 10.4 %copy-start = (f32[80]{0:T(128)S(1)}, f32[80]{0:T(128)}, u32[]{:S(2)}) copy-start(f32[80]{0:T(128)} %param.26) | copy-start | bytes 964

commit v6 on v5

--- a/solution.py
+++ b/solution.py
@@ -488,6 +488,18 @@
 
         lax.fori_loop(0, features // tile, step, 0)
 
+    def project_both(at):
+        def step(c, carry):
+            lanes = pl.ds(pl.multiple_of(c * tile, tile), tile)
+            source = normed[at : at + rows, :]
+            k[at : at + rows, lanes] = dot(source, home[1, :, lanes], 1, 0).astype(BF16)
+            value = dot(source, home[2, :, lanes], 1, 0).astype(BF16)
+            v[at : at + rows, lanes] = value
+            vt[lanes, at : at + rows] = value.T
+            return carry
+
+        lax.fori_loop(0, features // tile, step, 0)
+
     first, rest = range(3), range(3, 6)
     for w in range(6):
         work.pack(w)
@@ -560,15 +572,7 @@
             if qs:
                 tiles.append((kb, qs))
 
-        def head(h, carry):
-            for at in sorted(set(due.values())):
-
-                @pl.when(h == at)
-                def _():
-                    for w, r in due:
-                        if due[w, r] == at:
-                            work.advance(w, r)
-
+        def head(h):
             lanes, mine = head_lanes(h, features)
             feats = pl.ds(pl.multiple_of(h * HD, 16), HD)
             query = jnp.where(mine, q[:, lanes], jnp.zeros((), BF16))
@@ -611,9 +615,21 @@
                     ot[feats, at] = out
                     totals[pl.ds(h, 1), at] = one
                     tops[pl.ds(h, 1), at] = top[:, at]
+
+        def pair(i, carry):
+            for at in sorted(set(due.values())):
+
+                @pl.when(2 * i == at)
+                def _():
+                    for w, r in due:
+                        if due[w, r] == at:
+                            work.advance(w, r)
+
+            head(2 * i)
+            head(2 * i + 1)
             return carry
 
-        lax.fori_loop(0, heads, head, 0)
+        lax.fori_loop(0, heads // 2, pair, 0)
 
     inside, ready = {}, []
     if back and dp_bits > 2:
@@ -639,8 +655,7 @@
 
         at = own - (hop + 1) * rows
         norm(window.at[hop], at)
-        project(1, at, k, None)
-        project(2, at, v, vt)
+        project_both(at)
     for i in range(2, 5):
         keep(i).start()
     attend(0, rows if back else width, not back, True, {})
@@ -1175,23 +1190,21 @@
     return out[:3], out[3], out[4][levels]
 
 
-def hand_over_kernel(count, *refs):
+def hand_over_kernel(*refs):
     half = len(refs) // 2
-    for i, (source, result) in enumerate(zip(refs[:half], refs[half:])):
-        result[...] = source[...] if i < count else source[...].T
-
-
-def hand_over(plain, turned):
+    for source, result in zip(refs[:half], refs[half:]):
+        result[...] = source[...]
+
+
+def hand_over(arrays):
     vmem = pl.BlockSpec(memory_space=pltpu.VMEM)
-    sds = jax.ShapeDtypeStruct
     return pl.pallas_call(
-        functools.partial(hand_over_kernel, len(plain)),
-        in_specs=[vmem] * (len(plain) + len(turned)),
-        out_specs=[vmem] * (len(plain) + len(turned)),
-        out_shape=[sds(a.shape, a.dtype) for a in plain]
-        + [sds(a.shape[::-1], a.dtype) for a in turned],
+        hand_over_kernel,
+        in_specs=[vmem] * len(arrays),
+        out_specs=[vmem] * len(arrays),
+        out_shape=[jax.ShapeDtypeStruct(a.shape, a.dtype) for a in arrays],
         name="hand_over",
-    )(*plain, *turned)
+    )(*arrays)
 
 
 def body(
@@ -1232,11 +1245,11 @@
     scale_total = jnp.sum(sums[4].reshape(heads, HD), axis=0)
     grad_query_scale = scale_total * (LOG2E / math.sqrt(HD)) * jax.nn.sigmoid(query_scale)
     layer_out, tokens_grad, g_query, g_key, g_value, g_up, g_output, g_down = hand_over(
-        (layer_out, tokens_grad, *grads, mlp[1]), (mlp[2], mlp[0])
+        (layer_out, tokens_grad, *grads, mlp[1], mlp[2], mlp[0])
     )
     return (
-        layer_out, tokens_grad, g_query, g_key, g_value, g_output, g_up, sum_b_up,
-        g_down, sums[1], sums[3], sums[0], grad_query_scale,
+        layer_out, tokens_grad, g_query, g_key, g_value, g_output.T, g_up, sum_b_up,
+        g_down.T, sums[1], sums[3], sums[0], grad_query_scale,
     )
 
 

time: 311 us -> 304 us (0.977)
  local copies, waits for them, and re-layouts: 6.81 us -> 3.2 us
    unnamed x4 -> x2, local copies, waits for them, and re-layouts: 3.62 us -> 0.01 us
    pallas_call x1, Pallas kernels: 127 us -> 124 us  [attend_forward(): pl.pallas_call(functools.partial(forward_kernel, block, dp.bit_length() -...]
where the time goes in v6:
time: 304 us; the launch traced here: 301 us
  Pallas kernels  295 us (97%)
  local copies, waits for them, and re-layouts  3.2 us (1%)
    pallas_call x1, Pallas kernels, attend_forward(): pl.pallas_call(functools.partial(forward_kernel, block, dp.bit_length() -...  124 us
    pallas_call x1, Pallas kernels, middle(): pl.pallas_call(functools.partial(middle_kernel, block, dp.bit_length() -...  86.4 us
    pallas_call x1, Pallas kernels, input_gradients(): pl.pallas_call(functools.partial(input_kernel, dp_bits, stages, back), in...  80.6 us

profile of v6, /device:TPU:0, one launch (start us, length us, event | category | flops | bytes accessed | tf_op | source)
XLA Modules:
  0.0 301.4 jit_solution(9057228144594844157)
XLA Ops:
  0.7 0.7 fusion
  1.3 0.1 broadcast_in_dim.40
  1.4 0.7 pad.4
  2.1 1.4 select_select_fusion.refs_7_.refs_13_.refs_11_
  3.5 123.6 %attend_forward.1 = (bf16[1280,1280]{1,0:T(8,128)(2,1)}, bf16[1280,1280]{1,0:T(8,128)(2,1)}, bf16[1280,1280]{1,0:T(8,128)(2,1)}, bf16[1280,1280]{1,0:T(8,128)(2,...) custom-call(bf16[160,320]{1,0:T(8,128)(2,1)} %refs_0_.1, ...), custom_call_target="tpu_custom_call" | custom-call | tf_op jit(solution)/shard_map/attend_forward/pallas_call | solution.py:691
  127.1 86.4 %middle.1 = (bf16[512,1280]{1,0:T(8,128)(2,1)}, f32[512,1280]{1,0:T(8,128)}, bf16[512,1280]{1,0:T(8,128)(2,1)}, bf16[3,512,1280]{2,1,0:T(8,128)(2,1)}, bf16[3,51...) custom-call(bf16[512,1280]{1,0:T(8,128)(2,1)} %get-tuple-element.51., ...), custom_call_target="tpu_custom_call" | custom-call | tf_op jit(solution)/shard_map/middle/pallas_call | solution.py:980
  213.6 80.6 %input_gradients.1 = (f32[160,320]{1,0:T(8,128)}, f32[160,320]{1,0:T(8,128)}, f32[160,320]{1,0:T(8,128)}, bf16[512,1280]{1,0:T(8,128)(2,1)}, f32[6,8,1280]{2,1,0:T(8,128)}) custom-call(bf16[1536,1280]{1,0:T(8,128)(2,1)} %bitcast.7, bf16[1280,1536]{1,0:T(8,128)(2,1)} %get-tuple-element.65.refs_1_, bf16[1536,1280]{1,0:T(8,128)(2,1)} %bitcast.6, ...), custom_call_target="tpu_custom_call" | custom-call | tf_op jit(solution)/shard_map/input_gradients/pallas_call | solution.py:1169
  294.2 0.0 copy-start
  294.2 4.2 %hand_over.1 = (bf16[512,1280]{1,0:T(8,128)(2,1)}, bf16[512,1280]{1,0:T(8,128)(2,1)}, f32[160,320]{1,0:T(8,128)}, f32[160,320]{1,0:T(8,128)}, f32[160,320]{1,0:T...) custom-call(bf16[512,1280]{1,0:T(8,128)(2,1)} %get-tuple-element.63.refs_0_, ...), custom_call_target="tpu_custom_call" | custom-call | tf_op jit(solution)/shard_map/hand_over/pallas_call | solution.py:1201
  298.4 1.7 slice_reduce_fusion
  300.1 0.7 dynamic-slice_reduce_fusion
  300.7 0.1 reshape_squeeze.3
  300.8 0.0 copy-done
  300.8 0.5 divide_multiply_fusion
  (5 shorter events, 0.0 us)
Async XLA Ops:
  294.2 6.6 %copy-start = (f32[80]{0:T(128)S(1)}, f32[80]{0:T(128)}, u32[]{:S(2)}) copy-start(f32[80]{0:T(128)} %param.26) | copy-start | bytes 964

commit v7 on v6

--- a/solution.py
+++ b/solution.py
@@ -477,17 +477,6 @@
             lanes = slice(c * tile, (c + 1) * tile)
             nt[lanes, at : at + rows] = normed[at : at + rows, lanes].T
 
-    def project(w, at, out, out_t):
-        def step(c, carry):
-            lanes = pl.ds(pl.multiple_of(c * tile, tile), tile)
-            value = dot(normed[at : at + rows, :], home[w, :, lanes], 1, 0).astype(BF16)
-            out[at : at + rows, lanes] = value
-            if out_t is not None:
-                out_t[lanes, at : at + rows] = value.T
-            return carry
-
-        lax.fori_loop(0, features // tile, step, 0)
-
     def project_both(at):
         def step(c, carry):
             lanes = pl.ds(pl.multiple_of(c * tile, tile), tile)
@@ -560,8 +549,8 @@
             lax.fori_loop(0, features // tile, query, 0)
             keep(0).start()
             keep(1).start()
-        else:
-            project(w, own, *((k, None) if w == 1 else (v, vt)))
+        elif w == 2:
+            project_both(own)
 
     sp = spans(rows, width, block)
 
@@ -572,7 +561,7 @@
             if qs:
                 tiles.append((kb, qs))
 
-        def head(h):
+        def head(h, scores):
             lanes, mine = head_lanes(h, features)
             feats = pl.ds(pl.multiple_of(h * HD, 16), HD)
             query = jnp.where(mine, q[:, lanes], jnp.zeros((), BF16))
@@ -625,8 +614,8 @@
                         if due[w, r] == at:
                             work.advance(w, r)
 
-            head(2 * i)
-            head(2 * i + 1)
+            head(2 * i, scores.at[0])
+            head(2 * i + 1, scores.at[1])
             return carry
 
         lax.fori_loop(0, heads // 2, pair, 0)
@@ -715,7 +704,7 @@
             pltpu.VMEM((features, width), BF16),
             pltpu.VMEM((features, rows), F32),
             pltpu.VMEM((width, rows), F32),
-            pltpu.VMEM((width, rows), F32),
+            pltpu.VMEM((2, width, rows), F32),
             pltpu.VMEM((heads, rows), F32),
             pltpu.VMEM((heads, rows), F32),
             pltpu.VMEM((1, features // stages), F32),
@@ -754,7 +743,7 @@
     half = rows // 2
     outside = (spare, hidden, dq, dk, dv, part.at[half:])
     loads = Loads(list(zip(sources, inside)) + list(zip(outside, results)), sems)
-    loads.start(*range(9))
+    loads.start(0, 1, 2)
     fill_bias(segments, z, bias, block, width - rows)
 
     def by_tile(body):
@@ -824,9 +813,11 @@
     sums[3:8, :] = jnp.zeros((5, features), F32)
     delta_ref[...] = jnp.zeros_like(delta_ref)
     loads.wait(0, 1, 2)
+    loads.start(3, 4, 5)
     by_tile(add_attention)
     by_rows(norm, 0)
     loads.wait(3, 4, 5)
+    loads.start(6, 7, 8)
     by_tile(activate)
     flip(cot)
     work.weight_grad(0, lambda at: tr[at, :], lambda: active[...])
@@ -1040,7 +1031,7 @@
         def _():
             down(0).start()
 
-    loads.start(*range(10))
+    loads.start(0, 1)
 
     def arrived(hop):
         source = incoming if hop == 1 else landed.at[hop - 2]
@@ -1085,7 +1076,9 @@
             down(hop).start()
 
     loads.wait(0, 1)
+    loads.start(2, 3, 4, 5)
     weight_grad(0)
+    loads.start(6, 7, 8, 9)
     loads.wait(2)
     weight_grad(1)
     work.advance(2, 0)
@@ -1197,11 +1190,13 @@
 
 
 def hand_over(arrays):
-    vmem = pl.BlockSpec(memory_space=pltpu.VMEM)
+    steps = 4 if all(a.shape[0] % 64 == 0 or (a.shape[0] % 32 == 0 and a.dtype == F32) for a in arrays) else 1
+    specs = [pl.BlockSpec((a.shape[0] // steps, a.shape[1]), lambda i: (i, 0)) for a in arrays]
     return pl.pallas_call(
         hand_over_kernel,
-        in_specs=[vmem] * len(arrays),
-        out_specs=[vmem] * len(arrays),
+        grid=(steps,),
+        in_specs=specs,
+        out_specs=specs,
         out_shape=[jax.ShapeDtypeStruct(a.shape, a.dtype) for a in arrays],
         name="hand_over",
     )(*arrays)

time: 304 us -> 305 us (level)
  no operation moved by 1% of the time
where the time goes in v7:
time: 305 us; the launch traced here: 304 us
  Pallas kernels  297 us (97%)
  local copies, waits for them, and re-layouts  3.2 us (1%)
    pallas_call x1, Pallas kernels, attend_forward(): pl.pallas_call(functools.partial(forward_kernel, block, dp.bit_length() -...  124 us
    pallas_call x1, Pallas kernels, middle(): pl.pallas_call(functools.partial(middle_kernel, block, dp.bit_length() -...  86.7 us
    pallas_call x1, Pallas kernels, input_gradients(): pl.pallas_call(functools.partial(input_kernel, dp_bits, stages, back), in...  82.3 us

profile of v7, /device:TPU:0, one launch (start us, length us, event | category | flops | bytes accessed | tf_op | source)
XLA Modules:
  0.0 303.6 jit_solution(13599287583227916359)
XLA Ops:
  0.7 0.7 fusion
  1.3 0.1 broadcast_in_dim.40
  1.4 0.7 pad.4
  2.1 1.4 select_select_fusion.refs_7_.refs_13_.refs_11_
  3.5 123.6 %attend_forward.1 = (bf16[1280,1280]{1,0:T(8,128)(2,1)}, bf16[1280,1280]{1,0:T(8,128)(2,1)}, bf16[1280,1280]{1,0:T(8,128)(2,1)}, bf16[1280,1280]{1,0:T(8,128)(2,...) custom-call(bf16[160,320]{1,0:T(8,128)(2,1)} %refs_0_.1, ...), custom_call_target="tpu_custom_call" | custom-call | tf_op jit(solution)/shard_map/attend_forward/pallas_call | solution.py:680
  127.1 86.7 %middle.1 = (bf16[512,1280]{1,0:T(8,128)(2,1)}, f32[512,1280]{1,0:T(8,128)}, bf16[512,1280]{1,0:T(8,128)(2,1)}, bf16[3,512,1280]{2,1,0:T(8,128)(2,1)}, bf16[3,51...) custom-call(bf16[512,1280]{1,0:T(8,128)(2,1)} %get-tuple-element.51., ...), custom_call_target="tpu_custom_call" | custom-call | tf_op jit(solution)/shard_map/middle/pallas_call | solution.py:971
  213.8 82.3 %input_gradients.1 = (f32[160,320]{1,0:T(8,128)}, f32[160,320]{1,0:T(8,128)}, f32[160,320]{1,0:T(8,128)}, bf16[512,1280]{1,0:T(8,128)(2,1)}, f32[6,8,1280]{2,1,0:T(8,128)}) custom-call(bf16[1536,1280]{1,0:T(8,128)(2,1)} %bitcast.7, bf16[1280,1536]{1,0:T(8,128)(2,1)} %get-tuple-element.65.refs_1_, bf16[1536,1280]{1,0:T(8,128)(2,1)} %bitcast.6, ...), custom_call_target="tpu_custom_call" | custom-call | tf_op jit(solution)/shard_map/input_gradients/pallas_call | solution.py:1162
  296.1 0.0 copy-start
  296.1 4.5 %hand_over.1 = (bf16[512,1280]{1,0:T(8,128)(2,1)}, bf16[512,1280]{1,0:T(8,128)(2,1)}, f32[160,320]{1,0:T(8,128)}, f32[160,320]{1,0:T(8,128)}, f32[160,320]{1,0:T...) custom-call(bf16[512,1280]{1,0:T(8,128)(2,1)} %get-tuple-element.63.refs_0_, ...), custom_call_target="tpu_custom_call" | custom-call | tf_op jit(solution)/shard_map/hand_over/pallas_call | solution.py:1195
  300.7 1.7 slice_reduce_fusion
  302.3 0.7 dynamic-slice_reduce_fusion
  303.0 0.1 reshape_squeeze.3
  303.1 0.0 copy-done
  303.1 0.5 divide_multiply_fusion
  (5 shorter events, 0.0 us)
Async XLA Ops:
  296.1 7.0 %copy-start = (f32[80]{0:T(128)S(1)}, f32[80]{0:T(128)}, u32[]{:S(2)}) copy-start(f32[80]{0:T(128)} %param.26) | copy-start | bytes 964

commit v8 on v6

--- a/solution.py
+++ b/solution.py
@@ -54,16 +54,21 @@
     return out
 
 
-def greet(dp_bits, stages, extra=()):
+def greet(dp_bits, stages, everyone=False):
     d, z = lax.axis_index("dp"), lax.axis_index("mp")
     barrier = pltpu.get_barrier_semaphore()
-    for b in range(dp_bits):
-        pl.semaphore_signal(barrier, device_id={"dp": flipped(d, (b,))}, device_id_type=MESH)
+    dp = 1 << dp_bits
+    if everyone:
+        peers = [lax.rem(d + step, dp) for step in range(1, dp)]
+    else:
+        peers = [flipped(d, (b,)) for b in range(dp_bits)]
+    for peer in peers:
+        pl.semaphore_signal(barrier, device_id={"dp": peer}, device_id_type=MESH)
     for step in range(1, stages):
         pl.semaphore_signal(
             barrier, device_id={"mp": lax.rem(z + step, stages)}, device_id_type=MESH
         )
-    pl.semaphore_wait(barrier, dp_bits + stages - 1)
+    pl.semaphore_wait(barrier, len(peers) + stages - 1)
     return d, z
 
 
@@ -1015,16 +1020,16 @@
     outs, result, total, refs = refs[:3], refs[3], refs[4], refs[5:]
     inside, tokens_grad, refs = refs[:10], refs[10], refs[11:]
     dv, nt, dk, wk, wv, incoming, dq, wq, tokens, d_hidden = inside
-    part, landed, d_first, sgot, ss, sr, ps, pr, sems = refs[:9]
-    d, z = greet(dp_bits, stages)
-    work = Reduction(dp_bits, stages, d, z, None, outs, refs[9:])
+    part, landed, d_first, mine, sgot, zgot, ss, sr, ps, pr, sems = refs[:11]
+    d, z = greet(dp_bits, stages, True)
+    work = Reduction(dp_bits, stages, d, z, None, outs, refs[11:])
     rows, features = tokens.shape
     own, half = back * rows, rows // 2
     inside = inside[:5] + (incoming.at[:half],) + inside[6:]
     loads = Loads(list(zip(sources, inside)) + [(tokens_grad, result)], sems)
-    levels = dp_bits + stages.bit_length() - 1
+    dp = 1 << dp_bits
     held = features >> dp_bits
-    grads = ((dv, 2, 0), (dk, 1, 0), (dq, 0, own))
+    grads = {0: (dq, own), 1: (dk, 0), 2: (dv, 0)}
 
     def down(hop):
         return pltpu.make_async_remote_copy(
@@ -1051,56 +1056,76 @@
 
         return there, take
 
-    def weight_grad(i):
-        grad, w, at = grads[i]
+    def weight_grad(w):
+        grad, at = grads[w]
         work.weight_grad(w, lambda rows_at: nt[rows_at, at:], lambda: grad[...])
 
-    def sum_copy(k):
-        if k < dp_bits:
-            to = {"dp": flipped(d, (k,))}
+    def sum_copy(axis, step):
+        if axis == "dp":
+            to, source, target, at = lax.rem(d + step, dp), mine, sgot, step
         else:
-            to = {"mp": flipped(z, (k - dp_bits,))}
+            to, source, target, at = lax.rem(z + step, stages), sgot.at[0], zgot, dp + step
         return pltpu.make_async_remote_copy(
-            src_ref=total.at[k], dst_ref=sgot.at[k], send_sem=ss.at[k], recv_sem=sr.at[k],
-            device_id=to, device_id_type=MESH,
+            src_ref=source, dst_ref=target.at[step], send_sem=ss.at[at], recv_sem=sr.at[at],
+            device_id={axis: to}, device_id_type=MESH,
         )
 
-    def sum_step(k):
-        sum_copy(k).wait_recv()
-        total[k + 1] = total[k] + sgot[k]
-        if k + 1 < levels:
-            work.start(sum_copy, k + 1)
+    def sum_dp():
+        for step in range(1, dp):
+            sum_copy("dp", step).wait_recv()
+        sgot[0] = mine[...]
+        value = sgot[lax.rem(d, dp)]
+        for e in range(1, dp):
+            value = value + sgot[lax.rem(d - e + dp, dp)]
+        sgot[0] = value
+        for step in range(1, stages):
+            work.start(sum_copy, "mp", step)
+
+    def sum_mp():
+        for step in range(1, stages):
+            sum_copy("mp", step).wait_recv()
+        zgot[0] = sgot[0]
+        value = zgot[lax.rem(z, stages)]
+        for e in range(1, stages):
+            value = value + zgot[lax.rem(z - e + stages, stages)]
+        total[...] = value
 
     def pass_down(hop):
         there, take = arrived(hop)
+        back_project(d_first, ((dk, wk), (dv, wv)), hop * rows, None)
+        if hop == 1:
+            work.advance(2, 0)
+            weight_grad(1)
 
         @pl.when(there)
         def _():
             down(hop - 1).wait_recv()
 
-        back_project(part.at[hop - 1], ((dk, wk), (dv, wv)), hop * rows, take)
+        for c in range(features // LANES):
+            lanes = slice(c * LANES, (c + 1) * LANES)
+            part[hop - 1, :, lanes] = (d_first[:, lanes] + take(lanes)).astype(BF16)
 
         @pl.when(z >= back - hop)
         def _():
             down(hop).start()
 
     loads.wait(0, 1)
-    weight_grad(0)
-    loads.wait(2)
-    weight_grad(1)
-    work.advance(2, 0)
-    loads.wait(3, 4, 5)
+    weight_grad(2)
+    loads.wait(2, 3, 4, 5)
     if back > 1:
         pass_down(1)
+    else:
+        work.advance(2, 0)
+        weight_grad(1)
     work.advance(1, 0)
     loads.wait(6, 7)
-    weight_grad(2)
+    weight_grad(0)
     for hop in range(2, back):
         pass_down(hop)
     work.advance(0, 0)
     back_project(d_first, ((dk, wk), (dv, wv), (dq, wq)), own, None)
     events = [(w, k) for w in (2, 1, 0) for k in range(1, dp_bits)]
-    for event in events[:1]:
+    for event in events[:-2]:
         work.advance(*event)
     loads.wait(8, 9)
     there, take = arrived(back) if back else (None, None)
@@ -1129,18 +1154,18 @@
         return column + jnp.sum(grad * x * inverse, axis=0, keepdims=True)
 
     column = lax.fori_loop(0, rows // chunk, finish, jnp.zeros((1, features), F32))
-    total[0] = sums[...]
-    total[0, 3:4, :] = column
-    work.start(sum_copy, 0)
+    mine[...] = sums[...]
+    mine[3:4, :] = column
+    for step in range(1, dp):
+        work.start(sum_copy, "dp", step)
     loads.start(10)
-    done = 0
-    for event in events[1:]:
+    follow = [sum_dp, sum_mp]
+    for event in events[-2:]:
         work.advance(*event)
-        if done < levels:
-            sum_step(done)
-            done += 1
-    for k in range(done, levels):
-        sum_step(k)
+        if follow:
+            follow.pop(0)()
+    for other in follow:
+        other()
     for w in (2, 1, 0):
         work.finish(w)
     for hop in range(back):
@@ -1160,7 +1185,6 @@
     back = dk.shape[0] // rows - 1
     held, cols = features // dp, features // stages
     dp_bits = dp.bit_length() - 1
-    levels = dp_bits + stages.bit_length() - 1
     hbm = pl.BlockSpec(memory_space=pl.ANY)
     vmem = pl.BlockSpec(memory_space=pltpu.VMEM)
     dma = pltpu.SemaphoreType.DMA
@@ -1173,13 +1197,14 @@
         out_shape=[jax.ShapeDtypeStruct((held, cols), F32)] * 3
         + [
             jax.ShapeDtypeStruct((rows, features), BF16),
-            jax.ShapeDtypeStruct((levels + 1,) + sums.shape, F32),
+            jax.ShapeDtypeStruct(sums.shape, F32),
         ],
         scratch_shapes=[pltpu.VMEM(tokens.shape if a is incoming else a.shape, a.dtype) for a in sources + (tokens,)]
         + [
             pltpu.VMEM((hops, rows, features), BF16), pltpu.VMEM((hops, rows, features), BF16),
-            pltpu.VMEM((rows, features), F32), pltpu.VMEM((levels,) + sums.shape, F32),
-            dma((levels,)), dma((levels,)), dma((hops + 1,)), dma((hops + 1,)), dma((11,)),
+            pltpu.VMEM((rows, features), F32), pltpu.VMEM(sums.shape, F32),
+            pltpu.VMEM((dp,) + sums.shape, F32), pltpu.VMEM((stages,) + sums.shape, F32),
+            dma((dp + stages,)), dma((dp + stages,)), dma((hops + 1,)), dma((hops + 1,)), dma((11,)),
         ]
         + reduction_scratch(3, dp, stages, held, features, True),
         compiler_params=pltpu.CompilerParams(
@@ -1187,7 +1212,7 @@
         ),
         name="input_gradients",
     )(*sources, farther, vectors, sums)
-    return out[:3], out[3], out[4][levels]
+    return out[:3], out[3], out[4]
 
 
 def hand_over_kernel(*refs):

time: 304 us -> 304 us (level)
  no operation moved by 1% of the time
where the time goes in v8:
time: 304 us; the launch traced here: 303 us
  Pallas kernels  298 us (98%)
    pallas_call x1, Pallas kernels, attend_forward(): pl.pallas_call(functools.partial(forward_kernel, block, dp.bit_length() -...  124 us
    pallas_call x1, Pallas kernels, middle(): pl.pallas_call(functools.partial(middle_kernel, block, dp.bit_length() -...  86.4 us
    pallas_call x1, Pallas kernels, input_gradients(): pl.pallas_call(functools.partial(input_kernel, dp_bits, stages, back), in...  83.6 us

profile of v8, /device:TPU:0, one launch (start us, length us, event | category | flops | bytes accessed | tf_op | source)
XLA Modules:
  0.0 303.3 jit_solution(9906034772243641657)
XLA Ops:
  0.7 0.7 fusion
  1.3 0.1 broadcast_in_dim.40
  1.4 0.7 pad.4
  2.1 1.4 select_select_fusion.refs_7_.refs_13_.refs_11_
  3.5 123.6 %attend_forward.1 = (bf16[1280,1280]{1,0:T(8,128)(2,1)}, bf16[1280,1280]{1,0:T(8,128)(2,1)}, bf16[1280,1280]{1,0:T(8,128)(2,1)}, bf16[1280,1280]{1,0:T(8,128)(2,...) custom-call(bf16[160,320]{1,0:T(8,128)(2,1)} %refs_0_.1, ...), custom_call_target="tpu_custom_call" | custom-call | tf_op jit(solution)/shard_map/attend_forward/pallas_call | solution.py:696
  127.1 86.4 %middle.1 = (bf16[512,1280]{1,0:T(8,128)(2,1)}, f32[512,1280]{1,0:T(8,128)}, bf16[512,1280]{1,0:T(8,128)(2,1)}, bf16[3,512,1280]{2,1,0:T(8,128)(2,1)}, bf16[3,51...) custom-call(bf16[512,1280]{1,0:T(8,128)(2,1)} %get-tuple-element.51., ...), custom_call_target="tpu_custom_call" | custom-call | tf_op jit(solution)/shard_map/middle/pallas_call | solution.py:985
  213.6 83.6 %input_gradients.1 = (f32[160,320]{1,0:T(8,128)}, f32[160,320]{1,0:T(8,128)}, f32[160,320]{1,0:T(8,128)}, bf16[512,1280]{1,0:T(8,128)(2,1)}, f32[8,1280]{1,0:T(8,128)}) custom-call(bf16[1536,1280]{1,0:T(8,128)(2,1)} %bitcast.7, bf16[1280,1536]{1,0:T(8,128)(2,1)} %get-tuple-element.65.refs_1_, bf16[1536,1280]{1,0:T(8,128)(2,1)} %bitcast.6, ...), custom_call_target="tpu_custom_call" | custom-call | tf_op jit(solution)/shard_map/input_gradients/pallas_call | solution.py:1193
  297.1 0.0 copy-start
  297.2 0.0 copy-start.1
  297.2 4.2 %hand_over.1 = (bf16[512,1280]{1,0:T(8,128)(2,1)}, bf16[512,1280]{1,0:T(8,128)(2,1)}, f32[160,320]{1,0:T(8,128)}, f32[160,320]{1,0:T(8,128)}, f32[160,320]{1,0:T...) custom-call(bf16[512,1280]{1,0:T(8,128)(2,1)} %get-tuple-element.63.refs_0_, ...), custom_call_target="tpu_custom_call" | custom-call | tf_op jit(solution)/shard_map/hand_over/pallas_call | solution.py:1226
  301.3 0.0 copy-done
  301.3 0.7 slice_reduce_fusion
  302.0 0.7 dynamic-slice_reduce_fusion
  302.7 0.1 reshape_squeeze.3
  302.8 0.0 copy-done.1
  302.8 0.5 divide_multiply_fusion
  (5 shorter events, 0.0 us)
Async XLA Ops:
  297.1 4.2 %copy-start = (f32[8,1280]{1,0:T(8,128)S(1)}, f32[8,1280]{1,0:T(8,128)}, u32[]{:S(2)}) copy-start(f32[8,1280]{1,0:T(8,128)} %get-tuple-element.87) | copy-start | bytes 122884
  297.2 5.6 %copy-start.1 = (f32[80]{0:T(128)S(1)}, f32[80]{0:T(128)}, u32[]{:S(2)}) copy-start(f32[80]{0:T(128)} %param.26) | copy-start | bytes 964
